TPU v7x, 128 devices: a whole 4x4x4 slice. The times are simulated.
128 devices in a mesh: row: 16 (over z_hi, y, core), col: 8 (over x, z_lo).
Axes of the slice: x: 4, y: 4, z: 4 (z_hi: 2, z_lo: 2; z = z_hi * 2 + z_lo), core: 2. Of those that a mesh axis runs over, the one named last changes fastest.
Arguments:
- word_topic: bfloat16 [131072, 128], P(('row', 'col')), may hold values from 0.25 to 4
- topic_weight: float32 [128], replicated, may hold values from 0.1 to 10
- tile_blocks: int32 [16, 8, 64, 2], P('row', 'col'), may hold values from 0 to 63, as said below
- tile_live: int32 [16, 8], P('row', 'col'), may hold values from 16 to 64, as said below
- pair_counts: int32 [16, 8, 64, 256, 256], P('row', 'col'), may hold values from 0 to 63
Outputs:
- next_word_topic: bfloat16 [131072, 128], P(('row', 'col'))
- next_topic_weight: float32 [128], replicated
Inputs may be any that keep to these rules, and one draw needn't show every extreme that they name: `tile_blocks`: each entry pair is (a word block among the device's 32 blocks of first words, a word block among its 64 blocks of second words); the slots of one device name distinct tiles. `tile_live`: slots at or beyond a device's count hold no tile; some device fills all slots.
All inputs are finite; a program needn't handle non-finite values.
Results may differ from a plain program's by a relative error of at most 0.0049.
Values may be sent and summed in bfloat16 or wider, within the bound.
No kernel may reach another device: no remote copies, remote signals or barrier semaphores. Data moves between devices by JAX's collectives and lax.ppermute only.
A program may use at most 128 MiB of HBM per device.

v0:
```python
from functools import partial

import jax
import jax.numpy as jnp
from jax import lax
from jax.sharding import PartitionSpec as P

V = 131072
K = 128
BLK = 256
ITERS = 2


def group_step(
    left_blocks, right_blocks, blocks, tiles_all, live, want_row, want_col, group, carry
):
    tile_group = 8
    start = group * tile_group
    row_ids = lax.dynamic_slice_in_dim(blocks[:, 0], start, tile_group)
    col_ids = lax.dynamic_slice_in_dim(blocks[:, 1], start, tile_group)
    tiles = lax.dynamic_slice_in_dim(tiles_all, start, tile_group, 0)
    alive = start + jnp.arange(tile_group, dtype=jnp.int32) < live
    left = left_blocks[row_ids]
    right = right_blocks[col_ids]
    denoms = jnp.einsum("gak,gbk->gab", left, right, preferred_element_type=jnp.float32)
    ratio = jnp.where(alive[:, None, None], tiles.astype(jnp.float32) / denoms, 0.0).astype(
        jnp.bfloat16
    )
    results = []
    place = 0
    row_part = jnp.einsum("gab,gbk->gak", ratio, right, preferred_element_type=jnp.float32)
    results.append(carry[place].at[row_ids].add(row_part))
    place = place + 1
    col_part = jnp.einsum("gab,gak->gbk", ratio, left, preferred_element_type=jnp.float32)
    results.append(carry[place].at[col_ids].add(col_part))
    return tuple(results)


def sweep(left_blocks, right_blocks, blocks, tiles_all, live):
    starts = []
    starts.append(jnp.zeros(left_blocks.shape, jnp.float32))
    starts.append(jnp.zeros(right_blocks.shape, jnp.float32))
    stepper = partial(group_step, left_blocks, right_blocks, blocks, tiles_all, live, True, True)
    turns = (live + 7) // 8
    return lax.fori_loop(0, turns, stepper, tuple(starts))


def local(word_topic, topic_weight, tile_blocks, tile_live, pair_counts):
    blocks = tile_blocks[0, 0]
    live = tile_live[0, 0]
    tiles_all = pair_counts[0, 0]
    weights = word_topic
    shares = topic_weight
    for step in range(ITERS):
        row_phi = lax.all_gather(weights, "col", axis=0, tiled=True)
        col_phi = lax.all_gather(weights, "row", axis=0, tiled=True)
        scaled = (row_phi.astype(jnp.float32) * shares).astype(jnp.bfloat16)
        left_blocks = scaled.reshape(-1, BLK, K)
        right_blocks = col_phi.reshape(-1, BLK, K)
        row_acc, col_acc = sweep(left_blocks, right_blocks, blocks, tiles_all, live)
        row_terms = row_acc.reshape(-1, K)
        col_terms = col_acc.reshape(-1, K)
        row_sum = lax.psum_scatter(row_terms, "col", scatter_dimension=0, tiled=True)
        col_sum = lax.psum_scatter(col_terms, "row", scatter_dimension=0, tiled=True)
        expected = weights.astype(jnp.float32) * (shares * row_sum + col_sum)
        totals = lax.psum(jnp.sum(expected, axis=0), ("row", "col"))
        weights = (V * expected / totals).astype(jnp.bfloat16)
        shares = K * totals / jnp.sum(totals)
    return (weights, shares)


def solution(mesh):
    in_specs = (
        P(("row", "col"), None),
        P(),
        P("row", "col", None, None),
        P("row", "col"),
        P("row", "col", None, None, None),
    )
    out_specs = (P(("row", "col"), None), P())
    return jax.shard_map(local, mesh=mesh, in_specs=in_specs, out_specs=out_specs, check_vma=False)
```

profile of v0, /device:TPU:1, one launch (start us, length us, event | category | flops | bytes accessed | tf_op | source)
XLA Modules:
  0.0 1028.5 jit_solution(16607636807630387287)
XLA Ops:
  9.4 52.8 %all-gather.5.cloned.1.call-done = bf16[8192,128]{1,0:T(8,128)(2,1)} async-done(((bf16[1024,128]{1,0:T(8,128)(2,1)}), bf16[8192,128]{1,0:T(8,128)(2,1)}) %all-gather.5.cloned.1.call-update) | async-done | bytes 2097168 | tf_op jit(solution)/shard_map/all_gather | solution.py:55
  62.1 3.3 multiply_convert_fusion.1
  65.5 57.8 %all-gather.7.cloned.1.call-done = bf16[16384,128]{1,0:T(8,128)(2,1)} async-done(((bf16[1024,128]{1,0:T(8,128)(2,1)}), bf16[16384,128]{1,0:T(8,128)(2,1)}) %all-gather.7.cloned.1.call-update) | async-done | bytes 4194320 | tf_op jit(solution)/shard_map/all_gather | solution.py:56
  123.3 4.2 broadcast.60.clone
  127.6 2.4 broadcast.59.clone
  130.0 108.2 %while.24 = (s32[]{:T(128)}, f32[32,256,128]{2,1,0:T(8,128)}, f32[64,256,128]{2,1,0:T(8,128)}, s32[]{:T(128)}, s32[64,2]{0,1:T(2,128)S(1)}, /*index=5*/s32[]{:T(...) while((s32[]{:T(128)}, f32[32,256,128]{2,1,0:T(8,128)}, ...), condition=%wide.region_3.4_spmd, body=%wide.region_0.3_spmd.sunk | while | flops 405276736 | bytes 17835532 | solution.py:45
  130.1 2.2 gather_fusion
  132.4 2.8 gather_fusion.1
  138.4 3.3 scatter_fusion.1
  142.2 3.3 scatter_fusion
  145.6 2.2 gather_fusion
  147.8 2.8 gather_fusion.1
  153.9 3.4 scatter_fusion.1
  157.7 3.3 scatter_fusion
  161.1 2.2 gather_fusion
  163.3 2.8 gather_fusion.1
  169.4 3.3 scatter_fusion.1
  173.1 3.3 scatter_fusion
  178.7 2.8 gather_fusion.1
  184.8 3.4 scatter_fusion.1
  188.6 3.3 scatter_fusion
  192.0 2.2 gather_fusion
  194.2 2.8 gather_fusion.1
  200.3 3.4 scatter_fusion.1
  204.1 3.2 scatter_fusion
  209.7 2.8 gather_fusion.1
  215.8 3.2 scatter_fusion.1
  219.4 3.3 scatter_fusion
  225.1 2.8 gather_fusion.1
  231.2 3.3 scatter_fusion.1
  234.9 3.3 scatter_fusion
  238.8 103.5 %reduce-scatter.5.cloned.1.call-done = f32[1024,128]{1,0:T(8,128)} async-done(((f32[8192,128]{1,0:T(8,128)}), f32[1024,128]{1,0:T(8,128)}) %reduce-scatter.5.cloned.1.call-update) | async-done | bytes 524304 | tf_op jit(solution)/shard_map/reduce_scatter | solution.py:63
  342.4 106.8 %reduce-scatter.7.cloned.1.call-done = f32[1024,128]{1,0:T(8,128)} async-done(((f32[16384,128]{1,0:T(8,128)}), f32[1024,128]{1,0:T(8,128)}) %reduce-scatter.7.cloned.1.call-update) | async-done | bytes 524304 | tf_op jit(solution)/shard_map/reduce_scatter | solution.py:64
  450.5 65.3 %psum.14 = f32[128]{0:T(128)S(1)} all-reduce(f32[128]{0:T(128)S(1)} %fusion.4), channel_id=1, replica_groups=mesh['row'=16,'col'=8] {'row','col'}, use_global_device_ids=true, to_apply=%region_7.8 | all-reduce | flops 128 | bytes 1024 | tf_op jit(solution)/shard_map/psum | solution.py:66
  519.8 43.9 %all-gather.9.cloned.1.call-done = bf16[8192,128]{1,0:T(8,128)(2,1)} async-done(((bf16[1024,128]{1,0:T(8,128)(2,1)}), bf16[8192,128]{1,0:T(8,128)(2,1)}) %all-gather.9.cloned.1.call-update) | async-done | bytes 2097168 | tf_op jit(solution)/shard_map/all_gather | solution.py:55
  563.7 3.3 multiply_convert_fusion
  567.0 58.3 %all-gather.11.cloned.1.call-done = bf16[16384,128]{1,0:T(8,128)(2,1)} async-done(((bf16[1024,128]{1,0:T(8,128)(2,1)}), bf16[16384,128]{1,0:T(8,128)(2,1)}) %all-gather.11.cloned.1.call-update) | async-done | bytes 4194320 | tf_op jit(solution)/shard_map/all_gather | solution.py:56
  625.3 4.2 broadcast.60
  629.6 2.4 broadcast.59
  632.0 108.2 %while.25 = (s32[]{:T(128)}, f32[32,256,128]{2,1,0:T(8,128)}, f32[64,256,128]{2,1,0:T(8,128)}, s32[]{:T(128)}, s32[64,2]{0,1:T(2,128)S(1)}, /*index=5*/s32[]{:T(...) while((s32[]{:T(128)}, f32[32,256,128]{2,1,0:T(8,128)}, ...), condition=%wide.region_12.13_spmd, body=%wide.region_9.12_spmd.sunk | while | flops 405276736 | bytes 17835532 | solution.py:45
  634.4 2.8 gather_fusion.3
  640.4 3.3 scatter_fusion.3
  644.2 3.3 scatter_fusion.2
  649.8 2.8 gather_fusion.3
  655.9 3.4 scatter_fusion.3
  659.7 3.3 scatter_fusion.2
  665.3 2.8 gather_fusion.3
  671.4 3.3 scatter_fusion.3
  675.1 3.3 scatter_fusion.2
  680.7 2.8 gather_fusion.3
  686.8 3.4 scatter_fusion.3
  690.6 3.3 scatter_fusion.2
  696.2 2.8 gather_fusion.3
  702.3 3.4 scatter_fusion.3
  706.1 3.2 scatter_fusion.2
  711.7 2.8 gather_fusion.3
  717.8 3.2 scatter_fusion.3
  721.4 3.3 scatter_fusion.2
  727.1 2.8 gather_fusion.3
  733.2 3.3 scatter_fusion.3
  736.9 3.3 scatter_fusion.2
  741.0 103.4 %reduce-scatter.9.cloned.1.call-done = f32[1024,128]{1,0:T(8,128)} async-done(((f32[8192,128]{1,0:T(8,128)}), f32[1024,128]{1,0:T(8,128)}) %reduce-scatter.9.cloned.1.call-update) | async-done | bytes 524304 | tf_op jit(solution)/shard_map/reduce_scatter | solution.py:63
  844.4 106.9 %reduce-scatter.11.cloned.1.call-done = f32[1024,128]{1,0:T(8,128)} async-done(((f32[16384,128]{1,0:T(8,128)}), f32[1024,128]{1,0:T(8,128)}) %reduce-scatter.11.cloned.1.call-update) | async-done | bytes 524304 | tf_op jit(solution)/shard_map/reduce_scatter | solution.py:64
  952.6 65.3 %psum.15 = f32[128]{0:T(128)S(1)} all-reduce(f32[128]{0:T(128)S(1)} %fusion.5), channel_id=1, replica_groups=mesh['row'=16,'col'=8] {'row','col'}, use_global_device_ids=true, to_apply=%region_16.17 | all-reduce | flops 128 | bytes 1024 | tf_op jit(solution)/shard_map/psum | solution.py:66
  (154 shorter events, 87.9 us)
Async XLA Ops:
  7.2 55.0 %all-gather.5.cloned.1.call-start = ((), (), s32[]{:S(2)}) async-start(), calls=%async_computation.4 | async-start | bytes 2359296 | tf_op jit(solution)/shard_map/all_gather | solution.py:55
  7.9 115.4 %all-gather.7.cloned.1.call-start = ((), (), s32[]{:S(2)}) async-start(), calls=%async_computation.5 | async-start | bytes 4456448 | tf_op jit(solution)/shard_map/all_gather | solution.py:56
  8.6 333.7 %reduce-scatter.5.cloned.1.call-start = ((), (), s32[]{:S(2)}) async-start(), calls=%async_computation.6 | async-start | bytes 4718592 | tf_op jit(solution)/shard_map/reduce_scatter | solution.py:63
  127.6 2.5 copy-start.2
  238.2 210.9 %reduce-scatter.7.cloned.1.call-start = ((), (), s32[]{:S(2)}) async-start(), calls=%async_computation.7 | async-start | bytes 8912896 | tf_op jit(solution)/shard_map/reduce_scatter | solution.py:64
  238.3 210.9 %copy-start.1 = (bf16[1024,128]{1,0:T(8,128)(2,1)S(1)}, bf16[1024,128]{1,0:T(8,128)(2,1)}, u32[]{:S(2)}) copy-start(bf16[1024,128]{1,0:T(8,128)(2,1)} %param.9) | copy-start | bytes 786436
  238.3 210.9 %copy-start.3 = (f32[128]{0:T(128)S(1)}, f32[128]{0:T(128)}, u32[]{:S(2)}) copy-start(f32[128]{0:T(128)} %param.10) | copy-start | bytes 1540
  238.8 324.9 %all-gather.9.cloned.1.call-start = ((), (), s32[]{:S(2)}) async-start(), calls=%async_computation.8 | async-start | bytes 2359296 | tf_op jit(solution)/shard_map/all_gather | solution.py:55
  517.8 107.5 %all-gather.11.cloned.1.call-start = ((), (), s32[]{:S(2)}) async-start(), calls=%async_computation.9 | async-start | bytes 4456448 | tf_op jit(solution)/shard_map/all_gather | solution.py:56
  518.4 325.9 %reduce-scatter.9.cloned.1.call-start = ((), (), s32[]{:S(2)}) async-start(), calls=%async_computation.10 | async-start | bytes 4718592 | tf_op jit(solution)/shard_map/reduce_scatter | solution.py:63
  740.2 211.0 %reduce-scatter.11.cloned.1.call-start = ((), (), s32[]{:S(2)}) async-start(), calls=%async_computation.11 | async-start | bytes 8912896 | tf_op jit(solution)/shard_map/reduce_scatter | solution.py:64
  740.3 211.0 %copy-start = (bf16[1024,128]{1,0:T(8,128)(2,1)S(1)}, bf16[1024,128]{1,0:T(8,128)(2,1)}, u32[]{:S(2)}) copy-start(bf16[1024,128]{1,0:T(8,128)(2,1)} %divide_convert_fusion.1) | copy-start | bytes 786436
Sparse Core Ops, SparseCore 0:
  9.6 52.4 all-gather.4
  64.6 58.7 all-gather.6
  238.3 103.9 reduce-scatter.4
  346.6 102.5 reduce-scatter.6
  518.0 45.6 all-gather.8
  566.6 58.7 all-gather.10
  740.3 103.9 reduce-scatter.8
  848.7 102.4 reduce-scatter.10
where the time goes:
time: 1030 us
  waiting for transfers between devices  636 us (62%)
  blocking collectives  131 us (13%)
  other arithmetic  119 us (12%)
  local copies, waits for them, and re-layouts  84.5 us (8%)
  matrix products  41.8 us (4%)
  between operations  14.8 us (1%)
    reduce_scatter x2, waiting for transfers between devices, local(): lax.psum_scatter(col_terms, 'row', scatter_dimension=0, tiled=True)  214 us
    reduce_scatter x2, waiting for transfers between devices, local(): lax.psum_scatter(row_terms, 'col', scatter_dimension=0, tiled=True)  207 us
    psum x2, blocking collectives, local(): totals = lax.psum(jnp.sum(expected, axis=0), ('row', 'col'))  131 us
    all_gather x2, waiting for transfers between devices, local(): col_phi = lax.all_gather(weights, 'row', axis=0, tiled=True)  116 us
    all_gather x2, waiting for transfers between devices, local(): row_phi = lax.all_gather(weights, 'col', axis=0, tiled=True)  96.7 us
    scatter-add x14, other arithmetic, group_step(): results.append(carry[place].at[col_ids].add(col_part))  46.4 us
    scatter-add x14, other arithmetic, group_step(): results.append(carry[place].at[row_ids].add(row_part))  46 us
    gather x14, local copies, waits for them, and re-layouts, group_step(): right = right_blocks[col_ids]  39.7 us
  transfers between devices with their start and end apart: 8, of which 8 were waited for; matrix products, arithmetic and copies ran while one was open for 1% of the time, Pallas kernels for 0%

commit v1 on v0

v1 whole, which is shorter than its diff:
```python
import jax
import jax.numpy as jnp
from jax import lax
from jax.experimental import pallas as pl
from jax.experimental.pallas import tpu as pltpu
from jax.sharding import PartitionSpec as P

V = 131072
K = 128
BLK = 256
SLOTS = 64
ITERS = 2
SPAN = 1024
GROUP = 8
AXES = ("row", "col")
ROW_PARTS = (("zh", 2), ("y", 4), ("k", 2))
COL_PARTS = (("x", 4), ("zl", 2))
SIZES = dict(ROW_PARTS + COL_PARTS)


def parts_of(index):
    out = {}
    for name, size in reversed(ROW_PARTS + COL_PARTS):
        out[name] = index % size
        index = index // size
    return out


def index_of(parts):
    index = 0
    for name, size in ROW_PARTS + COL_PARTS:
        index = index * size + parts[name]
    return index


def send(value, part, step):
    pairs = []
    for source in range(128):
        target = parts_of(source)
        target[part] = (target[part] + step) % SIZES[part]
        pairs.append((source, index_of(target)))
    return lax.ppermute(value, AXES, pairs)


def coords():
    row, col = lax.axis_index("row"), lax.axis_index("col")
    return {"zh": row // 8, "y": (row // 2) % 4, "k": row % 2, "x": col // 2, "zl": col % 2}


def tiles_kernel(
    blocks, live, pos, shares, r0, r1, r2, r3, c00, c01, c02, c03, c10, c11, c12, c13, tiles,
    x0, x1, x2, x3, k0, k1, k2, k3, s0, s1, s2, s3, totals,
    rows, scaled, cols, row_acc, col_acc, sem,
):
    group = pl.program_id(0)
    zh, y, k, x, zl = pos[0], pos[1], pos[2], pos[3], pos[4]

    def row_span(back, other):
        return (x + 4 - back) % 4 * 2 + (zl + other) % 2

    def col_span(other_k, back, other):
        return ((zh + other) % 2 * 4 + (y + 4 - back) % 4) * 2 + (k + other_k) % 2

    def at(span):
        return pl.ds(pl.multiple_of(span * SPAN, SPAN), SPAN)

    @pl.when(group == 0)
    def _():
        copies = []
        for back, ref in enumerate((r0, r1, r2, r3)):
            for other in range(2):
                half = ref.at[pl.ds(other * SPAN, SPAN), :]
                copies.append((half, rows.at[at(row_span(back, other)), :]))
        for other_k, refs in enumerate(((c00, c01, c02, c03), (c10, c11, c12, c13))):
            for back, ref in enumerate(refs):
                for other in range(2):
                    half = ref.at[pl.ds(other * SPAN, SPAN), :]
                    copies.append((half, cols.at[at(col_span(other_k, back, other)), :]))
        started = [
            pltpu.make_async_copy(source, target, sem.at[i])
            for i, (source, target) in enumerate(copies)
        ]
        for copy in started:
            copy.start()
        row_acc[...] = jnp.zeros_like(row_acc)
        col_acc[...] = jnp.zeros_like(col_acc)
        for copy in started:
            copy.wait()
        scaled[...] = (rows[...].astype(jnp.float32) * shares[...]).astype(jnp.bfloat16)

    alive = live[0]

    @pl.when(group * GROUP < alive)
    def _():
        for t in range(GROUP):
            slot = group * GROUP + t
            p = pl.multiple_of(jnp.clip(blocks[2 * slot], 0, 31) * BLK, BLK)
            q = pl.multiple_of(jnp.clip(blocks[2 * slot + 1], 0, 63) * BLK, BLK)
            left = scaled[pl.ds(p, BLK), :]
            right = cols[pl.ds(q, BLK), :]
            denom = lax.dot_general(
                left, right, (((1,), (1,)), ((), ())), preferred_element_type=jnp.float32
            )
            ratio = jnp.where(slot < alive, tiles[t].astype(jnp.float32) / denom, 0.0)
            ratio = ratio.astype(jnp.bfloat16)
            row_acc[pl.ds(p, BLK), :] += jnp.dot(ratio, right, preferred_element_type=jnp.float32)
            col_acc[pl.ds(q, BLK), :] += lax.dot_general(
                ratio, left, (((0,), (0,)), ((), ())), preferred_element_type=jnp.float32
            )

    @pl.when(group == pl.num_programs(0) - 1)
    def _():
        total = jnp.zeros((8, K), jnp.float32)
        for step, ref in enumerate((x0, x1, x2, x3)):
            for other in range(2):
                span = (x + step) % 4 * 2 + (zl + other) % 2
                terms = row_acc[at(span), :]
                both = terms * (rows[at(span), :].astype(jnp.float32) * shares[...])
                total += jnp.sum(both.reshape(SPAN // 8, 8, K), axis=0)
                ref[pl.ds(other * SPAN, SPAN), :] = terms.astype(ref.dtype)
        for other_k, refs in enumerate(((k0, k1, k2, k3), (s0, s1, s2, s3))):
            for step, ref in enumerate(refs):
                for other in range(2):
                    span = ((zh + other) % 2 * 4 + (y + step) % 4) * 2 + (k + other_k) % 2
                    terms = col_acc[at(span), :]
                    both = terms * cols[at(span), :].astype(jnp.float32)
                    total += jnp.sum(both.reshape(SPAN // 8, 8, K), axis=0)
                    ref[pl.ds(other * SPAN, SPAN), :] = terms.astype(ref.dtype)
        totals[...] = jnp.broadcast_to(jnp.sum(total, axis=0, keepdims=True), (8, K))


def sweep(blocks, live, pos, shares, row_parts, col_parts, tiles):
    whole = pl.BlockSpec(memory_space=pl.ANY)
    kept = pl.BlockSpec((2 * SPAN, K), lambda g, *_: (0, 0))

    def tile_at(g, blocks, live, pos):
        return (jnp.minimum(g, (live[0] - 1) // GROUP), 0, 0)

    f32 = jax.ShapeDtypeStruct((2 * SPAN, K), jnp.float32)
    b16 = jax.ShapeDtypeStruct((2 * SPAN, K), jnp.bfloat16)
    return pl.pallas_call(
        tiles_kernel,
        grid_spec=pltpu.PrefetchScalarGridSpec(
            num_scalar_prefetch=3,
            grid=(SLOTS // GROUP,),
            in_specs=[pl.BlockSpec((1, K), lambda g, *_: (0, 0))]
            + [whole] * 12
            + [pl.BlockSpec((GROUP, BLK, BLK), tile_at)],
            out_specs=[kept] * 12 + [pl.BlockSpec((8, K), lambda g, *_: (0, 0))],
            scratch_shapes=[
                pltpu.VMEM((8 * SPAN, K), jnp.bfloat16),
                pltpu.VMEM((8 * SPAN, K), jnp.bfloat16),
                pltpu.VMEM((16 * SPAN, K), jnp.bfloat16),
                pltpu.VMEM((8 * SPAN, K), jnp.float32),
                pltpu.VMEM((16 * SPAN, K), jnp.float32),
                pltpu.SemaphoreType.DMA((24,)),
            ],
        ),
        out_shape=[f32, b16, b16, b16]
        + [f32] * 4
        + [b16] * 4
        + [jax.ShapeDtypeStruct((8, K), jnp.float32)],
        compiler_params=pltpu.CompilerParams(vmem_limit_bytes=58 << 20),
        name="tiles",
    )(blocks, live, pos, shares.reshape(1, K), *row_parts, *col_parts, tiles)


def gather_words(weights):
    with jax.named_scope("gather_z"):
        low = send(weights, "zl", 1)
        high = send(weights, "zh", 1)
    row_own = jnp.concatenate([weights, low])
    col_own = jnp.concatenate([weights, high])
    with jax.named_scope("gather_xy"):
        col_parts = [col_own] + [send(col_own, "y", s) for s in (1, 2, 3)]
        row_parts = [row_own] + [send(row_own, "x", s) for s in (1, 2, 3)]
    with jax.named_scope("gather_core"):
        col_other = [send(part, "k", 1) for part in col_parts]
    return row_parts, col_parts + col_other


def sum_everywhere(value, at):
    value = value + send(value, "k", 1)
    for part in ("x", "y"):
        stack = jnp.stack([value] + [send(value, part, s) for s in (3, 2, 1)])
        value = jnp.sum(jnp.roll(stack, at[part], axis=0), axis=0)
    value = value + send(value, "zl", 1)
    return value + send(value, "zh", 1)


def local(word_topic, topic_weight, tile_blocks, tile_live, pair_counts):
    at = coords()
    pos = jnp.stack([at[n] for n in ("zh", "y", "k", "x", "zl")]).astype(jnp.int32)
    blocks = tile_blocks.reshape(2 * SLOTS)
    live = tile_live.reshape(1)
    tiles = pair_counts.reshape(SLOTS, BLK, BLK)
    weights = word_topic
    shares = topic_weight
    for _ in range(ITERS):
        row_parts, col_parts = gather_words(weights)
        outs = sweep(blocks, live, pos, shares, row_parts, col_parts, tiles)
        x_kept, x_sent = outs[0], outs[1:4]
        k_kept, k_sent = outs[4:8], outs[8:12]
        totals = sum_everywhere(outs[12], at)[0]
        with jax.named_scope("scatter_core"):
            k_got = {s: send(k_sent[s], "k", 1) for s in (1, 2, 3, 0)}
        with jax.named_scope("scatter_x"):
            x_got = [send(x_sent[s - 1], "x", s).astype(jnp.float32) for s in (1, 2, 3)]
        y_sum = {s: k_kept[s] + k_got[s].astype(jnp.float32) for s in (1, 2, 3, 0)}
        with jax.named_scope("scatter_y"):
            y_got = [
                send(y_sum[s].astype(jnp.bfloat16), "y", s).astype(jnp.float32) for s in (1, 2, 3)
            ]
        x_sum = x_kept + x_got[0] + x_got[1] + x_got[2]
        y_all = y_sum[0] + y_got[0] + y_got[1] + y_got[2]
        with jax.named_scope("scatter_z"):
            low = send(x_sum[SPAN:].astype(jnp.bfloat16), "zl", 1)
            high = send(y_all[SPAN:].astype(jnp.bfloat16), "zh", 1)
        row_sum = x_sum[:SPAN] + low.astype(jnp.float32)
        col_sum = y_all[:SPAN] + high.astype(jnp.float32)
        expected = weights.astype(jnp.float32) * (shares * row_sum + col_sum)
        weights = (V * expected / totals).astype(jnp.bfloat16)
        shares = K * totals / jnp.sum(totals)
    return (weights, shares)


def solution(mesh):
    in_specs = (
        P(("row", "col"), None),
        P(),
        P("row", "col", None, None),
        P("row", "col"),
        P("row", "col", None, None, None),
    )
    out_specs = (P(("row", "col"), None), P())
    return jax.shard_map(local, mesh=mesh, in_specs=in_specs, out_specs=out_specs, check_vma=False)
```

time: 1030 us -> 292 us (0.28)
  waiting for transfers between devices: 636 us -> 85 us
  starting transfers between devices: 0.32 us -> 139 us
  blocking collectives: 131 us -> 0 us
  other arithmetic: 119 us -> 20.2 us
  local copies, waits for them, and re-layouts: 84.5 us -> 4.13 us
  matrix products: 41.8 us -> 0 us
  Pallas kernels: 0 us -> 37.6 us
  between operations: 14.8 us -> 1.84 us
    reduce_scatter x4 -> x0, waiting for transfers between devices: 421 us -> none  [the longest x2 214 us: local(): lax.psum_scatter(col_terms, 'row', scatter_dimension=0, tiled=True)]
    all_gather x4 -> x0, waiting for transfers between devices: 213 us -> none  [the longest x2 116 us: local(): col_phi = lax.all_gather(weights, 'row', axis=0, tiled=True)]
    ppermute x0 -> x66, starting transfers between devices: none -> 139 us  [send(): return lax.ppermute(value, AXES, pairs)]
    psum x2 -> x0, blocking collectives: 131 us -> none  [local(): totals = lax.psum(jnp.sum(expected, axis=0), ('row', 'col'))]
    scatter-add x28 -> x0, other arithmetic: 92.4 us -> none  [the longest x14 46.4 us: group_step(): results.append(carry[place].at[col_ids].add(col_part))]
    ppermute x0 -> x66, waiting for transfers between devices: none -> 85 us  [send(): return lax.ppermute(value, AXES, pairs)]
    gather x28 -> x0, local copies, waits for them, and re-layouts: 71 us -> none  [the longest x14 39.7 us: group_step(): right = right_blocks[col_ids]]
    dot_general x42 -> x0, matrix products: 41.8 us -> none  [the longest x14 29.2 us: group_step(): jnp.einsum('gak,gbk->gab', left, right, preferred_element_type=jnp.float32)]
  transfers between devices with their start and end apart: 8 -> 66, of which waited for: 8 -> 26; matrix products, arithmetic and copies ran while one was open for 1% -> 8% of each run, Pallas kernels for 0% -> 0%
where the time goes in v1:
time: 292 us; the launch traced here: 288 us
  starting transfers between devices  139 us (48%)
  waiting for transfers between devices  85 us (29%)
  Pallas kernels  37.6 us (13%)
  other arithmetic  20.2 us (7%)
  local copies, waits for them, and re-layouts  4.13 us (1%)
    ppermute x66, starting transfers between devices, send(): return lax.ppermute(value, AXES, pairs)  139 us
    ppermute x66, waiting for transfers between devices, send(): return lax.ppermute(value, AXES, pairs)  85 us
    pallas_call x2, Pallas kernels, sweep(): pl.pallas_call(tiles_kernel, grid_spec=pltpu.PrefetchScalarGridSpec(num_s...  37.6 us
    convert_element_type x6, other arithmetic, local(): y_sum[s].astype(jnp.bfloat16)  8.03 us
  transfers between devices with their start and end apart: 66, of which 26 were waited for; matrix products, arithmetic and copies ran while one was open for 8% of the time, Pallas kernels for 0%

profile of v1, /device:TPU:1, one launch (start us, length us, event | category | flops | bytes accessed | tf_op | source)
XLA Modules:
  0.0 287.7 jit_solution(14117129898500198176)
XLA Ops:
  0.6 2.5 collective-permute-start
  3.2 3.3 %collective-permute-start.4 = (bf16[1024,128]{1,0:T(8,128)(2,1)}, bf16[1024,128]{1,0:T(8,128)(2,1)S(1)}, u32[]{:S(2)}, u32[]{:S(2)}) collective-permute-start(bf16[1024,128]{1,0:T(8,128)(2,1)} %param.7), channel_id=1, source_target_pairs={{0,64},{1,65},{2,66},{3,67},{4,68},{5,69},{6,70},{7,71},{8,72},{9,... | collective-permute-start | bytes 786440 | tf_op jit(solution)/shard_map/gather_z/ppermute | solution.py:42
  7.5 1.9 collective-permute-done
  9.4 2.5 collective-permute-start.3
  12.4 5.6 %collective-permute-done.4 = bf16[1024,128]{1,0:T(8,128)(2,1)S(1)} collective-permute-done((bf16[1024,128]{1,0:T(8,128)(2,1)}, bf16[1024,128]{1,0:T(8,128)(2,1)S(1)}, u32[]{:S(2)}, u32[]{:S(2)}) %collective-permute-start.4) | collective-permute-done | bytes 262176 | tf_op jit(solution)/shard_map/gather_z/ppermute | solution.py:42
  18.1 2.8 collective-permute-start.7
  21.9 1.2 collective-permute-start.1
  24.3 11.1 %collective-permute-start.8 = (bf16[2048,128]{1,0:T(8,128)(2,1)S(1)}, bf16[2048,128]{1,0:T(8,128)(2,1)}, u32[]{:S(2)}, u32[]{:S(2)}) collective-permute-start(bf16[2048,128]{1,0:T(8,128)(2,1)S(1)} %constant_dynamic-update-slice_fusion.2.c00), channel_id=1, source_target_pairs={{0,8},{1,9},{2,10},{3,11},{4,12},{5,13},{6,14},{7,15},{8,0},{9,1},... | collective-permute-start | bytes 1572872 | tf_op jit(solution)/shard_map/gather_core/ppermute | solution.py:42
  35.4 8.8 %collective-permute-start.11 = (bf16[2048,128]{1,0:T(8,128)(2,1)S(1)}, bf16[2048,128]{1,0:T(8,128)(2,1)}, u32[]{:S(2)}, u32[]{:S(2)}) collective-permute-start(bf16[2048,128]{1,0:T(8,128)(2,1)S(1)} %collective-permute-done.7.c03), channel_id=1, source_target_pairs={{0,8},{1,9},{2,10},{3,11},{4,12},{5,13},{6,14},{7,15},{8,0},{9,1},... | collective-permute-start | bytes 1572872 | tf_op jit(solution)/shard_map/gather_core/ppermute | solution.py:42
  44.3 3.2 %collective-permute-done.5.c01 = bf16[2048,128]{1,0:T(8,128)(2,1)} collective-permute-done((bf16[2048,128]{1,0:T(8,128)(2,1)S(1)}, bf16[2048,128]{1,0:T(8,128)(2,1)}, u32[]{:S(2)}, u32[]{:S(2)}) %collective-permute-start.5) | collective-permute-done | bytes 524320 | tf_op jit(solution)/shard_map/gather_xy/ppermute | solution.py:42
  50.9 18.8 %tiles.2 = (f32[2048,128]{1,0:T(8,128)}, bf16[2048,128]{1,0:T(8,128)(2,1)}, bf16[2048,128]{1,0:T(8,128)(2,1)}, bf16[2048,128]{1,0:T(8,128)(2,1)}, f32[2048,128]{...) custom-call(s32[128]{0:T(128)} %reshape.16.blocks, ...), custom_call_target="tpu_custom_call" | custom-call | tf_op jit(solution)/shard_map/tiles/pallas_call | solution.py:141
  69.7 1.9 collective-permute-start.17
  72.1 1.2 collective-permute-done.24
  74.0 1.6 collective-permute-start.27
  75.6 6.9 %collective-permute-start.26 = (f32[8,128]{1,0:T(8,128)S(1)}, f32[8,128]{1,0:T(8,128)S(1)}, u32[]{:S(2)}, u32[]{:S(2)}) collective-permute-start(f32[8,128]{1,0:T(8,128)S(1)} %add.133), channel_id=1, source_target_pairs={{0,4},{1,5},{2,6},{3,7},{4,0},{5,1},{6,2},{7,3},{8,12},{9,13},{10,... | collective-permute-start | bytes 12296 | tf_op jit(solution)/shard_map/ppermute | solution.py:42
  82.6 2.1 collective-permute-start.25
  85.5 1.5 collective-permute-start.29
  90.1 2.4 collective-permute-done.31
  93.3 3.4 %collective-permute-start.13 = (bf16[2048,128]{1,0:T(8,128)(2,1)}, bf16[2048,128]{1,0:T(8,128)(2,1)S(1)}, u32[]{:S(2)}, u32[]{:S(2)}) collective-permute-start(bf16[2048,128]{1,0:T(8,128)(2,1)} %get-tuple-element.31), channel_id=1, source_target_pairs={{0,4},{1,5},{2,6},{3,7},{4,0},{5,1},{6,2},{7,3},{8,12},{9,13},{10,... | collective-permute-start | bytes 1572872 | tf_op jit(solution)/shard_map/scatter_x/ppermute | solution.py:42
  96.8 2.8 collective-permute-start.14
  99.6 5.7 %collective-permute-start.21 = (bf16[2048,128]{1,0:T(8,128)(2,1)}, bf16[2048,128]{1,0:T(8,128)(2,1)S(1)}, u32[]{:S(2)}, u32[]{:S(2)}) collective-permute-start(bf16[2048,128]{1,0:T(8,128)(2,1)} %get-tuple-element.40), channel_id=1, source_target_pairs={{0,8},{1,9},{2,10},{3,11},{4,12},{5,13},{6,14},{7,15},{8,0},{9,1},... | collective-permute-start | bytes 1572872 | tf_op jit(solution)/shard_map/scatter_core/ppermute | solution.py:42
  105.3 1.4 add_convert_fusion.5
  106.7 1.4 add_convert_fusion.4
  108.1 1.8 collective-permute-start.18
  109.9 1.3 add_convert_fusion.3
  111.2 1.9 collective-permute-start.20
  113.1 2.7 collective-permute-done.13
  115.9 2.3 collective-permute-start.22
  118.2 1.5 convert_add_fusion.3
  119.8 2.5 collective-permute-done.18
  122.4 12.1 %collective-permute-done.20 = bf16[2048,128]{1,0:T(8,128)(2,1)S(1)} collective-permute-done((bf16[2048,128]{1,0:T(8,128)(2,1)S(1)}, bf16[2048,128]{1,0:T(8,128)(2,1)S(1)}, u32[]{:S(2)}, u32[]{:S(2)}) %collective-permute-start.20) | collective-permute-done | bytes 524320 | tf_op jit(solution)/shard_map/scatter_y/ppermute | solution.py:42
  134.5 1.5 convert_add_fusion.2
  137.9 5.0 %collective-permute-done.23 = bf16[1024,128]{1,0:T(8,128)(2,1)S(1)} collective-permute-done((bf16[1024,128]{1,0:T(8,128)(2,1)S(1)}, bf16[1024,128]{1,0:T(8,128)(2,1)S(1)}, u32[]{:S(2)}, u32[]{:S(2)}) %collective-permute-start.23) | collective-permute-done | bytes 262176 | tf_op jit(solution)/shard_map/scatter_z/ppermute | solution.py:42
  143.2 6.6 %collective-permute-done.37 = bf16[1024,128]{1,0:T(8,128)(2,1)S(1)} collective-permute-done((bf16[1024,128]{1,0:T(8,128)(2,1)S(1)}, bf16[1024,128]{1,0:T(8,128)(2,1)S(1)}, u32[]{:S(2)}, u32[]{:S(2)}) %collective-permute-start.37) | collective-permute-done | bytes 262176 | tf_op jit(solution)/shard_map/gather_z/ppermute | solution.py:42
  150.8 5.6 %collective-permute-start.35 = (bf16[2048,128]{1,0:T(8,128)(2,1)S(1)}, bf16[2048,128]{1,0:T(8,128)(2,1)S(1)}, u32[]{:S(2)}, u32[]{:S(2)}) collective-permute-start(bf16[2048,128]{1,0:T(8,128)(2,1)S(1)} %get-tuple-element.56.r0), channel_id=1, source_target_pairs={{0,4},{1,5},{2,6},{3,7},{4,0},{5,1},{6,2},{7,3},{8,12},{9,13},{10,... | collective-permute-start | bytes 1572872 | tf_op jit(solution)/shard_map/gather_xy/ppermute | solution.py:42
  156.4 5.6 %collective-permute-start.40 = (bf16[2048,128]{1,0:T(8,128)(2,1)S(1)}, bf16[2048,128]{1,0:T(8,128)(2,1)S(1)}, u32[]{:S(2)}, u32[]{:S(2)}) collective-permute-start(bf16[2048,128]{1,0:T(8,128)(2,1)S(1)} %get-tuple-element.55.c00), channel_id=1, source_target_pairs={{0,48},{1,49},{2,50},{3,51},{4,52},{5,53},{6,54},{7,55},{8,56},{9,... | collective-permute-start | bytes 1572872 | tf_op jit(solution)/shard_map/gather_xy/ppermute | solution.py:42
  162.1 1.9 collective-permute-start.39
  163.9 12.9 %collective-permute-start.34 = (bf16[2048,128]{1,0:T(8,128)(2,1)S(1)}, bf16[2048,128]{1,0:T(8,128)(2,1)S(1)}, u32[]{:S(2)}, u32[]{:S(2)}) collective-permute-start(bf16[2048,128]{1,0:T(8,128)(2,1)S(1)} %get-tuple-element.56.r0), channel_id=1, source_target_pairs={{0,2},{1,3},{2,4},{3,5},{4,6},{5,7},{6,0},{7,1},{8,10},{9,11},{10,... | collective-permute-start | bytes 1572872 | tf_op jit(solution)/shard_map/gather_xy/ppermute | solution.py:42
  176.8 3.7 %collective-permute-start.41 = (bf16[2048,128]{1,0:T(8,128)(2,1)S(1)}, bf16[2048,128]{1,0:T(8,128)(2,1)S(1)}, u32[]{:S(2)}, u32[]{:S(2)}) collective-permute-start(bf16[2048,128]{1,0:T(8,128)(2,1)S(1)} %get-tuple-element.55.c00), channel_id=1, source_target_pairs={{0,8},{1,9},{2,10},{3,11},{4,12},{5,13},{6,14},{7,15},{8,0},{9,1},... | collective-permute-start | bytes 1572872 | tf_op jit(solution)/shard_map/gather_core/ppermute | solution.py:42
  180.6 1.2 collective-permute-start.43
  181.8 6.8 %collective-permute-done.38.c01 = bf16[2048,128]{1,0:T(8,128)(2,1)S(1)} collective-permute-done((bf16[2048,128]{1,0:T(8,128)(2,1)S(1)}, bf16[2048,128]{1,0:T(8,128)(2,1)S(1)}, u32[]{:S(2)}, u32[]{:S(2)}) %collective-permute-start.38) | collective-permute-done | bytes 524320 | tf_op jit(solution)/shard_map/gather_xy/ppermute | solution.py:42
  189.2 1.5 collective-permute-done.42.c11
  191.6 18.7 %tiles.3 = (f32[2048,128]{1,0:T(8,128)}, bf16[2048,128]{1,0:T(8,128)(2,1)}, bf16[2048,128]{1,0:T(8,128)(2,1)}, bf16[2048,128]{1,0:T(8,128)(2,1)}, f32[2048,128]{...) custom-call(s32[128]{0:T(128)} %reshape.16.blocks, ...), custom_call_target="tpu_custom_call" | custom-call | tf_op jit(solution)/shard_map/tiles/pallas_call | solution.py:141
  210.3 2.3 collective-permute-start.50
  213.1 1.2 collective-permute-done.57
  215.7 4.6 %collective-permute-start.59 = (f32[8,128]{1,0:T(8,128)S(1)}, f32[8,128]{1,0:T(8,128)S(1)}, u32[]{:S(2)}, u32[]{:S(2)}) collective-permute-start(f32[8,128]{1,0:T(8,128)S(1)} %add.149), channel_id=1, source_target_pairs={{0,4},{1,5},{2,6},{3,7},{4,0},{5,1},{6,2},{7,3},{8,12},{9,13},{10,... | collective-permute-start | bytes 12296 | tf_op jit(solution)/shard_map/ppermute | solution.py:42
  220.4 2.1 collective-permute-start.58
  223.3 7.8 %collective-permute-start.63 = (f32[8,128]{1,0:T(8,128)S(1)}, f32[8,128]{1,0:T(8,128)S(1)}, u32[]{:S(2)}, u32[]{:S(2)}) collective-permute-start(f32[8,128]{1,0:T(8,128)S(1)} %fusion.24), channel_id=1, source_target_pairs={{0,16},{1,17},{2,18},{3,19},{4,20},{5,21},{6,22},{7,23},{8,24},{9,... | collective-permute-start | bytes 12296 | tf_op jit(solution)/shard_map/ppermute | solution.py:42
  231.1 2.5 collective-permute-start.61
  233.6 1.5 collective-permute-done.62
  235.2 2.7 collective-permute-done.64
  237.9 1.9 collective-permute-start.65
  239.8 3.3 %collective-permute-start.46 = (bf16[2048,128]{1,0:T(8,128)(2,1)}, bf16[2048,128]{1,0:T(8,128)(2,1)S(1)}, u32[]{:S(2)}, u32[]{:S(2)}) collective-permute-start(bf16[2048,128]{1,0:T(8,128)(2,1)} %get-tuple-element.44), channel_id=1, source_target_pairs={{0,4},{1,5},{2,6},{3,7},{4,0},{5,1},{6,2},{7,3},{8,12},{9,13},{10,... | collective-permute-start | bytes 1572872 | tf_op jit(solution)/shard_map/scatter_x/ppermute | solution.py:42
  244.0 5.6 %collective-permute-start.54 = (bf16[2048,128]{1,0:T(8,128)(2,1)}, bf16[2048,128]{1,0:T(8,128)(2,1)S(1)}, u32[]{:S(2)}, u32[]{:S(2)}) collective-permute-start(bf16[2048,128]{1,0:T(8,128)(2,1)} %get-tuple-element.53), channel_id=1, source_target_pairs={{0,8},{1,9},{2,10},{3,11},{4,12},{5,13},{6,14},{7,15},{8,0},{9,1},... | collective-permute-start | bytes 1572872 | tf_op jit(solution)/shard_map/scatter_core/ppermute | solution.py:42
  249.5 1.3 add_convert_fusion.2
  251.0 1.3 add_convert_fusion.1
  252.4 1.3 add_convert_fusion
  253.7 3.4 %collective-permute-start.53 = (bf16[2048,128]{1,0:T(8,128)(2,1)S(1)}, bf16[2048,128]{1,0:T(8,128)(2,1)S(1)}, u32[]{:S(2)}, u32[]{:S(2)}) collective-permute-start(bf16[2048,128]{1,0:T(8,128)(2,1)S(1)} %add_convert_fusion.1), channel_id=1, source_target_pairs={{0,32},{1,33},{2,34},{3,35},{4,36},{5,37},{6,38},{7,39},{8,40},{9,... | collective-permute-start | bytes 1572872 | tf_op jit(solution)/shard_map/scatter_y/ppermute | solution.py:42
  257.2 4.9 %collective-permute-done.46 = bf16[2048,128]{1,0:T(8,128)(2,1)S(1)} collective-permute-done((bf16[2048,128]{1,0:T(8,128)(2,1)}, bf16[2048,128]{1,0:T(8,128)(2,1)S(1)}, u32[]{:S(2)}, u32[]{:S(2)}) %collective-permute-start.46) | collective-permute-done | bytes 524320 | tf_op jit(solution)/shard_map/scatter_x/ppermute | solution.py:42
  263.0 2.5 collective-permute-done.47
  265.6 1.5 convert_add_fusion.1
  267.2 11.3 %collective-permute-done.53 = bf16[2048,128]{1,0:T(8,128)(2,1)S(1)} collective-permute-done((bf16[2048,128]{1,0:T(8,128)(2,1)S(1)}, bf16[2048,128]{1,0:T(8,128)(2,1)S(1)}, u32[]{:S(2)}, u32[]{:S(2)}) %collective-permute-start.53) | collective-permute-done | bytes 524320 | tf_op jit(solution)/shard_map/scatter_y/ppermute | solution.py:42
  278.5 1.5 convert_add_fusion
  282.6 4.3 %collective-permute-done.56 = bf16[1024,128]{1,0:T(8,128)(2,1)S(1)} collective-permute-done((bf16[1024,128]{1,0:T(8,128)(2,1)S(1)}, bf16[1024,128]{1,0:T(8,128)(2,1)S(1)}, u32[]{:S(2)}, u32[]{:S(2)}) %collective-permute-start.56) | collective-permute-done | bytes 262176 | tf_op jit(solution)/shard_map/scatter_z/ppermute | solution.py:42
  (150 shorter events, 25.7 us)
Async XLA Ops:
  0.6 8.8 %collective-permute-start = (bf16[1024,128]{1,0:T(8,128)(2,1)}, bf16[1024,128]{1,0:T(8,128)(2,1)S(1)}, u32[]{:S(2)}, u32[]{:S(2)}) collective-permute-start(bf16[1024,128]{1,0:T(8,128)(2,1)} %param.7), channel_id=1, source_target_pairs={{0,1},{1,0},{2,3},{3,2},{4,5},{5,4},{6,7},{7,6},{8,9},{9,8},{10,11... | collective-permute-start | bytes 786440 | tf_op jit(solution)/shard_map/gather_z/ppermute | solution.py:42
  3.2 14.8 %collective-permute-start.4 = (bf16[1024,128]{1,0:T(8,128)(2,1)}, bf16[1024,128]{1,0:T(8,128)(2,1)S(1)}, u32[]{:S(2)}, u32[]{:S(2)}) collective-permute-start(bf16[1024,128]{1,0:T(8,128)(2,1)} %param.7), channel_id=1, source_target_pairs={{0,64},{1,65},{2,66},{3,67},{4,68},{5,69},{6,70},{7,71},{8,72},{9,... | collective-permute-start | bytes 786440 | tf_op jit(solution)/shard_map/gather_z/ppermute | solution.py:42
  9.4 12.5 %collective-permute-start.3 = (bf16[2048,128]{1,0:T(8,128)(2,1)S(1)}, bf16[2048,128]{1,0:T(8,128)(2,1)S(1)}, u32[]{:S(2)}, u32[]{:S(2)}) collective-permute-start(bf16[2048,128]{1,0:T(8,128)(2,1)S(1)} %constant_dynamic-update-slice_fusion.r0), channel_id=1, source_target_pairs={{0,6},{1,7},{2,0},{3,1},{4,2},{5,3},{6,4},{7,5},{8,14},{9,15},{10,... | collective-permute-start | bytes 1572872 | tf_op jit(solution)/shard_map/gather_xy/ppermute | solution.py:42
  11.9 12.4 %collective-permute-start.2 = (bf16[2048,128]{1,0:T(8,128)(2,1)S(1)}, bf16[2048,128]{1,0:T(8,128)(2,1)S(1)}, u32[]{:S(2)}, u32[]{:S(2)}) collective-permute-start(bf16[2048,128]{1,0:T(8,128)(2,1)S(1)} %constant_dynamic-update-slice_fusion.r0), channel_id=1, source_target_pairs={{0,4},{1,5},{2,6},{3,7},{4,0},{5,1},{6,2},{7,3},{8,12},{9,13},{10,... | collective-permute-start | bytes 1572872 | tf_op jit(solution)/shard_map/gather_xy/ppermute | solution.py:42
  18.1 17.3 %collective-permute-start.7 = (bf16[2048,128]{1,0:T(8,128)(2,1)S(1)}, bf16[2048,128]{1,0:T(8,128)(2,1)S(1)}, u32[]{:S(2)}, u32[]{:S(2)}) collective-permute-start(bf16[2048,128]{1,0:T(8,128)(2,1)S(1)} %constant_dynamic-update-slice_fusion.2.c00), channel_id=1, source_target_pairs={{0,48},{1,49},{2,50},{3,51},{4,52},{5,53},{6,54},{7,55},{8,56},{9,... | collective-permute-start | bytes 1572872 | tf_op jit(solution)/shard_map/gather_xy/ppermute | solution.py:42
  20.9 23.4 %collective-permute-start.6 = (bf16[2048,128]{1,0:T(8,128)(2,1)S(1)}, bf16[2048,128]{1,0:T(8,128)(2,1)S(1)}, u32[]{:S(2)}, u32[]{:S(2)}) collective-permute-start(bf16[2048,128]{1,0:T(8,128)(2,1)S(1)} %constant_dynamic-update-slice_fusion.2.c00), channel_id=1, source_target_pairs={{0,32},{1,33},{2,34},{3,35},{4,36},{5,37},{6,38},{7,39},{8,40},{9,... | collective-permute-start | bytes 1572872 | tf_op jit(solution)/shard_map/gather_xy/ppermute | solution.py:42
  21.2 26.3 %collective-permute-start.5 = (bf16[2048,128]{1,0:T(8,128)(2,1)S(1)}, bf16[2048,128]{1,0:T(8,128)(2,1)}, u32[]{:S(2)}, u32[]{:S(2)}) collective-permute-start(bf16[2048,128]{1,0:T(8,128)(2,1)S(1)} %constant_dynamic-update-slice_fusion.2.c00), channel_id=1, source_target_pairs={{0,16},{1,17},{2,18},{3,19},{4,20},{5,21},{6,22},{7,23},{8,24},{9,... | collective-permute-start | bytes 1572872 | tf_op jit(solution)/shard_map/gather_xy/ppermute | solution.py:42
  21.9 28.8 %collective-permute-start.1 = (bf16[2048,128]{1,0:T(8,128)(2,1)S(1)}, bf16[2048,128]{1,0:T(8,128)(2,1)}, u32[]{:S(2)}, u32[]{:S(2)}) collective-permute-start(bf16[2048,128]{1,0:T(8,128)(2,1)S(1)} %constant_dynamic-update-slice_fusion.r0), channel_id=1, source_target_pairs={{0,2},{1,3},{2,4},{3,5},{4,6},{5,7},{6,0},{7,1},{8,10},{9,11},{10,... | collective-permute-start | bytes 1572872 | tf_op jit(solution)/shard_map/gather_xy/ppermute | solution.py:42
  24.3 26.5 %collective-permute-start.8 = (bf16[2048,128]{1,0:T(8,128)(2,1)S(1)}, bf16[2048,128]{1,0:T(8,128)(2,1)}, u32[]{:S(2)}, u32[]{:S(2)}) collective-permute-start(bf16[2048,128]{1,0:T(8,128)(2,1)S(1)} %constant_dynamic-update-slice_fusion.2.c00), channel_id=1, source_target_pairs={{0,8},{1,9},{2,10},{3,11},{4,12},{5,13},{6,14},{7,15},{8,0},{9,1},... | collective-permute-start | bytes 1572872 | tf_op jit(solution)/shard_map/gather_core/ppermute | solution.py:42
  35.4 15.3 %collective-permute-start.11 = (bf16[2048,128]{1,0:T(8,128)(2,1)S(1)}, bf16[2048,128]{1,0:T(8,128)(2,1)}, u32[]{:S(2)}, u32[]{:S(2)}) collective-permute-start(bf16[2048,128]{1,0:T(8,128)(2,1)S(1)} %collective-permute-done.7.c03), channel_id=1, source_target_pairs={{0,8},{1,9},{2,10},{3,11},{4,12},{5,13},{6,14},{7,15},{8,0},{9,1},... | collective-permute-start | bytes 1572872 | tf_op jit(solution)/shard_map/gather_core/ppermute | solution.py:42
  44.2 6.5 %collective-permute-start.10 = (bf16[2048,128]{1,0:T(8,128)(2,1)S(1)}, bf16[2048,128]{1,0:T(8,128)(2,1)}, u32[]{:S(2)}, u32[]{:S(2)}) collective-permute-start(bf16[2048,128]{1,0:T(8,128)(2,1)S(1)} %collective-permute-done.6.c02), channel_id=1, source_target_pairs={{0,8},{1,9},{2,10},{3,11},{4,12},{5,13},{6,14},{7,15},{8,0},{9,1},... | collective-permute-start | bytes 1572872 | tf_op jit(solution)/shard_map/gather_core/ppermute | solution.py:42
  47.6 3.2 %collective-permute-start.9 = (bf16[2048,128]{1,0:T(8,128)(2,1)}, bf16[2048,128]{1,0:T(8,128)(2,1)}, u32[]{:S(2)}, u32[]{:S(2)}) collective-permute-start(bf16[2048,128]{1,0:T(8,128)(2,1)} %collective-permute-done.5.c01), channel_id=1, source_target_pairs={{0,8},{1,9},{2,10},{3,11},{4,12},{5,13},{6,14},{7,15},{8,0},{9,1},... | collective-permute-start | bytes 1572872 | tf_op jit(solution)/shard_map/gather_core/ppermute | solution.py:42
  69.7 29.8 %collective-permute-start.17 = (bf16[2048,128]{1,0:T(8,128)(2,1)}, bf16[2048,128]{1,0:T(8,128)(2,1)S(1)}, u32[]{:S(2)}, u32[]{:S(2)}) collective-permute-start(bf16[2048,128]{1,0:T(8,128)(2,1)} %get-tuple-element.36), channel_id=1, source_target_pairs={{0,8},{1,9},{2,10},{3,11},{4,12},{5,13},{6,14},{7,15},{8,0},{9,1},... | collective-permute-start | bytes 1572872 | tf_op jit(solution)/shard_map/scatter_core/ppermute | solution.py:42
  71.7 34.9 %collective-permute-start.19 = (bf16[2048,128]{1,0:T(8,128)(2,1)}, bf16[2048,128]{1,0:T(8,128)(2,1)S(1)}, u32[]{:S(2)}, u32[]{:S(2)}) collective-permute-start(bf16[2048,128]{1,0:T(8,128)(2,1)} %get-tuple-element.38), channel_id=1, source_target_pairs={{0,8},{1,9},{2,10},{3,11},{4,12},{5,13},{6,14},{7,15},{8,0},{9,1},... | collective-permute-start | bytes 1572872 | tf_op jit(solution)/shard_map/scatter_core/ppermute | solution.py:42
  74.0 10.6 %collective-permute-start.27 = (f32[8,128]{1,0:T(8,128)S(1)}, f32[8,128]{1,0:T(8,128)S(1)}, u32[]{:S(2)}, u32[]{:S(2)}) collective-permute-start(f32[8,128]{1,0:T(8,128)S(1)} %add.133), channel_id=1, source_target_pairs={{0,2},{1,3},{2,4},{3,5},{4,6},{5,7},{6,0},{7,1},{8,10},{9,11},{10,... | collective-permute-start | bytes 12296 | tf_op jit(solution)/shard_map/ppermute | solution.py:42
  75.6 9.0 %collective-permute-start.26 = (f32[8,128]{1,0:T(8,128)S(1)}, f32[8,128]{1,0:T(8,128)S(1)}, u32[]{:S(2)}, u32[]{:S(2)}) collective-permute-start(f32[8,128]{1,0:T(8,128)S(1)} %add.133), channel_id=1, source_target_pairs={{0,4},{1,5},{2,6},{3,7},{4,0},{5,1},{6,2},{7,3},{8,12},{9,13},{10,... | collective-permute-start | bytes 12296 | tf_op jit(solution)/shard_map/ppermute | solution.py:42
  82.6 2.8 collective-permute-start.25
  85.4 3.7 %collective-permute-start.30 = (f32[8,128]{1,0:T(8,128)S(1)}, f32[8,128]{1,0:T(8,128)S(1)}, u32[]{:S(2)}, u32[]{:S(2)}) collective-permute-start(f32[8,128]{1,0:T(8,128)S(1)} %fusion.40), channel_id=1, source_target_pairs={{0,16},{1,17},{2,18},{3,19},{4,20},{5,21},{6,22},{7,23},{8,24},{9,... | collective-permute-start | bytes 12296 | tf_op jit(solution)/shard_map/ppermute | solution.py:42
  85.5 4.0 %collective-permute-start.29 = (f32[8,128]{1,0:T(8,128)S(1)}, f32[8,128]{1,0:T(8,128)S(1)}, u32[]{:S(2)}, u32[]{:S(2)}) collective-permute-start(f32[8,128]{1,0:T(8,128)S(1)} %fusion.40), channel_id=1, source_target_pairs={{0,32},{1,33},{2,34},{3,35},{4,36},{5,37},{6,38},{7,39},{8,40},{9,... | collective-permute-start | bytes 12296 | tf_op jit(solution)/shard_map/ppermute | solution.py:42
  87.0 2.8 collective-permute-start.28
  89.8 2.7 collective-permute-start.31
  92.5 4.2 %collective-permute-start.32 = (f32[8,128]{1,0:T(8,128)S(1)}, f32[8,128]{1,0:T(8,128)S(1)}, u32[]{:S(2)}, u32[]{:S(2)}) collective-permute-start(f32[8,128]{1,0:T(8,128)S(1)} %add.134), channel_id=1, source_target_pairs={{0,64},{1,65},{2,66},{3,67},{4,68},{5,69},{6,70},{7,71},{8,72},{9,... | collective-permute-start | bytes 12296 | tf_op jit(solution)/shard_map/ppermute | solution.py:42
  92.5 18.7 %collective-permute-start.12 = (bf16[2048,128]{1,0:T(8,128)(2,1)}, bf16[2048,128]{1,0:T(8,128)(2,1)S(1)}, u32[]{:S(2)}, u32[]{:S(2)}) collective-permute-start(bf16[2048,128]{1,0:T(8,128)(2,1)} %get-tuple-element.30), channel_id=1, source_target_pairs={{0,2},{1,3},{2,4},{3,5},{4,6},{5,7},{6,0},{7,1},{8,10},{9,11},{10,... | collective-permute-start | bytes 1572872 | tf_op jit(solution)/shard_map/scatter_x/ppermute | solution.py:42
  93.3 22.5 %collective-permute-start.13 = (bf16[2048,128]{1,0:T(8,128)(2,1)}, bf16[2048,128]{1,0:T(8,128)(2,1)S(1)}, u32[]{:S(2)}, u32[]{:S(2)}) collective-permute-start(bf16[2048,128]{1,0:T(8,128)(2,1)} %get-tuple-element.31), channel_id=1, source_target_pairs={{0,4},{1,5},{2,6},{3,7},{4,0},{5,1},{6,2},{7,3},{8,12},{9,13},{10,... | collective-permute-start | bytes 1572872 | tf_op jit(solution)/shard_map/scatter_x/ppermute | solution.py:42
  96.8 21.4 %collective-permute-start.14 = (bf16[2048,128]{1,0:T(8,128)(2,1)}, bf16[2048,128]{1,0:T(8,128)(2,1)S(1)}, u32[]{:S(2)}, u32[]{:S(2)}) collective-permute-start(bf16[2048,128]{1,0:T(8,128)(2,1)} %get-tuple-element.32), channel_id=1, source_target_pairs={{0,6},{1,7},{2,0},{3,1},{4,2},{5,3},{6,4},{7,5},{8,14},{9,15},{10,... | collective-permute-start | bytes 1572872 | tf_op jit(solution)/shard_map/scatter_x/ppermute | solution.py:42
  99.6 8.6 %collective-permute-start.21 = (bf16[2048,128]{1,0:T(8,128)(2,1)}, bf16[2048,128]{1,0:T(8,128)(2,1)S(1)}, u32[]{:S(2)}, u32[]{:S(2)}) collective-permute-start(bf16[2048,128]{1,0:T(8,128)(2,1)} %get-tuple-element.40), channel_id=1, source_target_pairs={{0,8},{1,9},{2,10},{3,11},{4,12},{5,13},{6,14},{7,15},{8,0},{9,1},... | collective-permute-start | bytes 1572872 | tf_op jit(solution)/shard_map/scatter_core/ppermute | solution.py:42
  106.7 13.2 %collective-permute-start.16 = (bf16[2048,128]{1,0:T(8,128)(2,1)}, bf16[2048,128]{1,0:T(8,128)(2,1)S(1)}, u32[]{:S(2)}, u32[]{:S(2)}) collective-permute-start(bf16[2048,128]{1,0:T(8,128)(2,1)} %get-tuple-element.34), channel_id=1, source_target_pairs={{0,8},{1,9},{2,10},{3,11},{4,12},{5,13},{6,14},{7,15},{8,0},{9,1},... | collective-permute-start | bytes 1572872 | tf_op jit(solution)/shard_map/scatter_core/ppermute | solution.py:42
  108.1 14.3 %collective-permute-start.18 = (bf16[2048,128]{1,0:T(8,128)(2,1)S(1)}, bf16[2048,128]{1,0:T(8,128)(2,1)S(1)}, u32[]{:S(2)}, u32[]{:S(2)}) collective-permute-start(bf16[2048,128]{1,0:T(8,128)(2,1)S(1)} %add_convert_fusion.5), channel_id=1, source_target_pairs={{0,16},{1,17},{2,18},{3,19},{4,20},{5,21},{6,22},{7,23},{8,24},{9,... | collective-permute-start | bytes 1572872 | tf_op jit(solution)/shard_map/scatter_y/ppermute | solution.py:42
  111.2 23.3 %collective-permute-start.20 = (bf16[2048,128]{1,0:T(8,128)(2,1)S(1)}, bf16[2048,128]{1,0:T(8,128)(2,1)S(1)}, u32[]{:S(2)}, u32[]{:S(2)}) collective-permute-start(bf16[2048,128]{1,0:T(8,128)(2,1)S(1)} %add_convert_fusion.4), channel_id=1, source_target_pairs={{0,32},{1,33},{2,34},{3,35},{4,36},{5,37},{6,38},{7,39},{8,40},{9,... | collective-permute-start | bytes 1572872 | tf_op jit(solution)/shard_map/scatter_y/ppermute | solution.py:42
  115.9 18.6 %collective-permute-start.22 = (bf16[2048,128]{1,0:T(8,128)(2,1)S(1)}, bf16[2048,128]{1,0:T(8,128)(2,1)S(1)}, u32[]{:S(2)}, u32[]{:S(2)}) collective-permute-start(bf16[2048,128]{1,0:T(8,128)(2,1)S(1)} %add_convert_fusion.3), channel_id=1, source_target_pairs={{0,48},{1,49},{2,50},{3,51},{4,52},{5,53},{6,54},{7,55},{8,56},{9,... | collective-permute-start | bytes 1572872 | tf_op jit(solution)/shard_map/scatter_y/ppermute | solution.py:42
  119.7 18.1 %collective-permute-start.15 = (bf16[1024,128]{1,0:T(8,128)(2,1)S(1)}, bf16[1024,128]{1,0:T(8,128)(2,1)S(1)}, u32[]{:S(2)}, u32[]{:S(2)}) collective-permute-start(bf16[1024,128]{1,0:T(8,128)(2,1)S(1)} %slice.102), channel_id=1, source_target_pairs={{0,1},{1,0},{2,3},{3,2},{4,5},{5,4},{6,7},{7,6},{8,9},{9,8},{10,11... | collective-permute-start | bytes 786440 | tf_op jit(solution)/shard_map/scatter_z/ppermute | solution.py:42
  136.0 6.8 %collective-permute-start.23 = (bf16[1024,128]{1,0:T(8,128)(2,1)S(1)}, bf16[1024,128]{1,0:T(8,128)(2,1)S(1)}, u32[]{:S(2)}, u32[]{:S(2)}) collective-permute-start(bf16[1024,128]{1,0:T(8,128)(2,1)S(1)} %slice.101), channel_id=1, source_target_pairs={{0,64},{1,65},{2,66},{3,67},{4,68},{5,69},{6,70},{7,71},{8,72},{9,... | collective-permute-start | bytes 786440 | tf_op jit(solution)/shard_map/scatter_z/ppermute | solution.py:42
  143.0 6.8 %collective-permute-start.37 = (bf16[1024,128]{1,0:T(8,128)(2,1)S(1)}, bf16[1024,128]{1,0:T(8,128)(2,1)S(1)}, u32[]{:S(2)}, u32[]{:S(2)}) collective-permute-start(bf16[1024,128]{1,0:T(8,128)(2,1)S(1)} %fusion.10), channel_id=1, source_target_pairs={{0,64},{1,65},{2,66},{3,67},{4,68},{5,69},{6,70},{7,71},{8,72},{9,... | collective-permute-start | bytes 786440 | tf_op jit(solution)/shard_map/gather_z/ppermute | solution.py:42
  143.1 7.3 %collective-permute-start.33 = (bf16[1024,128]{1,0:T(8,128)(2,1)S(1)}, bf16[1024,128]{1,0:T(8,128)(2,1)S(1)}, u32[]{:S(2)}, u32[]{:S(2)}) collective-permute-start(bf16[1024,128]{1,0:T(8,128)(2,1)S(1)} %fusion.10), channel_id=1, source_target_pairs={{0,1},{1,0},{2,3},{3,2},{4,5},{5,4},{6,7},{7,6},{8,9},{9,8},{10,11... | collective-permute-start | bytes 786440 | tf_op jit(solution)/shard_map/gather_z/ppermute | solution.py:42
  150.5 13.4 %collective-permute-start.36 = (bf16[2048,128]{1,0:T(8,128)(2,1)S(1)}, bf16[2048,128]{1,0:T(8,128)(2,1)S(1)}, u32[]{:S(2)}, u32[]{:S(2)}) collective-permute-start(bf16[2048,128]{1,0:T(8,128)(2,1)S(1)} %get-tuple-element.56.r0), channel_id=1, source_target_pairs={{0,6},{1,7},{2,0},{3,1},{4,2},{5,3},{6,4},{7,5},{8,14},{9,15},{10,... | collective-permute-start | bytes 1572872 | tf_op jit(solution)/shard_map/gather_xy/ppermute | solution.py:42
  150.8 26.0 %collective-permute-start.35 = (bf16[2048,128]{1,0:T(8,128)(2,1)S(1)}, bf16[2048,128]{1,0:T(8,128)(2,1)S(1)}, u32[]{:S(2)}, u32[]{:S(2)}) collective-permute-start(bf16[2048,128]{1,0:T(8,128)(2,1)S(1)} %get-tuple-element.56.r0), channel_id=1, source_target_pairs={{0,4},{1,5},{2,6},{3,7},{4,0},{5,1},{6,2},{7,3},{8,12},{9,13},{10,... | collective-permute-start | bytes 1572872 | tf_op jit(solution)/shard_map/gather_xy/ppermute | solution.py:42
  156.4 24.1 %collective-permute-start.40 = (bf16[2048,128]{1,0:T(8,128)(2,1)S(1)}, bf16[2048,128]{1,0:T(8,128)(2,1)S(1)}, u32[]{:S(2)}, u32[]{:S(2)}) collective-permute-start(bf16[2048,128]{1,0:T(8,128)(2,1)S(1)} %get-tuple-element.55.c00), channel_id=1, source_target_pairs={{0,48},{1,49},{2,50},{3,51},{4,52},{5,53},{6,54},{7,55},{8,56},{9,... | collective-permute-start | bytes 1572872 | tf_op jit(solution)/shard_map/gather_xy/ppermute | solution.py:42
  162.1 18.6 %collective-permute-start.39 = (bf16[2048,128]{1,0:T(8,128)(2,1)S(1)}, bf16[2048,128]{1,0:T(8,128)(2,1)S(1)}, u32[]{:S(2)}, u32[]{:S(2)}) collective-permute-start(bf16[2048,128]{1,0:T(8,128)(2,1)S(1)} %get-tuple-element.55.c00), channel_id=1, source_target_pairs={{0,32},{1,33},{2,34},{3,35},{4,36},{5,37},{6,38},{7,39},{8,40},{9,... | collective-permute-start | bytes 1572872 | tf_op jit(solution)/shard_map/gather_xy/ppermute | solution.py:42
  163.9 24.7 %collective-permute-start.38 = (bf16[2048,128]{1,0:T(8,128)(2,1)S(1)}, bf16[2048,128]{1,0:T(8,128)(2,1)S(1)}, u32[]{:S(2)}, u32[]{:S(2)}) collective-permute-start(bf16[2048,128]{1,0:T(8,128)(2,1)S(1)} %get-tuple-element.55.c00), channel_id=1, source_target_pairs={{0,16},{1,17},{2,18},{3,19},{4,20},{5,21},{6,22},{7,23},{8,24},{9,... | collective-permute-start | bytes 1572872 | tf_op jit(solution)/shard_map/gather_xy/ppermute | solution.py:42
  163.9 25.2 %collective-permute-start.34 = (bf16[2048,128]{1,0:T(8,128)(2,1)S(1)}, bf16[2048,128]{1,0:T(8,128)(2,1)S(1)}, u32[]{:S(2)}, u32[]{:S(2)}) collective-permute-start(bf16[2048,128]{1,0:T(8,128)(2,1)S(1)} %get-tuple-element.56.r0), channel_id=1, source_target_pairs={{0,2},{1,3},{2,4},{3,5},{4,6},{5,7},{6,0},{7,1},{8,10},{9,11},{10,... | collective-permute-start | bytes 1572872 | tf_op jit(solution)/shard_map/gather_xy/ppermute | solution.py:42
  176.8 12.4 %collective-permute-start.41 = (bf16[2048,128]{1,0:T(8,128)(2,1)S(1)}, bf16[2048,128]{1,0:T(8,128)(2,1)S(1)}, u32[]{:S(2)}, u32[]{:S(2)}) collective-permute-start(bf16[2048,128]{1,0:T(8,128)(2,1)S(1)} %get-tuple-element.55.c00), channel_id=1, source_target_pairs={{0,8},{1,9},{2,10},{3,11},{4,12},{5,13},{6,14},{7,15},{8,0},{9,1},... | collective-permute-start | bytes 1572872 | tf_op jit(solution)/shard_map/gather_core/ppermute | solution.py:42
  180.5 8.7 %collective-permute-start.44 = (bf16[2048,128]{1,0:T(8,128)(2,1)S(1)}, bf16[2048,128]{1,0:T(8,128)(2,1)S(1)}, u32[]{:S(2)}, u32[]{:S(2)}) collective-permute-start(bf16[2048,128]{1,0:T(8,128)(2,1)S(1)} %collective-permute-done.40.c03), channel_id=1, source_target_pairs={{0,8},{1,9},{2,10},{3,11},{4,12},{5,13},{6,14},{7,15},{8,0},{9,1},... | collective-permute-start | bytes 1572872 | tf_op jit(solution)/shard_map/gather_core/ppermute | solution.py:42
  180.6 8.6 %collective-permute-start.43 = (bf16[2048,128]{1,0:T(8,128)(2,1)S(1)}, bf16[2048,128]{1,0:T(8,128)(2,1)S(1)}, u32[]{:S(2)}, u32[]{:S(2)}) collective-permute-start(bf16[2048,128]{1,0:T(8,128)(2,1)S(1)} %collective-permute-done.39.c02), channel_id=1, source_target_pairs={{0,8},{1,9},{2,10},{3,11},{4,12},{5,13},{6,14},{7,15},{8,0},{9,1},... | collective-permute-start | bytes 1572872 | tf_op jit(solution)/shard_map/gather_core/ppermute | solution.py:42
  188.6 2.0 collective-permute-start.42
  210.3 33.7 %collective-permute-start.50 = (bf16[2048,128]{1,0:T(8,128)(2,1)}, bf16[2048,128]{1,0:T(8,128)(2,1)S(1)}, u32[]{:S(2)}, u32[]{:S(2)}) collective-permute-start(bf16[2048,128]{1,0:T(8,128)(2,1)} %get-tuple-element.49), channel_id=1, source_target_pairs={{0,8},{1,9},{2,10},{3,11},{4,12},{5,13},{6,14},{7,15},{8,0},{9,1},... | collective-permute-start | bytes 1572872 | tf_op jit(solution)/shard_map/scatter_core/ppermute | solution.py:42
  212.6 38.2 %collective-permute-start.52 = (bf16[2048,128]{1,0:T(8,128)(2,1)}, bf16[2048,128]{1,0:T(8,128)(2,1)S(1)}, u32[]{:S(2)}, u32[]{:S(2)}) collective-permute-start(bf16[2048,128]{1,0:T(8,128)(2,1)} %get-tuple-element.51), channel_id=1, source_target_pairs={{0,8},{1,9},{2,10},{3,11},{4,12},{5,13},{6,14},{7,15},{8,0},{9,1},... | collective-permute-start | bytes 1572872 | tf_op jit(solution)/shard_map/scatter_core/ppermute | solution.py:42
  215.0 7.5 %collective-permute-start.60 = (f32[8,128]{1,0:T(8,128)S(1)}, f32[8,128]{1,0:T(8,128)S(1)}, u32[]{:S(2)}, u32[]{:S(2)}) collective-permute-start(f32[8,128]{1,0:T(8,128)S(1)} %add.149), channel_id=1, source_target_pairs={{0,2},{1,3},{2,4},{3,5},{4,6},{5,7},{6,0},{7,1},{8,10},{9,11},{10,... | collective-permute-start | bytes 12296 | tf_op jit(solution)/shard_map/ppermute | solution.py:42
  215.7 6.7 %collective-permute-start.59 = (f32[8,128]{1,0:T(8,128)S(1)}, f32[8,128]{1,0:T(8,128)S(1)}, u32[]{:S(2)}, u32[]{:S(2)}) collective-permute-start(f32[8,128]{1,0:T(8,128)S(1)} %add.149), channel_id=1, source_target_pairs={{0,4},{1,5},{2,6},{3,7},{4,0},{5,1},{6,2},{7,3},{8,12},{9,13},{10,... | collective-permute-start | bytes 12296 | tf_op jit(solution)/shard_map/ppermute | solution.py:42
  220.4 2.8 collective-permute-start.58
  223.3 10.3 %collective-permute-start.63 = (f32[8,128]{1,0:T(8,128)S(1)}, f32[8,128]{1,0:T(8,128)S(1)}, u32[]{:S(2)}, u32[]{:S(2)}) collective-permute-start(f32[8,128]{1,0:T(8,128)S(1)} %fusion.24), channel_id=1, source_target_pairs={{0,16},{1,17},{2,18},{3,19},{4,20},{5,21},{6,22},{7,23},{8,24},{9,... | collective-permute-start | bytes 12296 | tf_op jit(solution)/shard_map/ppermute | solution.py:42
  231.1 4.0 %collective-permute-start.62 = (f32[8,128]{1,0:T(8,128)S(1)}, f32[8,128]{1,0:T(8,128)S(1)}, u32[]{:S(2)}, u32[]{:S(2)}) collective-permute-start(f32[8,128]{1,0:T(8,128)S(1)} %fusion.24), channel_id=1, source_target_pairs={{0,32},{1,33},{2,34},{3,35},{4,36},{5,37},{6,38},{7,39},{8,40},{9,... | collective-permute-start | bytes 12296 | tf_op jit(solution)/shard_map/ppermute | solution.py:42
  231.1 4.0 %collective-permute-start.61 = (f32[8,128]{1,0:T(8,128)S(1)}, f32[8,128]{1,0:T(8,128)S(1)}, u32[]{:S(2)}, u32[]{:S(2)}) collective-permute-start(f32[8,128]{1,0:T(8,128)S(1)} %fusion.24), channel_id=1, source_target_pairs={{0,48},{1,49},{2,50},{3,51},{4,52},{5,53},{6,54},{7,55},{8,56},{9,... | collective-permute-start | bytes 12296 | tf_op jit(solution)/shard_map/ppermute | solution.py:42
  235.1 2.8 collective-permute-start.64
  237.9 5.2 %collective-permute-start.65 = (f32[8,128]{1,0:T(8,128)S(1)}, f32[8,128]{1,0:T(8,128)S(1)}, u32[]{:S(2)}, u32[]{:S(2)}) collective-permute-start(f32[8,128]{1,0:T(8,128)S(1)} %add.150), channel_id=1, source_target_pairs={{0,64},{1,65},{2,66},{3,67},{4,68},{5,69},{6,70},{7,71},{8,72},{9,... | collective-permute-start | bytes 12296 | tf_op jit(solution)/shard_map/ppermute | solution.py:42
  239.8 13.9 %collective-permute-start.45 = (bf16[2048,128]{1,0:T(8,128)(2,1)}, bf16[2048,128]{1,0:T(8,128)(2,1)S(1)}, u32[]{:S(2)}, u32[]{:S(2)}) collective-permute-start(bf16[2048,128]{1,0:T(8,128)(2,1)} %get-tuple-element.43), channel_id=1, source_target_pairs={{0,2},{1,3},{2,4},{3,5},{4,6},{5,7},{6,0},{7,1},{8,10},{9,11},{10,... | collective-permute-start | bytes 1572872 | tf_op jit(solution)/shard_map/scatter_x/ppermute | solution.py:42
  239.8 22.3 %collective-permute-start.46 = (bf16[2048,128]{1,0:T(8,128)(2,1)}, bf16[2048,128]{1,0:T(8,128)(2,1)S(1)}, u32[]{:S(2)}, u32[]{:S(2)}) collective-permute-start(bf16[2048,128]{1,0:T(8,128)(2,1)} %get-tuple-element.44), channel_id=1, source_target_pairs={{0,4},{1,5},{2,6},{3,7},{4,0},{5,1},{6,2},{7,3},{8,12},{9,13},{10,... | collective-permute-start | bytes 1572872 | tf_op jit(solution)/shard_map/scatter_x/ppermute | solution.py:42
  243.1 22.5 %collective-permute-start.47 = (bf16[2048,128]{1,0:T(8,128)(2,1)}, bf16[2048,128]{1,0:T(8,128)(2,1)S(1)}, u32[]{:S(2)}, u32[]{:S(2)}) collective-permute-start(bf16[2048,128]{1,0:T(8,128)(2,1)} %get-tuple-element.45), channel_id=1, source_target_pairs={{0,6},{1,7},{2,0},{3,1},{4,2},{5,3},{6,4},{7,5},{8,14},{9,15},{10,... | collective-permute-start | bytes 1572872 | tf_op jit(solution)/shard_map/scatter_x/ppermute | solution.py:42
  244.0 8.3 %collective-permute-start.54 = (bf16[2048,128]{1,0:T(8,128)(2,1)}, bf16[2048,128]{1,0:T(8,128)(2,1)S(1)}, u32[]{:S(2)}, u32[]{:S(2)}) collective-permute-start(bf16[2048,128]{1,0:T(8,128)(2,1)} %get-tuple-element.53), channel_id=1, source_target_pairs={{0,8},{1,9},{2,10},{3,11},{4,12},{5,13},{6,14},{7,15},{8,0},{9,1},... | collective-permute-start | bytes 1572872 | tf_op jit(solution)/shard_map/scatter_core/ppermute | solution.py:42
  250.9 16.3 %collective-permute-start.49 = (bf16[2048,128]{1,0:T(8,128)(2,1)}, bf16[2048,128]{1,0:T(8,128)(2,1)S(1)}, u32[]{:S(2)}, u32[]{:S(2)}) collective-permute-start(bf16[2048,128]{1,0:T(8,128)(2,1)} %get-tuple-element.47), channel_id=1, source_target_pairs={{0,8},{1,9},{2,10},{3,11},{4,12},{5,13},{6,14},{7,15},{8,0},{9,1},... | collective-permute-start | bytes 1572872 | tf_op jit(solution)/shard_map/scatter_core/ppermute | solution.py:42
  252.3 14.9 %collective-permute-start.51 = (bf16[2048,128]{1,0:T(8,128)(2,1)S(1)}, bf16[2048,128]{1,0:T(8,128)(2,1)S(1)}, u32[]{:S(2)}, u32[]{:S(2)}) collective-permute-start(bf16[2048,128]{1,0:T(8,128)(2,1)S(1)} %add_convert_fusion.2), channel_id=1, source_target_pairs={{0,16},{1,17},{2,18},{3,19},{4,20},{5,21},{6,22},{7,23},{8,24},{9,... | collective-permute-start | bytes 1572872 | tf_op jit(solution)/shard_map/scatter_y/ppermute | solution.py:42
  253.7 24.8 %collective-permute-start.53 = (bf16[2048,128]{1,0:T(8,128)(2,1)S(1)}, bf16[2048,128]{1,0:T(8,128)(2,1)S(1)}, u32[]{:S(2)}, u32[]{:S(2)}) collective-permute-start(bf16[2048,128]{1,0:T(8,128)(2,1)S(1)} %add_convert_fusion.1), channel_id=1, source_target_pairs={{0,32},{1,33},{2,34},{3,35},{4,36},{5,37},{6,38},{7,39},{8,40},{9,... | collective-permute-start | bytes 1572872 | tf_op jit(solution)/shard_map/scatter_y/ppermute | solution.py:42
  262.1 16.4 %collective-permute-start.55 = (bf16[2048,128]{1,0:T(8,128)(2,1)S(1)}, bf16[2048,128]{1,0:T(8,128)(2,1)S(1)}, u32[]{:S(2)}, u32[]{:S(2)}) collective-permute-start(bf16[2048,128]{1,0:T(8,128)(2,1)S(1)} %add_convert_fusion), channel_id=1, source_target_pairs={{0,48},{1,49},{2,50},{3,51},{4,52},{5,53},{6,54},{7,55},{8,56},{9,... | collective-permute-start | bytes 1572872 | tf_op jit(solution)/shard_map/scatter_y/ppermute | solution.py:42
  267.1 15.5 %collective-permute-start.48 = (bf16[1024,128]{1,0:T(8,128)(2,1)S(1)}, bf16[1024,128]{1,0:T(8,128)(2,1)S(1)}, u32[]{:S(2)}, u32[]{:S(2)}) collective-permute-start(bf16[1024,128]{1,0:T(8,128)(2,1)S(1)} %slice.100), channel_id=1, source_target_pairs={{0,1},{1,0},{2,3},{3,2},{4,5},{5,4},{6,7},{7,6},{8,9},{9,8},{10,11... | collective-permute-start | bytes 786440 | tf_op jit(solution)/shard_map/scatter_z/ppermute | solution.py:42
  280.0 6.8 %collective-permute-start.56 = (bf16[1024,128]{1,0:T(8,128)(2,1)S(1)}, bf16[1024,128]{1,0:T(8,128)(2,1)S(1)}, u32[]{:S(2)}, u32[]{:S(2)}) collective-permute-start(bf16[1024,128]{1,0:T(8,128)(2,1)S(1)} %slice.99), channel_id=1, source_target_pairs={{0,64},{1,65},{2,66},{3,67},{4,68},{5,69},{6,70},{7,71},{8,72},{9,... | collective-permute-start | bytes 786440 | tf_op jit(solution)/shard_map/scatter_z/ppermute | solution.py:42
  (23 other events, 593.5 us)

commit v2 on v0

v2 whole, which is shorter than its diff:
```python
from functools import partial

import jax
import jax.numpy as jnp
from jax import lax
from jax.experimental import pallas as pl
from jax.experimental.pallas import tpu as pltpu
from jax.sharding import PartitionSpec as P

V = 131072
K = 128
BLK = 256
SLOTS = 64
ITERS = 2
SPAN = 1024
GROUP = 8
EXTRA = 16
VMEM_MIB = 44
AXES = ("row", "col")
ROW_PARTS = (("zh", 2), ("y", 4), ("k", 2))
COL_PARTS = (("x", 4), ("zl", 2))
SIZES = dict(ROW_PARTS + COL_PARTS)


def parts_of(index):
    out = {}
    for name, size in reversed(ROW_PARTS + COL_PARTS):
        out[name] = index % size
        index = index // size
    return out


def index_of(parts):
    index = 0
    for name, size in ROW_PARTS + COL_PARTS:
        index = index * size + parts[name]
    return index


def send(value, part, step):
    pairs = []
    for source in range(128):
        target = parts_of(source)
        target[part] = (target[part] + step) % SIZES[part]
        pairs.append((source, index_of(target)))
    return lax.ppermute(value, AXES, pairs)


def together(*parts):
    groups = {}
    for place in range(128):
        key = parts_of(place)
        for part in parts:
            key.pop(part)
        groups.setdefault(tuple(key.values()), []).append(place)
    return list(groups.values())


def coords():
    row, col = lax.axis_index("row"), lax.axis_index("col")
    return {"zh": row // 8, "y": (row // 2) % 4, "k": row % 2, "x": col // 2, "zl": col % 2}


def placed(tile_blocks, at):
    p = jnp.clip(tile_blocks[:, 0], 0, 31)
    q = jnp.clip(tile_blocks[:, 1], 0, 63)
    row_span, col_span = p // 4, q // 4
    row_at = (at["x"] + 4 - row_span // 2) % 4 * 2 + (row_span + at["zl"]) % 2
    col_at = (col_span + at["k"]) % 2 * 8 + col_span // 2
    return jnp.concatenate([row_at * 4 + p % 4, col_at * 4 + q % 4]).astype(jnp.int32)


def in_parts(value):
    high = lax.reduce_precision(value, 8, 7)
    middle = lax.reduce_precision(value - high, 8, 7)
    low = value - high - middle
    rows = jnp.stack([high, middle, low])
    return jnp.pad(rows, ((0, EXTRA - 3), (0, 0))).astype(jnp.bfloat16)


def joined(rows):
    rows = rows.astype(jnp.float32)
    return rows[0] + rows[1] + rows[2]


def tiles_kernel(
    first, places, live, shares_in, row_0, row_1, row_2, row_3, own_in, other_in, tiles_in,
    x_0, x_1, x_2, x_3, k_hbm, s_hbm, rows, scaled, cols, shared, tiles, ratios, row_acc, col_acc,
    x_out, k_out, s_out, sem, tile_sem, out_sem,
):
    f32, b16 = jnp.float32, jnp.bfloat16
    row_in = (row_0, row_1, row_2, row_3)
    copies = []
    for i in range(4):
        source = row_in[i].at[pl.ds(0, 2 * SPAN), :]
        copies.append((source, rows.at[pl.ds(2 * i * SPAN, 2 * SPAN), :]))
    if not first:
        for i in range(4):
            source = row_in[i].at[pl.ds(2 * SPAN, EXTRA), :]
            copies.append((source, shared.at[pl.ds(i * EXTRA, EXTRA), :]))
    row_copies = len(copies)
    copies.append((own_in, cols.at[pl.ds(0, 8 * SPAN), :]))
    copies.append((other_in, cols.at[pl.ds(8 * SPAN, 8 * SPAN), :]))
    started = [
        pltpu.make_async_copy(source, target, sem.at[i])
        for i, (source, target) in enumerate(copies)
    ]
    for copy in started:
        copy.start()
    alive = live[0]
    turns = (alive + GROUP - 1) // GROUP

    def fetch(group):
        span = pl.ds(group * GROUP, GROUP)
        return pltpu.make_async_copy(tiles_in.at[span], tiles.at[span], tile_sem.at[group])

    def start(group, carry):
        fetch(group).start()
        return carry

    lax.fori_loop(0, turns, start, 0)
    row_acc[...] = jnp.zeros_like(row_acc)
    col_acc[...] = jnp.zeros_like(col_acc)
    for copy in started[:row_copies]:
        copy.wait()
    if first:
        shares = shares_in[...]
    else:
        totals = jnp.sum(shared[...].astype(f32), axis=0, keepdims=True)
        shares = (K * V / jnp.sum(totals)) * (V / totals)
    scaled[...] = (rows[...].astype(f32) * shares).astype(b16)
    for copy in started[row_copies:]:
        copy.wait()

    def group_step(group, carry):
        fetch(group).wait()
        where = []
        for t in range(GROUP):
            slot = group * GROUP + t
            p = pl.ds(pl.multiple_of(places[slot] * BLK, BLK), BLK)
            q = pl.ds(pl.multiple_of(places[SLOTS + slot] * BLK, BLK), BLK)
            where.append((p, q))
            denom = lax.dot_general(
                scaled[p, :], cols[q, :], (((1,), (1,)), ((), ())), preferred_element_type=f32
            )
            ratio = jnp.where(slot < alive, tiles[slot].astype(f32) / denom, 0.0)
            ratios[t] = ratio.astype(b16)
        for t, (p, q) in enumerate(where):
            row_acc[p, :] += jnp.dot(ratios[t], cols[q, :], preferred_element_type=f32)
            col_acc[q, :] += lax.dot_general(
                ratios[t], scaled[p, :], (((0,), (0,)), ((), ())), preferred_element_type=f32
            )
        return carry

    lax.fori_loop(0, turns, group_step, 0)

    total = jnp.zeros((8, K), f32)
    for i in range(8):
        span = pl.ds(i * SPAN, SPAN)
        terms = row_acc[span, :]
        both = terms * (rows[span, :].astype(f32) * shares + scaled[span, :].astype(f32))
        total += jnp.sum(both.reshape(SPAN // 8, 8, K), axis=0)
        x_out[span, :] = terms.astype(b16)
    written = []
    for step, ref in enumerate((x_0, x_1, x_2, x_3)):
        source = x_out.at[pl.ds((4 - step) % 4 * 2 * SPAN, 2 * SPAN), :]
        written.append(pltpu.make_async_copy(source, ref, out_sem.at[2 + step]))
        written[-1].start()
    total = jnp.sum(total, axis=0, keepdims=True)
    high = total.astype(b16).astype(f32)
    middle = (total - high).astype(b16).astype(f32)
    low = total - high - middle
    at = lax.broadcasted_iota(jnp.int32, (EXTRA, K), 0)
    zero = jnp.zeros((EXTRA, K), f32)
    out = jnp.where(at == 0, high, jnp.where(at == 1, middle, jnp.where(at == 2, low, zero)))
    for i, (ref, hbm) in enumerate(((s_out, s_hbm), (k_out, k_hbm))):
        ref[pl.ds(8 * SPAN, EXTRA), :] = out.astype(b16)
        ref[pl.ds(0, 8 * SPAN), :] = col_acc[pl.ds((1 - i) * 8 * SPAN, 8 * SPAN), :].astype(b16)
        written.append(pltpu.make_async_copy(ref, hbm, out_sem.at[i]))
        written[-1].start()
    for copy in written:
        copy.wait()


def sweep(first, places, live, shares, rows, own_in, other_in, tiles):
    whole = pl.BlockSpec(memory_space=pl.ANY)
    near = pl.BlockSpec(memory_space=pltpu.VMEM)
    far = pl.BlockSpec(memory_space=pltpu.HBM)
    scalars = pl.BlockSpec(memory_space=pltpu.SMEM)
    return pl.pallas_call(
        partial(tiles_kernel, first),
        in_specs=[scalars, scalars, near] + [whole] * 6 + [far],
        out_specs=[far] * 6,
        scratch_shapes=[
            pltpu.VMEM((8 * SPAN, K), jnp.bfloat16),
            pltpu.VMEM((8 * SPAN, K), jnp.bfloat16),
            pltpu.VMEM((16 * SPAN, K), jnp.bfloat16),
            pltpu.VMEM((4 * EXTRA, K), jnp.bfloat16),
            pltpu.VMEM((SLOTS, BLK, BLK), jnp.bfloat16),
            pltpu.VMEM((GROUP, BLK, BLK), jnp.bfloat16),
            pltpu.VMEM((8 * SPAN, K), jnp.float32),
            pltpu.VMEM((16 * SPAN, K), jnp.float32),
            pltpu.VMEM((8 * SPAN, K), jnp.bfloat16),
            pltpu.VMEM((8 * SPAN + EXTRA, K), jnp.bfloat16),
            pltpu.VMEM((8 * SPAN + EXTRA, K), jnp.bfloat16),
            pltpu.SemaphoreType.DMA((10,)),
            pltpu.SemaphoreType.DMA((SLOTS // GROUP,)),
            pltpu.SemaphoreType.DMA((6,)),
        ],
        out_shape=[jax.ShapeDtypeStruct((2 * SPAN, K), jnp.bfloat16)] * 4
        + [
            jax.ShapeDtypeStruct((8 * SPAN + EXTRA, K), jnp.bfloat16),
            jax.ShapeDtypeStruct((8 * SPAN + EXTRA, K), jnp.bfloat16),
        ],
        compiler_params=pltpu.CompilerParams(vmem_limit_bytes=VMEM_MIB << 20),
        name="tiles",
    )(places, live, shares.reshape(1, K), *rows, own_in, other_in, tiles)


def after(value, *others):
    return lax.optimization_barrier((value, *others))[0]


def gather_words(weights, totals, tiles):
    if totals is None:
        low = send(weights, "zl", 1)
        row_sent = jnp.concatenate([weights, low])
    else:
        low = send(jnp.concatenate([weights, in_parts(totals)]), "zl", 1)
        both = in_parts(totals + joined(low[SPAN:]))
        row_sent = jnp.concatenate([weights, low[:SPAN], both])
    rows = [row_sent] + [send(row_sent, "x", s) for s in (1, 2, 3)]
    copies = after(jnp.broadcast_to(weights[None], (8, SPAN, K)), row_sent)
    own = lax.all_to_all(copies, AXES, 0, 0, axis_index_groups=together("zh", "y"))
    if totals is None:
        tiles = after(tiles, row_sent).astype(jnp.bfloat16)
        own = after(own, tiles)
    own = after(own, *rows[1:])
    own = own.reshape(8 * SPAN, K)
    return (rows, own, send(own, "k", 1)), tiles


def scatter_terms(x_0, x_1, x_2, x_3, k_out, s_out):
    f32, b16 = jnp.float32, jnp.bfloat16
    x_got = [send(x, "x", s + 1) for s, x in enumerate((x_1, x_2, x_3))]
    x_sum = x_0.astype(f32) + sum(x.astype(f32) for x in x_got)
    s_got = send(s_out, "k", 1)
    both = k_out[: 8 * SPAN].astype(f32) + s_got[: 8 * SPAN].astype(f32)
    pair = in_parts(joined(k_out[8 * SPAN :]) + joined(s_got[8 * SPAN :]))
    sent = jnp.concatenate(
        [both.astype(b16).reshape(8, SPAN, K), jnp.broadcast_to(pair[None], (8, EXTRA, K))], axis=1
    )
    got = lax.all_to_all(sent, AXES, 0, 0, axis_index_groups=together("zh", "y"))
    low = send(x_sum[SPAN:].astype(b16), "zl", 1)
    got = after(got, low)
    col_sum = jnp.sum(got[:, :SPAN].astype(f32), axis=0)
    totals = jnp.sum(got[:, SPAN:].astype(f32), axis=(0, 1))
    row_sum = x_sum[:SPAN] + low.astype(f32)
    return row_sum, col_sum, totals


def sum_columns(value, at):
    value = jnp.broadcast_to(value[None], (8, K))
    stack = jnp.stack([value] + [send(value, "x", s) for s in (3, 2, 1)])
    value = jnp.sum(jnp.roll(stack, at["x"], axis=0), axis=0)
    return (value + send(value, "zl", 1))[0]


def local(word_topic, topic_weight, tile_blocks, tile_live, pair_counts):
    at = coords()
    places = placed(tile_blocks[0, 0], at)
    live = tile_live.reshape(1)
    tiles = pair_counts.reshape(SLOTS, BLK, BLK)
    weights, shares, totals = word_topic, topic_weight, None
    for step in range(ITERS):
        gathered, tiles = gather_words(weights, totals, tiles)
        outs = sweep(step == 0, places, live, shares, *gathered, tiles)
        row_sum, col_sum, totals = scatter_terms(*outs)
        if step > 0:
            shares = (K * V / jnp.sum(before)) * (V / before)
        expected = weights.astype(jnp.float32) * (shares * row_sum + col_sum)
        if step < ITERS - 1:
            weights = expected.astype(jnp.bfloat16)
            before = sum_columns(totals, at)
    totals = sum_columns(totals, at)
    return (V * expected / totals).astype(jnp.bfloat16), K * totals / jnp.sum(totals)


def solution(mesh):
    in_specs = (
        P(("row", "col"), None),
        P(),
        P("row", "col", None, None),
        P("row", "col"),
        P("row", "col", None, None, None),
    )
    out_specs = (P(("row", "col"), None), P())
    return jax.shard_map(local, mesh=mesh, in_specs=in_specs, out_specs=out_specs, check_vma=False)
```

time: 1030 us -> 253 us (0.25)
  waiting for transfers between devices: 636 us -> 123 us
  blocking collectives: 131 us -> 0 us
  other arithmetic: 119 us -> 27.7 us
  local copies, waits for them, and re-layouts: 84.5 us -> 9.04 us
  starting transfers between devices: 0.32 us -> 70 us
  matrix products: 41.8 us -> 0 us
  Pallas kernels: 0 us -> 16.5 us
  between operations: 14.8 us -> 2.46 us
    reduce_scatter x4 -> x0, waiting for transfers between devices: 421 us -> none  [the longest x2 214 us: local(): lax.psum_scatter(col_terms, 'row', scatter_dimension=0, tiled=True)]
    all_gather x4 -> x0, waiting for transfers between devices: 213 us -> none  [the longest x2 116 us: local(): col_phi = lax.all_gather(weights, 'row', axis=0, tiled=True)]
    psum x2 -> x0, blocking collectives: 131 us -> none  [local(): totals = lax.psum(jnp.sum(expected, axis=0), ('row', 'col'))]
    ppermute x0 -> x28, waiting for transfers between devices: none -> 107 us  [send(): return lax.ppermute(value, AXES, pairs)]
    scatter-add x28 -> x0, other arithmetic: 92.4 us -> none  [the longest x14 46.4 us: group_step(): results.append(carry[place].at[col_ids].add(col_part))]
    gather x28 -> x0, local copies, waits for them, and re-layouts: 71 us -> none  [the longest x14 39.7 us: group_step(): right = right_blocks[col_ids]]
    ppermute x0 -> x28, starting transfers between devices: none -> 43.4 us  [send(): return lax.ppermute(value, AXES, pairs)]
    dot_general x42 -> x0, matrix products: 41.8 us -> none  [the longest x14 29.2 us: group_step(): jnp.einsum('gak,gbk->gab', left, right, preferred_element_type=jnp.float32)]
  transfers between devices with their start and end apart: 8 -> 32, of which waited for: 8 -> 22; matrix products, arithmetic and copies ran while one was open for 1% -> 6% of each run, Pallas kernels for 0% -> 0%
where the time goes in v2:
time: 253 us; the launch traced here: 248 us
  waiting for transfers between devices  123 us (49%)
  starting transfers between devices  70 us (28%)
  other arithmetic  27.7 us (11%)
  Pallas kernels  16.5 us (7%)
  local copies, waits for them, and re-layouts  9.04 us (4%)
    ppermute x28, waiting for transfers between devices, send(): return lax.ppermute(value, AXES, pairs)  107 us
    ppermute x28, starting transfers between devices, send(): return lax.ppermute(value, AXES, pairs)  43.4 us
    pallas_call x2, Pallas kernels, sweep(): pl.pallas_call(partial(tiles_kernel, first), in_specs=[scalars, scalars,...  16.5 us
    all_to_all x2, waiting for transfers between devices, gather_words(): lax.all_to_all(copies, AXES, 0, 0, axis_index_groups=together('zh', 'y'))  15.6 us
    all_to_all x2, starting transfers between devices, scatter_terms(): lax.all_to_all(sent, AXES, 0, 0, axis_index_groups=together('zh', 'y'))  13.6 us
    all_to_all x2, starting transfers between devices, gather_words(): lax.all_to_all(copies, AXES, 0, 0, axis_index_groups=together('zh', 'y'))  13 us
    convert_element_type x1, other arithmetic, gather_words(): tiles = after(tiles, row_sent).astype(jnp.bfloat16)  9.36 us
  transfers between devices with their start and end apart: 32, of which 22 were waited for; matrix products, arithmetic and copies ran while one was open for 6% of the time, Pallas kernels for 0%

profile of v2, /device:TPU:1, one launch (start us, length us, event | category | flops | bytes accessed | tf_op | source)
XLA Modules:
  0.0 248.5 jit_solution(13300527218573038082)
XLA Ops:
  0.6 2.5 %collective-permute-start = (bf16[1024,128]{1,0:T(8,128)(2,1)}, bf16[1024,128]{1,0:T(8,128)(2,1)S(1)}, u32[]{:S(2)}, u32[]{:S(2)}) collective-permute-start(bf16[1024,128]{1,0:T(8,128)(2,1)} %param.7), channel_id=1, source_target_pairs={{0,1},{1,0},{2,3},{3,2},{4,5},{5,4},{6,7},{7,6},{8,9},{9,8},{10,11... | collective-permute-start | bytes 786440 | tf_op jit(solution)/shard_map/ppermute | solution.py:46
  3.2 1.0 constant_dynamic-update-slice_fusion.1
  4.2 5.2 %collective-permute-done = bf16[1024,128]{1,0:T(8,128)(2,1)S(1)} collective-permute-done((bf16[1024,128]{1,0:T(8,128)(2,1)}, bf16[1024,128]{1,0:T(8,128)(2,1)S(1)}, u32[]{:S(2)}, u32[]{:S(2)}) %collective-permute-start) | collective-permute-done | bytes 262176 | tf_op jit(solution)/shard_map/ppermute | solution.py:46
  9.4 2.5 %broadcast_in_dim.15 = bf16[8,1024,128]{2,1,0:T(8,128)(2,1)} broadcast(bf16[1024,128]{1,0:T(8,128)(2,1)} %param.7), dimensions={1,2} | broadcast | bytes 2359296 | tf_op jit(solution)/shard_map/broadcast_in_dim | solution.py:233
  12.0 7.0 %all-to-all-start = ((bf16[8,1024,128]{2,1,0:T(8,128)(2,1)}), bf16[8,1024,128]{2,1,0:T(8,128)(2,1)S(1)}, u32[]{:S(2)}, u32[]{:S(2)}) async-start(bf16[8,1024,128]{2,1,0:T(8,128)(2,1)} %broadcast_in_dim.15), calls=%async_computation | async-start | bytes 4194304 | tf_op jit(solution)/shard_map/all_to_all | solution.py:234
  19.0 2.5 collective-permute-start.3
  21.5 0.5 collective-permute-start.2
  22.0 0.6 collective-permute-start.1
  22.6 9.4 %convert_element_type.102.tiles_in = bf16[64,256,256]{2,1,0:T(8,128)(2,1)} convert(s32[64,256,256]{2,1,0:T(8,128)} %bitcast.63) | non-fusion elementwise | flops 4194304 | bytes 25165824 | tf_op jit(solution)/shard_map/convert_element_type | solution.py:236
  32.0 15.6 %all-to-all-done = bf16[8,1024,128]{2,1,0:T(8,128)(2,1)S(1)} async-done(((bf16[8,1024,128]{2,1,0:T(8,128)(2,1)}), bf16[8,1024,128]{2,1,0:T(8,128)(2,1)S(1)}, u32[]{:S(2)}, u32[]{:S(2)}) %all-to-all-start) | async-done | bytes 2097184 | tf_op jit(solution)/shard_map/all_to_all | solution.py:234
  47.6 0.6 collective-permute-done.1.row_1
  48.2 0.5 collective-permute-start.4
  49.5 3.1 %collective-permute-done.4.other_in = bf16[8192,128]{1,0:T(8,128)(2,1)} collective-permute-done((bf16[8192,128]{1,0:T(8,128)(2,1)S(1)}, bf16[8192,128]{1,0:T(8,128)(2,1)}, u32[]{:S(2)}, u32[]{:S(2)}) %collective-permute-start.4) | collective-permute-done | bytes 2097184 | tf_op jit(solution)/shard_map/ppermute | solution.py:46
  52.6 8.3 %tiles.2 = (bf16[2048,128]{1,0:T(8,128)(2,1)S(1)}, bf16[2048,128]{1,0:T(8,128)(2,1)S(1)}, bf16[2048,128]{1,0:T(8,128)(2,1)S(1)}, bf16[2048,128]{1,0:T(8,128)(2,1...) custom-call(s32[128]{0:T(128)S(1)} %pad_add_fusion.places, s32[1]{0:T(128)} %bitcast.55.live, ...), custom_call_target="tpu_custom_call" | custom-call | tf_op jit(solution)/shard_map/tiles/pallas_call | solution.py:190
  61.0 6.7 %collective-permute-start.9 = (bf16[8208,128]{1,0:T(8,128)(2,1)}, bf16[8208,128]{1,0:T(8,128)(2,1)S(1)}, u32[]{:S(2)}, u32[]{:S(2)}) collective-permute-start(bf16[8208,128]{1,0:T(8,128)(2,1)} %get-tuple-element.32), channel_id=1, source_target_pairs={{0,8},{1,9},{2,10},{3,11},{4,12},{5,13},{6,14},{7,15},{8,0},{9,1},... | collective-permute-start | bytes 6303752 | tf_op jit(solution)/shard_map/ppermute | solution.py:46
  67.7 0.7 slice_convert_fusion.6
  68.4 3.3 %collective-permute-done.9 = bf16[8208,128]{1,0:T(8,128)(2,1)S(1)} collective-permute-done((bf16[8208,128]{1,0:T(8,128)(2,1)}, bf16[8208,128]{1,0:T(8,128)(2,1)S(1)}, u32[]{:S(2)}, u32[]{:S(2)}) %collective-permute-start.9) | collective-permute-done | bytes 2101280 | tf_op jit(solution)/shard_map/ppermute | solution.py:46
  71.7 2.1 add_convert_fusion.1
  73.9 1.6 pad_maximum_fusion
  75.5 6.8 %all-to-all-start.1 = ((bf16[8,1040,128]{2,1,0:T(8,128)(2,1)}), bf16[8,1040,128]{2,1,0:T(8,128)(2,1)}, u32[]{:S(2)}, u32[]{:S(2)}) async-start(bf16[8,1040,128]{2,1,0:T(8,128)(2,1)} %pad_maximum_fusion), calls=%async_computation.1 | async-start | bytes 4259840 | tf_op jit(solution)/shard_map/all_to_all | solution.py:253
  82.5 2.6 %collective-permute-start.7 = (bf16[2048,128]{1,0:T(8,128)(2,1)S(1)}, bf16[2048,128]{1,0:T(8,128)(2,1)S(1)}, u32[]{:S(2)}, u32[]{:S(2)}) collective-permute-start(bf16[2048,128]{1,0:T(8,128)(2,1)S(1)} %copy-done.12), channel_id=1, source_target_pairs={{0,6},{1,7},{2,0},{3,1},{4,2},{5,3},{6,4},{7,5},{8,14},{9,15},{10,... | collective-permute-start | bytes 1572872 | tf_op jit(solution)/shard_map/ppermute | solution.py:46
  85.1 22.6 %collective-permute-done.5 = bf16[2048,128]{1,0:T(8,128)(2,1)S(1)} collective-permute-done((bf16[2048,128]{1,0:T(8,128)(2,1)S(1)}, bf16[2048,128]{1,0:T(8,128)(2,1)S(1)}, u32[]{:S(2)}, u32[]{:S(2)}) %collective-permute-start.5) | collective-permute-done | bytes 524320 | tf_op jit(solution)/shard_map/ppermute | solution.py:46
  108.5 6.1 %collective-permute-done.8 = bf16[1024,128]{1,0:T(8,128)(2,1)S(1)} collective-permute-done((bf16[1024,128]{1,0:T(8,128)(2,1)S(1)}, bf16[1024,128]{1,0:T(8,128)(2,1)S(1)}, u32[]{:S(2)}, u32[]{:S(2)}) %collective-permute-start.8) | collective-permute-done | bytes 262176 | tf_op jit(solution)/shard_map/ppermute | solution.py:46
  114.6 0.8 convert_reduce_fusion.3
  115.4 1.9 convert_reduce_fusion.1
  117.9 5.0 %collective-permute-done.14 = bf16[1040,128]{1,0:T(8,128)(2,1)S(1)} collective-permute-done((bf16[1040,128]{1,0:T(8,128)(2,1)S(1)}, bf16[1040,128]{1,0:T(8,128)(2,1)S(1)}, u32[]{:S(2)}, u32[]{:S(2)}) %collective-permute-start.14) | collective-permute-done | bytes 266272 | tf_op jit(solution)/shard_map/ppermute | solution.py:46
  123.0 1.6 broadcast_in_dim.18
  124.6 6.0 %all-to-all-start.2 = ((bf16[8,1024,128]{2,1,0:T(8,128)(2,1)}), bf16[8,1024,128]{2,1,0:T(8,128)(2,1)S(1)}, u32[]{:S(2)}, u32[]{:S(2)}) async-start(bf16[8,1024,128]{2,1,0:T(8,128)(2,1)} %broadcast_in_dim.18), calls=%async_computation.2 | async-start | bytes 4194304 | tf_op jit(solution)/shard_map/all_to_all | solution.py:234
  130.5 5.8 %collective-permute-start.17 = (bf16[2064,128]{1,0:T(8,128)(2,1)S(1)}, bf16[2064,128]{1,0:T(8,128)(2,1)S(1)}, u32[]{:S(2)}, u32[]{:S(2)}) collective-permute-start(bf16[2064,128]{1,0:T(8,128)(2,1)S(1)} %pad_maximum_fusion.2.row_0), channel_id=1, source_target_pairs={{0,6},{1,7},{2,0},{3,1},{4,2},{5,3},{6,4},{7,5},{8,14},{9,15},{10,... | collective-permute-start | bytes 1585160 | tf_op jit(solution)/shard_map/ppermute | solution.py:46
  137.0 8.6 %collective-permute-done.17.row_3 = bf16[2064,128]{1,0:T(8,128)(2,1)S(1)} collective-permute-done((bf16[2064,128]{1,0:T(8,128)(2,1)S(1)}, bf16[2064,128]{1,0:T(8,128)(2,1)S(1)}, u32[]{:S(2)}, u32[]{:S(2)}) %collective-permute-start.17) | collective-permute-done | bytes 528416 | tf_op jit(solution)/shard_map/ppermute | solution.py:46
  145.6 2.8 %collective-permute-done.16.row_2 = bf16[2064,128]{1,0:T(8,128)(2,1)S(1)} collective-permute-done((bf16[2064,128]{1,0:T(8,128)(2,1)S(1)}, bf16[2064,128]{1,0:T(8,128)(2,1)S(1)}, u32[]{:S(2)}, u32[]{:S(2)}) %collective-permute-start.16) | collective-permute-done | bytes 528416 | tf_op jit(solution)/shard_map/ppermute | solution.py:46
  148.4 0.8 copy-done
  149.2 13.9 %collective-permute-done.15.row_1 = bf16[2064,128]{1,0:T(8,128)(2,1)S(1)} collective-permute-done((bf16[2064,128]{1,0:T(8,128)(2,1)S(1)}, bf16[2064,128]{1,0:T(8,128)(2,1)S(1)}, u32[]{:S(2)}, u32[]{:S(2)}) %collective-permute-start.15) | collective-permute-done | bytes 528416 | tf_op jit(solution)/shard_map/ppermute | solution.py:46
  163.1 0.8 copy-done.2
  163.9 0.5 collective-permute-start.18
  164.4 3.8 %collective-permute-done.18.other_in = bf16[8192,128]{1,0:T(8,128)(2,1)S(1)} collective-permute-done((bf16[8192,128]{1,0:T(8,128)(2,1)S(1)}, bf16[8192,128]{1,0:T(8,128)(2,1)S(1)}, u32[]{:S(2)}, u32[]{:S(2)}) %collective-permute-start.18) | collective-permute-done | bytes 2097184 | tf_op jit(solution)/shard_map/ppermute | solution.py:46
  168.2 1.0 copy-done.1
  169.2 1.0 copy-done.3
  170.3 8.2 %tiles.3 = (bf16[2048,128]{1,0:T(8,128)(2,1)S(1)}, bf16[2048,128]{1,0:T(8,128)(2,1)S(1)}, bf16[2048,128]{1,0:T(8,128)(2,1)S(1)}, bf16[2048,128]{1,0:T(8,128)(2,1...) custom-call(s32[128]{0:T(128)S(1)} %pad_add_fusion.places, s32[1]{0:T(128)} %bitcast.56.live, ...), custom_call_target="tpu_custom_call" | custom-call | tf_op jit(solution)/shard_map/tiles/pallas_call | solution.py:190
  178.5 6.7 %collective-permute-start.23 = (bf16[8208,128]{1,0:T(8,128)(2,1)}, bf16[8208,128]{1,0:T(8,128)(2,1)S(1)}, u32[]{:S(2)}, u32[]{:S(2)}) collective-permute-start(bf16[8208,128]{1,0:T(8,128)(2,1)} %get-tuple-element.41), channel_id=1, source_target_pairs={{0,8},{1,9},{2,10},{3,11},{4,12},{5,13},{6,14},{7,15},{8,0},{9,1},... | collective-permute-start | bytes 6303752 | tf_op jit(solution)/shard_map/ppermute | solution.py:46
  185.3 0.7 slice_convert_fusion.5
  186.0 3.3 %collective-permute-done.23 = bf16[8208,128]{1,0:T(8,128)(2,1)S(1)} collective-permute-done((bf16[8208,128]{1,0:T(8,128)(2,1)}, bf16[8208,128]{1,0:T(8,128)(2,1)S(1)}, u32[]{:S(2)}, u32[]{:S(2)}) %collective-permute-start.23) | collective-permute-done | bytes 2101280 | tf_op jit(solution)/shard_map/ppermute | solution.py:46
  189.3 2.1 add_convert_fusion
  191.5 1.5 pad_maximum_fusion.1
  193.0 6.8 %all-to-all-start.3 = ((bf16[8,1040,128]{2,1,0:T(8,128)(2,1)}), bf16[8,1040,128]{2,1,0:T(8,128)(2,1)}, u32[]{:S(2)}, u32[]{:S(2)}) async-start(bf16[8,1040,128]{2,1,0:T(8,128)(2,1)} %pad_maximum_fusion.1), calls=%async_computation.3 | async-start | bytes 4259840 | tf_op jit(solution)/shard_map/all_to_all | solution.py:253
  200.0 2.6 %collective-permute-start.21 = (bf16[2048,128]{1,0:T(8,128)(2,1)S(1)}, bf16[2048,128]{1,0:T(8,128)(2,1)S(1)}, u32[]{:S(2)}, u32[]{:S(2)}) collective-permute-start(bf16[2048,128]{1,0:T(8,128)(2,1)S(1)} %copy-done.10), channel_id=1, source_target_pairs={{0,6},{1,7},{2,0},{3,1},{4,2},{5,3},{6,4},{7,5},{8,14},{9,15},{10,... | collective-permute-start | bytes 1572872 | tf_op jit(solution)/shard_map/ppermute | solution.py:46
  202.6 22.6 %collective-permute-done.19 = bf16[2048,128]{1,0:T(8,128)(2,1)S(1)} collective-permute-done((bf16[2048,128]{1,0:T(8,128)(2,1)S(1)}, bf16[2048,128]{1,0:T(8,128)(2,1)S(1)}, u32[]{:S(2)}, u32[]{:S(2)}) %collective-permute-start.19) | collective-permute-done | bytes 524320 | tf_op jit(solution)/shard_map/ppermute | solution.py:46
  226.0 1.2 collective-permute-start.12
  227.2 3.1 %collective-permute-start.11 = (f32[8,128]{1,0:T(8,128)S(1)}, f32[8,128]{1,0:T(8,128)S(1)}, u32[]{:S(2)}, u32[]{:S(2)}) collective-permute-start(f32[8,128]{1,0:T(8,128)S(1)} %broadcast_in_dim.17), channel_id=1, source_target_pairs={{0,4},{1,5},{2,6},{3,7},{4,0},{5,1},{6,2},{7,3},{8,12},{9,13},{10,... | collective-permute-start | bytes 12296 | tf_op jit(solution)/shard_map/ppermute | solution.py:46
  230.3 1.0 collective-permute-done.11
  231.4 1.7 collective-permute-done.10
  233.1 1.5 collective-permute-start.13
  234.6 1.1 collective-permute-done.13
  235.7 0.6 slice_reduce_fusion.1
  237.0 0.8 convert_reduce_fusion.2
  237.9 2.5 %collective-permute-start.25 = (f32[8,128]{1,0:T(8,128)S(1)}, f32[8,128]{1,0:T(8,128)S(1)}, u32[]{:S(2)}, u32[]{:S(2)}) collective-permute-start(f32[8,128]{1,0:T(8,128)S(1)} %broadcast_in_dim.20), channel_id=1, source_target_pairs={{0,4},{1,5},{2,6},{3,7},{4,0},{5,1},{6,2},{7,3},{8,12},{9,13},{10,... | collective-permute-start | bytes 12296 | tf_op jit(solution)/shard_map/ppermute | solution.py:46
  240.4 0.8 collective-permute-start.24
  241.5 0.4 collective-permute-done.25
  241.9 0.9 collective-permute-done.24
  242.8 1.1 collective-permute-start.27
  243.9 1.9 convert_reduce_fusion
  245.8 0.6 slice_reduce_fusion
  246.4 1.2 multiply_divide_fusion
  247.6 0.9 fusion.9
  (102 shorter events, 3.9 us)
Async XLA Ops:
  0.6 8.8 %collective-permute-start = (bf16[1024,128]{1,0:T(8,128)(2,1)}, bf16[1024,128]{1,0:T(8,128)(2,1)S(1)}, u32[]{:S(2)}, u32[]{:S(2)}) collective-permute-start(bf16[1024,128]{1,0:T(8,128)(2,1)} %param.7), channel_id=1, source_target_pairs={{0,1},{1,0},{2,3},{3,2},{4,5},{5,4},{6,7},{7,6},{8,9},{9,8},{10,11... | collective-permute-start | bytes 786440 | tf_op jit(solution)/shard_map/ppermute | solution.py:46
  12.0 35.6 %all-to-all-start = ((bf16[8,1024,128]{2,1,0:T(8,128)(2,1)}), bf16[8,1024,128]{2,1,0:T(8,128)(2,1)S(1)}, u32[]{:S(2)}, u32[]{:S(2)}) async-start(bf16[8,1024,128]{2,1,0:T(8,128)(2,1)} %broadcast_in_dim.15), calls=%async_computation | async-start | bytes 4194304 | tf_op jit(solution)/shard_map/all_to_all | solution.py:234
  19.0 28.5 %collective-permute-start.3 = (bf16[2048,128]{1,0:T(8,128)(2,1)S(1)}, bf16[2048,128]{1,0:T(8,128)(2,1)S(1)}, u32[]{:S(2)}, u32[]{:S(2)}) collective-permute-start(bf16[2048,128]{1,0:T(8,128)(2,1)S(1)} %constant_dynamic-update-slice_fusion.row_0), channel_id=1, source_target_pairs={{0,6},{1,7},{2,0},{3,1},{4,2},{5,3},{6,4},{7,5},{8,14},{9,15},{10,... | collective-permute-start | bytes 1572872 | tf_op jit(solution)/shard_map/ppermute | solution.py:46
  21.5 26.1 %collective-permute-start.2 = (bf16[2048,128]{1,0:T(8,128)(2,1)S(1)}, bf16[2048,128]{1,0:T(8,128)(2,1)}, u32[]{:S(2)}, u32[]{:S(2)}) collective-permute-start(bf16[2048,128]{1,0:T(8,128)(2,1)S(1)} %constant_dynamic-update-slice_fusion.row_0), channel_id=1, source_target_pairs={{0,4},{1,5},{2,6},{3,7},{4,0},{5,1},{6,2},{7,3},{8,12},{9,13},{10,... | collective-permute-start | bytes 1572872 | tf_op jit(solution)/shard_map/ppermute | solution.py:46
  22.0 26.2 %collective-permute-start.1 = (bf16[2048,128]{1,0:T(8,128)(2,1)S(1)}, bf16[2048,128]{1,0:T(8,128)(2,1)}, u32[]{:S(2)}, u32[]{:S(2)}) collective-permute-start(bf16[2048,128]{1,0:T(8,128)(2,1)S(1)} %constant_dynamic-update-slice_fusion.row_0), channel_id=1, source_target_pairs={{0,2},{1,3},{2,4},{3,5},{4,6},{5,7},{6,0},{7,1},{8,10},{9,11},{10,... | collective-permute-start | bytes 1572872 | tf_op jit(solution)/shard_map/ppermute | solution.py:46
  22.6 26.7 %copy-start.22 = (s32[1,1,64,2]{2,3,1,0:T(2,128)S(1)}, s32[1,1,64,2]{2,3,1,0:T(2,128)}, u32[]{:S(2)}) copy-start(s32[1,1,64,2]{2,3,1,0:T(2,128)} %param.9) | copy-start | bytes 1540
  22.6 30.0 %copy-start.8 = (f32[128]{0:T(128)S(1)}, f32[128]{0:T(128)}, u32[]{:S(2)}) copy-start(f32[128]{0:T(128)} %param.8) | copy-start | bytes 1540
  48.2 4.4 %collective-permute-start.4 = (bf16[8192,128]{1,0:T(8,128)(2,1)S(1)}, bf16[8192,128]{1,0:T(8,128)(2,1)}, u32[]{:S(2)}, u32[]{:S(2)}) collective-permute-start(bf16[8192,128]{1,0:T(8,128)(2,1)S(1)} %bitcast.57), channel_id=1, source_target_pairs={{0,8},{1,9},{2,10},{3,11},{4,12},{5,13},{6,14},{7,15},{8,0},{9,1},... | collective-permute-start | bytes 6291464 | tf_op jit(solution)/shard_map/ppermute | solution.py:46
  60.9 12.9 %copy-start.6 = (bf16[2048,128]{1,0:T(8,128)(2,1)}, bf16[2048,128]{1,0:T(8,128)(2,1)S(1)}, u32[]{:S(2)}) copy-start(bf16[2048,128]{1,0:T(8,128)(2,1)S(1)} %get-tuple-element.27) | copy-start | bytes 1572868
  60.9 12.9 %copy-start.11 = (bf16[2048,128]{1,0:T(8,128)(2,1)}, bf16[2048,128]{1,0:T(8,128)(2,1)S(1)}, u32[]{:S(2)}) copy-start(bf16[2048,128]{1,0:T(8,128)(2,1)S(1)} %get-tuple-element.30) | copy-start | bytes 1572868
  61.0 12.9 %copy-start.15 = (bf16[2048,128]{1,0:T(8,128)(2,1)}, bf16[2048,128]{1,0:T(8,128)(2,1)S(1)}, u32[]{:S(2)}) copy-start(bf16[2048,128]{1,0:T(8,128)(2,1)S(1)} %get-tuple-element.29) | copy-start | bytes 1572868
  61.0 12.9 %copy-start.19 = (bf16[2048,128]{1,0:T(8,128)(2,1)}, bf16[2048,128]{1,0:T(8,128)(2,1)S(1)}, u32[]{:S(2)}) copy-start(bf16[2048,128]{1,0:T(8,128)(2,1)S(1)} %get-tuple-element.28) | copy-start | bytes 1572868
  61.0 10.7 %collective-permute-start.9 = (bf16[8208,128]{1,0:T(8,128)(2,1)}, bf16[8208,128]{1,0:T(8,128)(2,1)S(1)}, u32[]{:S(2)}, u32[]{:S(2)}) collective-permute-start(bf16[8208,128]{1,0:T(8,128)(2,1)} %get-tuple-element.32), channel_id=1, source_target_pairs={{0,8},{1,9},{2,10},{3,11},{4,12},{5,13},{6,14},{7,15},{8,0},{9,1},... | collective-permute-start | bytes 6303752 | tf_op jit(solution)/shard_map/ppermute | solution.py:46
  75.5 6.8 %copy-start.20 = (bf16[2048,128]{1,0:T(8,128)(2,1)S(1)}, bf16[2048,128]{1,0:T(8,128)(2,1)}, u32[]{:S(2)}) copy-start(bf16[2048,128]{1,0:T(8,128)(2,1)} %copy-done.19) | copy-start | bytes 1572868
  75.5 6.9 %copy-start.16 = (bf16[2048,128]{1,0:T(8,128)(2,1)S(1)}, bf16[2048,128]{1,0:T(8,128)(2,1)}, u32[]{:S(2)}) copy-start(bf16[2048,128]{1,0:T(8,128)(2,1)} %copy-done.15) | copy-start | bytes 1572868
  75.5 7.0 %copy-start.12 = (bf16[2048,128]{1,0:T(8,128)(2,1)S(1)}, bf16[2048,128]{1,0:T(8,128)(2,1)}, u32[]{:S(2)}) copy-start(bf16[2048,128]{1,0:T(8,128)(2,1)} %copy-done.11) | copy-start | bytes 1572868
  75.5 32.6 %copy-start.7 = (bf16[2048,128]{1,0:T(8,128)(2,1)S(1)}, bf16[2048,128]{1,0:T(8,128)(2,1)}, u32[]{:S(2)}) copy-start(bf16[2048,128]{1,0:T(8,128)(2,1)} %copy-done.6) | copy-start | bytes 1572868
  75.5 39.1 %all-to-all-start.1 = ((bf16[8,1040,128]{2,1,0:T(8,128)(2,1)}), bf16[8,1040,128]{2,1,0:T(8,128)(2,1)}, u32[]{:S(2)}, u32[]{:S(2)}) async-start(bf16[8,1040,128]{2,1,0:T(8,128)(2,1)} %pad_maximum_fusion), calls=%async_computation.1 | async-start | bytes 4259840 | tf_op jit(solution)/shard_map/all_to_all | solution.py:253
  82.3 25.4 %collective-permute-start.5 = (bf16[2048,128]{1,0:T(8,128)(2,1)S(1)}, bf16[2048,128]{1,0:T(8,128)(2,1)S(1)}, u32[]{:S(2)}, u32[]{:S(2)}) collective-permute-start(bf16[2048,128]{1,0:T(8,128)(2,1)S(1)} %copy-done.20), channel_id=1, source_target_pairs={{0,2},{1,3},{2,4},{3,5},{4,6},{5,7},{6,0},{7,1},{8,10},{9,11},{10,... | collective-permute-start | bytes 1572872 | tf_op jit(solution)/shard_map/ppermute | solution.py:46
  82.4 25.3 %collective-permute-start.6 = (bf16[2048,128]{1,0:T(8,128)(2,1)S(1)}, bf16[2048,128]{1,0:T(8,128)(2,1)S(1)}, u32[]{:S(2)}, u32[]{:S(2)}) collective-permute-start(bf16[2048,128]{1,0:T(8,128)(2,1)S(1)} %copy-done.16), channel_id=1, source_target_pairs={{0,4},{1,5},{2,6},{3,7},{4,0},{5,1},{6,2},{7,3},{8,12},{9,13},{10,... | collective-permute-start | bytes 1572872 | tf_op jit(solution)/shard_map/ppermute | solution.py:46
  82.5 25.6 %collective-permute-start.7 = (bf16[2048,128]{1,0:T(8,128)(2,1)S(1)}, bf16[2048,128]{1,0:T(8,128)(2,1)S(1)}, u32[]{:S(2)}, u32[]{:S(2)}) collective-permute-start(bf16[2048,128]{1,0:T(8,128)(2,1)S(1)} %copy-done.12), channel_id=1, source_target_pairs={{0,6},{1,7},{2,0},{3,1},{4,2},{5,3},{6,4},{7,5},{8,14},{9,15},{10,... | collective-permute-start | bytes 1572872 | tf_op jit(solution)/shard_map/ppermute | solution.py:46
  108.3 9.0 %copy-start.21 = (bf16[1024,128]{1,0:T(8,128)(2,1)S(1)}, bf16[1024,128]{1,0:T(8,128)(2,1)}, u32[]{:S(2)}) copy-start(bf16[1024,128]{1,0:T(8,128)(2,1)} %param.7) | copy-start | bytes 786436
  108.4 6.2 %collective-permute-start.8 = (bf16[1024,128]{1,0:T(8,128)(2,1)S(1)}, bf16[1024,128]{1,0:T(8,128)(2,1)S(1)}, u32[]{:S(2)}, u32[]{:S(2)}) collective-permute-start(bf16[1024,128]{1,0:T(8,128)(2,1)S(1)} %slice.256), channel_id=1, source_target_pairs={{0,1},{1,0},{2,3},{3,2},{4,5},{5,4},{6,7},{7,6},{8,9},{9,8},{10,11... | collective-permute-start | bytes 786440 | tf_op jit(solution)/shard_map/ppermute | solution.py:46
  117.5 5.3 %collective-permute-start.14 = (bf16[1040,128]{1,0:T(8,128)(2,1)S(1)}, bf16[1040,128]{1,0:T(8,128)(2,1)S(1)}, u32[]{:S(2)}, u32[]{:S(2)}) collective-permute-start(bf16[1040,128]{1,0:T(8,128)(2,1)S(1)} %pad_maximum_fusion.3), channel_id=1, source_target_pairs={{0,1},{1,0},{2,3},{3,2},{4,5},{5,4},{6,7},{7,6},{8,9},{9,8},{10,11... | collective-permute-start | bytes 798728 | tf_op jit(solution)/shard_map/ppermute | solution.py:46
  124.6 39.4 %all-to-all-start.2 = ((bf16[8,1024,128]{2,1,0:T(8,128)(2,1)}), bf16[8,1024,128]{2,1,0:T(8,128)(2,1)S(1)}, u32[]{:S(2)}, u32[]{:S(2)}) async-start(bf16[8,1024,128]{2,1,0:T(8,128)(2,1)} %broadcast_in_dim.18), calls=%async_computation.2 | async-start | bytes 4194304 | tf_op jit(solution)/shard_map/all_to_all | solution.py:234
  130.5 15.1 %collective-permute-start.17 = (bf16[2064,128]{1,0:T(8,128)(2,1)S(1)}, bf16[2064,128]{1,0:T(8,128)(2,1)S(1)}, u32[]{:S(2)}, u32[]{:S(2)}) collective-permute-start(bf16[2064,128]{1,0:T(8,128)(2,1)S(1)} %pad_maximum_fusion.2.row_0), channel_id=1, source_target_pairs={{0,6},{1,7},{2,0},{3,1},{4,2},{5,3},{6,4},{7,5},{8,14},{9,15},{10,... | collective-permute-start | bytes 1585160 | tf_op jit(solution)/shard_map/ppermute | solution.py:46
  136.3 12.1 %collective-permute-start.16 = (bf16[2064,128]{1,0:T(8,128)(2,1)S(1)}, bf16[2064,128]{1,0:T(8,128)(2,1)S(1)}, u32[]{:S(2)}, u32[]{:S(2)}) collective-permute-start(bf16[2064,128]{1,0:T(8,128)(2,1)S(1)} %pad_maximum_fusion.2.row_0), channel_id=1, source_target_pairs={{0,4},{1,5},{2,6},{3,7},{4,0},{5,1},{6,2},{7,3},{8,12},{9,13},{10,... | collective-permute-start | bytes 1585160 | tf_op jit(solution)/shard_map/ppermute | solution.py:46
  136.7 26.4 %collective-permute-start.15 = (bf16[2064,128]{1,0:T(8,128)(2,1)S(1)}, bf16[2064,128]{1,0:T(8,128)(2,1)S(1)}, u32[]{:S(2)}, u32[]{:S(2)}) collective-permute-start(bf16[2064,128]{1,0:T(8,128)(2,1)S(1)} %pad_maximum_fusion.2.row_0), channel_id=1, source_target_pairs={{0,2},{1,3},{2,4},{3,5},{4,6},{5,7},{6,0},{7,1},{8,10},{9,11},{10,... | collective-permute-start | bytes 1585160 | tf_op jit(solution)/shard_map/ppermute | solution.py:46
  148.4 0.8 copy-start
  163.1 0.8 copy-start.2
  163.9 4.3 %collective-permute-start.18 = (bf16[8192,128]{1,0:T(8,128)(2,1)S(1)}, bf16[8192,128]{1,0:T(8,128)(2,1)S(1)}, u32[]{:S(2)}, u32[]{:S(2)}) collective-permute-start(bf16[8192,128]{1,0:T(8,128)(2,1)S(1)} %bitcast.59), channel_id=1, source_target_pairs={{0,8},{1,9},{2,10},{3,11},{4,12},{5,13},{6,14},{7,15},{8,0},{9,1},... | collective-permute-start | bytes 6291464 | tf_op jit(solution)/shard_map/ppermute | solution.py:46
  168.2 1.0 copy-start.1
  169.2 1.0 copy-start.3
  178.5 13.0 %copy-start.4 = (bf16[2048,128]{1,0:T(8,128)(2,1)}, bf16[2048,128]{1,0:T(8,128)(2,1)S(1)}, u32[]{:S(2)}) copy-start(bf16[2048,128]{1,0:T(8,128)(2,1)S(1)} %get-tuple-element.36) | copy-start | bytes 1572868
  178.5 13.0 %copy-start.9 = (bf16[2048,128]{1,0:T(8,128)(2,1)}, bf16[2048,128]{1,0:T(8,128)(2,1)S(1)}, u32[]{:S(2)}) copy-start(bf16[2048,128]{1,0:T(8,128)(2,1)S(1)} %get-tuple-element.39) | copy-start | bytes 1572868
  178.5 13.0 %copy-start.13 = (bf16[2048,128]{1,0:T(8,128)(2,1)}, bf16[2048,128]{1,0:T(8,128)(2,1)S(1)}, u32[]{:S(2)}) copy-start(bf16[2048,128]{1,0:T(8,128)(2,1)S(1)} %get-tuple-element.38) | copy-start | bytes 1572868
  178.5 13.0 %copy-start.17 = (bf16[2048,128]{1,0:T(8,128)(2,1)}, bf16[2048,128]{1,0:T(8,128)(2,1)S(1)}, u32[]{:S(2)}) copy-start(bf16[2048,128]{1,0:T(8,128)(2,1)S(1)} %get-tuple-element.37) | copy-start | bytes 1572868
  178.5 10.7 %collective-permute-start.23 = (bf16[8208,128]{1,0:T(8,128)(2,1)}, bf16[8208,128]{1,0:T(8,128)(2,1)S(1)}, u32[]{:S(2)}, u32[]{:S(2)}) collective-permute-start(bf16[8208,128]{1,0:T(8,128)(2,1)} %get-tuple-element.41), channel_id=1, source_target_pairs={{0,8},{1,9},{2,10},{3,11},{4,12},{5,13},{6,14},{7,15},{8,0},{9,1},... | collective-permute-start | bytes 6303752 | tf_op jit(solution)/shard_map/ppermute | solution.py:46
  193.0 6.8 %copy-start.18 = (bf16[2048,128]{1,0:T(8,128)(2,1)S(1)}, bf16[2048,128]{1,0:T(8,128)(2,1)}, u32[]{:S(2)}) copy-start(bf16[2048,128]{1,0:T(8,128)(2,1)} %copy-done.17) | copy-start | bytes 1572868
  193.0 6.9 %copy-start.14 = (bf16[2048,128]{1,0:T(8,128)(2,1)S(1)}, bf16[2048,128]{1,0:T(8,128)(2,1)}, u32[]{:S(2)}) copy-start(bf16[2048,128]{1,0:T(8,128)(2,1)} %copy-done.13) | copy-start | bytes 1572868
  193.0 7.0 %copy-start.10 = (bf16[2048,128]{1,0:T(8,128)(2,1)S(1)}, bf16[2048,128]{1,0:T(8,128)(2,1)}, u32[]{:S(2)}) copy-start(bf16[2048,128]{1,0:T(8,128)(2,1)} %copy-done.9) | copy-start | bytes 1572868
  193.0 32.6 %copy-start.5 = (bf16[2048,128]{1,0:T(8,128)(2,1)S(1)}, bf16[2048,128]{1,0:T(8,128)(2,1)}, u32[]{:S(2)}) copy-start(bf16[2048,128]{1,0:T(8,128)(2,1)} %copy-done.4) | copy-start | bytes 1572868
  193.0 44.0 %all-to-all-start.3 = ((bf16[8,1040,128]{2,1,0:T(8,128)(2,1)}), bf16[8,1040,128]{2,1,0:T(8,128)(2,1)}, u32[]{:S(2)}, u32[]{:S(2)}) async-start(bf16[8,1040,128]{2,1,0:T(8,128)(2,1)} %pad_maximum_fusion.1), calls=%async_computation.3 | async-start | bytes 4259840 | tf_op jit(solution)/shard_map/all_to_all | solution.py:253
  199.8 25.4 %collective-permute-start.19 = (bf16[2048,128]{1,0:T(8,128)(2,1)S(1)}, bf16[2048,128]{1,0:T(8,128)(2,1)S(1)}, u32[]{:S(2)}, u32[]{:S(2)}) collective-permute-start(bf16[2048,128]{1,0:T(8,128)(2,1)S(1)} %copy-done.18), channel_id=1, source_target_pairs={{0,2},{1,3},{2,4},{3,5},{4,6},{5,7},{6,0},{7,1},{8,10},{9,11},{10,... | collective-permute-start | bytes 1572872 | tf_op jit(solution)/shard_map/ppermute | solution.py:46
  199.9 25.3 %collective-permute-start.20 = (bf16[2048,128]{1,0:T(8,128)(2,1)S(1)}, bf16[2048,128]{1,0:T(8,128)(2,1)S(1)}, u32[]{:S(2)}, u32[]{:S(2)}) collective-permute-start(bf16[2048,128]{1,0:T(8,128)(2,1)S(1)} %copy-done.14), channel_id=1, source_target_pairs={{0,4},{1,5},{2,6},{3,7},{4,0},{5,1},{6,2},{7,3},{8,12},{9,13},{10,... | collective-permute-start | bytes 1572872 | tf_op jit(solution)/shard_map/ppermute | solution.py:46
  200.0 25.6 %collective-permute-start.21 = (bf16[2048,128]{1,0:T(8,128)(2,1)S(1)}, bf16[2048,128]{1,0:T(8,128)(2,1)S(1)}, u32[]{:S(2)}, u32[]{:S(2)}) collective-permute-start(bf16[2048,128]{1,0:T(8,128)(2,1)S(1)} %copy-done.10), channel_id=1, source_target_pairs={{0,6},{1,7},{2,0},{3,1},{4,2},{5,3},{6,4},{7,5},{8,14},{9,15},{10,... | collective-permute-start | bytes 1572872 | tf_op jit(solution)/shard_map/ppermute | solution.py:46
  225.9 11.1 %collective-permute-start.22 = (bf16[1024,128]{1,0:T(8,128)(2,1)S(1)}, bf16[1024,128]{1,0:T(8,128)(2,1)S(1)}, u32[]{:S(2)}, u32[]{:S(2)}) collective-permute-start(bf16[1024,128]{1,0:T(8,128)(2,1)S(1)} %slice.255), channel_id=1, source_target_pairs={{0,1},{1,0},{2,3},{3,2},{4,5},{5,4},{6,7},{7,6},{8,9},{9,8},{10,11... | collective-permute-start | bytes 786440 | tf_op jit(solution)/shard_map/ppermute | solution.py:46
  226.0 4.4 %collective-permute-start.12 = (f32[8,128]{1,0:T(8,128)S(1)}, f32[8,128]{1,0:T(8,128)S(1)}, u32[]{:S(2)}, u32[]{:S(2)}) collective-permute-start(f32[8,128]{1,0:T(8,128)S(1)} %broadcast_in_dim.17), channel_id=1, source_target_pairs={{0,2},{1,3},{2,4},{3,5},{4,6},{5,7},{6,0},{7,1},{8,10},{9,11},{10,... | collective-permute-start | bytes 12296 | tf_op jit(solution)/shard_map/ppermute | solution.py:46
  227.2 4.2 %collective-permute-start.11 = (f32[8,128]{1,0:T(8,128)S(1)}, f32[8,128]{1,0:T(8,128)S(1)}, u32[]{:S(2)}, u32[]{:S(2)}) collective-permute-start(f32[8,128]{1,0:T(8,128)S(1)} %broadcast_in_dim.17), channel_id=1, source_target_pairs={{0,4},{1,5},{2,6},{3,7},{4,0},{5,1},{6,2},{7,3},{8,12},{9,13},{10,... | collective-permute-start | bytes 12296 | tf_op jit(solution)/shard_map/ppermute | solution.py:46
  230.3 2.8 %collective-permute-start.10 = (f32[8,128]{1,0:T(8,128)S(1)}, f32[8,128]{1,0:T(8,128)S(1)}, u32[]{:S(2)}, u32[]{:S(2)}) collective-permute-start(f32[8,128]{1,0:T(8,128)S(1)} %broadcast_in_dim.17), channel_id=1, source_target_pairs={{0,6},{1,7},{2,0},{3,1},{4,2},{5,3},{6,4},{7,5},{8,14},{9,15},{10,... | collective-permute-start | bytes 12296 | tf_op jit(solution)/shard_map/ppermute | solution.py:46
  233.1 2.5 %collective-permute-start.13 = (f32[8,128]{1,0:T(8,128)S(1)}, f32[8,128]{1,0:T(8,128)S(1)}, u32[]{:S(2)}, u32[]{:S(2)}) collective-permute-start(f32[8,128]{1,0:T(8,128)S(1)} %fusion.22), channel_id=1, source_target_pairs={{0,1},{1,0},{2,3},{3,2},{4,5},{5,4},{6,7},{7,6},{8,9},{9,8},{10,11... | collective-permute-start | bytes 12296 | tf_op jit(solution)/shard_map/ppermute | solution.py:46
  237.8 3.7 %collective-permute-start.26 = (f32[8,128]{1,0:T(8,128)S(1)}, f32[8,128]{1,0:T(8,128)S(1)}, u32[]{:S(2)}, u32[]{:S(2)}) collective-permute-start(f32[8,128]{1,0:T(8,128)S(1)} %broadcast_in_dim.20), channel_id=1, source_target_pairs={{0,2},{1,3},{2,4},{3,5},{4,6},{5,7},{6,0},{7,1},{8,10},{9,11},{10,... | collective-permute-start | bytes 12296 | tf_op jit(solution)/shard_map/ppermute | solution.py:46
  237.9 4.0 %collective-permute-start.25 = (f32[8,128]{1,0:T(8,128)S(1)}, f32[8,128]{1,0:T(8,128)S(1)}, u32[]{:S(2)}, u32[]{:S(2)}) collective-permute-start(f32[8,128]{1,0:T(8,128)S(1)} %broadcast_in_dim.20), channel_id=1, source_target_pairs={{0,4},{1,5},{2,6},{3,7},{4,0},{5,1},{6,2},{7,3},{8,12},{9,13},{10,... | collective-permute-start | bytes 12296 | tf_op jit(solution)/shard_map/ppermute | solution.py:46
  240.4 2.5 collective-permute-start.24
  242.8 3.0 %collective-permute-start.27 = (f32[8,128]{1,0:T(8,128)S(1)}, f32[8,128]{1,0:T(8,128)S(1)}, u32[]{:S(2)}, u32[]{:S(2)}) collective-permute-start(f32[8,128]{1,0:T(8,128)S(1)} %fusion.14), channel_id=1, source_target_pairs={{0,1},{1,0},{2,3},{3,2},{4,5},{5,4},{6,7},{7,6},{8,9},{9,8},{10,11... | collective-permute-start | bytes 12296 | tf_op jit(solution)/shard_map/ppermute | solution.py:46

commit v3 on v2

--- a/solution.py
+++ b/solution.py
@@ -85,7 +85,8 @@
 
 def tiles_kernel(
     first, places, live, shares_in, row_0, row_1, row_2, row_3, own_in, other_in, tiles_in,
-    x_0, x_1, x_2, x_3, k_hbm, s_hbm, rows, scaled, cols, shared, tiles, ratios, row_acc, col_acc,
+    x_00, x_01, x_10, x_11, x_20, x_21, x_30, x_31, k_hbm, s_hbm, shares_out,
+    rows, scaled, cols, shared, tiles, ratios, row_acc, col_acc,
     x_out, k_out, s_out, sem, tile_sem, out_sem,
 ):
     f32, b16 = jnp.float32, jnp.bfloat16
@@ -128,6 +129,7 @@
     else:
         totals = jnp.sum(shared[...].astype(f32), axis=0, keepdims=True)
         shares = (K * V / jnp.sum(totals)) * (V / totals)
+    shares_out[...] = jnp.broadcast_to(shares, (8, K))
     scaled[...] = (rows[...].astype(f32) * shares).astype(b16)
     for copy in started[row_copies:]:
         copy.wait()
@@ -162,20 +164,23 @@
         total += jnp.sum(both.reshape(SPAN // 8, 8, K), axis=0)
         x_out[span, :] = terms.astype(b16)
     written = []
-    for step, ref in enumerate((x_0, x_1, x_2, x_3)):
-        source = x_out.at[pl.ds((4 - step) % 4 * 2 * SPAN, 2 * SPAN), :]
-        written.append(pltpu.make_async_copy(source, ref, out_sem.at[2 + step]))
+    for i, ref in enumerate((x_00, x_01, x_10, x_11, x_20, x_21, x_30, x_31)):
+        source = x_out.at[pl.ds(((4 - i // 2) % 4 * 2 + i % 2) * SPAN, SPAN), :]
+        written.append(pltpu.make_async_copy(source, ref, out_sem.at[2 + i]))
         written[-1].start()
     total = jnp.sum(total, axis=0, keepdims=True)
     high = total.astype(b16).astype(f32)
     middle = (total - high).astype(b16).astype(f32)
     low = total - high - middle
-    at = lax.broadcasted_iota(jnp.int32, (EXTRA, K), 0)
+    at = lax.broadcasted_iota(jnp.int32, (EXTRA, K), 0) - 3
     zero = jnp.zeros((EXTRA, K), f32)
-    out = jnp.where(at == 0, high, jnp.where(at == 1, middle, jnp.where(at == 2, low, zero)))
     for i, (ref, hbm) in enumerate(((s_out, s_hbm), (k_out, k_hbm))):
-        ref[pl.ds(8 * SPAN, EXTRA), :] = out.astype(b16)
-        ref[pl.ds(0, 8 * SPAN), :] = col_acc[pl.ds((1 - i) * 8 * SPAN, 8 * SPAN), :].astype(b16)
+        at = at + 3 * i
+        out = jnp.where(at == 0, high, jnp.where(at == 1, middle, jnp.where(at == 2, low, zero)))
+        for j in range(8):
+            source = pl.ds(((1 - i) * 8 + j) * SPAN, SPAN)
+            ref[pl.ds(j * (SPAN + EXTRA), SPAN), :] = col_acc[source, :].astype(b16)
+            ref[pl.ds(j * (SPAN + EXTRA) + SPAN, EXTRA), :] = out.astype(b16)
         written.append(pltpu.make_async_copy(ref, hbm, out_sem.at[i]))
         written[-1].start()
     for copy in written:
@@ -183,14 +188,13 @@
 
 
 def sweep(first, places, live, shares, rows, own_in, other_in, tiles):
-    whole = pl.BlockSpec(memory_space=pl.ANY)
     near = pl.BlockSpec(memory_space=pltpu.VMEM)
-    far = pl.BlockSpec(memory_space=pltpu.HBM)
+    far = pl.BlockSpec(memory_space=pl.ANY)
     scalars = pl.BlockSpec(memory_space=pltpu.SMEM)
     return pl.pallas_call(
         partial(tiles_kernel, first),
-        in_specs=[scalars, scalars, near] + [whole] * 6 + [far],
-        out_specs=[far] * 6,
+        in_specs=[scalars, scalars, near] + [far] * 7,
+        out_specs=[far] * 10 + [near],
         scratch_shapes=[
             pltpu.VMEM((8 * SPAN, K), jnp.bfloat16),
             pltpu.VMEM((8 * SPAN, K), jnp.bfloat16),
@@ -201,16 +205,17 @@
             pltpu.VMEM((8 * SPAN, K), jnp.float32),
             pltpu.VMEM((16 * SPAN, K), jnp.float32),
             pltpu.VMEM((8 * SPAN, K), jnp.bfloat16),
-            pltpu.VMEM((8 * SPAN + EXTRA, K), jnp.bfloat16),
-            pltpu.VMEM((8 * SPAN + EXTRA, K), jnp.bfloat16),
+            pltpu.VMEM((8 * (SPAN + EXTRA), K), jnp.bfloat16),
+            pltpu.VMEM((8 * (SPAN + EXTRA), K), jnp.bfloat16),
             pltpu.SemaphoreType.DMA((10,)),
             pltpu.SemaphoreType.DMA((SLOTS // GROUP,)),
-            pltpu.SemaphoreType.DMA((6,)),
+            pltpu.SemaphoreType.DMA((10,)),
         ],
-        out_shape=[jax.ShapeDtypeStruct((2 * SPAN, K), jnp.bfloat16)] * 4
+        out_shape=[jax.ShapeDtypeStruct((SPAN, K), jnp.bfloat16)] * 8
         + [
-            jax.ShapeDtypeStruct((8 * SPAN + EXTRA, K), jnp.bfloat16),
-            jax.ShapeDtypeStruct((8 * SPAN + EXTRA, K), jnp.bfloat16),
+            jax.ShapeDtypeStruct((8 * (SPAN + EXTRA), K), jnp.bfloat16),
+            jax.ShapeDtypeStruct((8 * (SPAN + EXTRA), K), jnp.bfloat16),
+            jax.ShapeDtypeStruct((8, K), jnp.float32),
         ],
         compiler_params=pltpu.CompilerParams(vmem_limit_bytes=VMEM_MIB << 20),
         name="tiles",
@@ -222,15 +227,16 @@
 
 
 def gather_words(weights, totals, tiles):
+    copies = jnp.broadcast_to(weights[None], (8, SPAN, K))
     if totals is None:
-        low = send(weights, "zl", 1)
+        low = after(send(weights, "zl", 1), copies)
         row_sent = jnp.concatenate([weights, low])
     else:
-        low = send(jnp.concatenate([weights, in_parts(totals)]), "zl", 1)
+        low = after(send(jnp.concatenate([weights, in_parts(totals)]), "zl", 1), copies)
         both = in_parts(totals + joined(low[SPAN:]))
         row_sent = jnp.concatenate([weights, low[:SPAN], both])
     rows = [row_sent] + [send(row_sent, "x", s) for s in (1, 2, 3)]
-    copies = after(jnp.broadcast_to(weights[None], (8, SPAN, K)), row_sent)
+    copies = after(copies, row_sent)
     own = lax.all_to_all(copies, AXES, 0, 0, axis_index_groups=together("zh", "y"))
     if totals is None:
         tiles = after(tiles, row_sent).astype(jnp.bfloat16)
@@ -240,22 +246,21 @@
     return (rows, own, send(own, "k", 1)), tiles
 
 
-def scatter_terms(x_0, x_1, x_2, x_3, k_out, s_out):
+def scatter_terms(*outs):
     f32, b16 = jnp.float32, jnp.bfloat16
-    x_got = [send(x, "x", s + 1) for s, x in enumerate((x_1, x_2, x_3))]
-    x_sum = x_0.astype(f32) + sum(x.astype(f32) for x in x_got)
+    x_outs, k_out, s_out = outs[:8], outs[8], outs[9]
+    others = [send(x_outs[2 * s + 1], "x", s) for s in (1, 2, 3)]
+    owns = [send(after(x_outs[2 * s], others[s - 1]), "x", s) for s in (1, 2, 3)]
+    x_other = x_outs[1].astype(f32) + sum(x.astype(f32) for x in others)
+    x_own = x_outs[0].astype(f32) + sum(x.astype(f32) for x in owns)
     s_got = send(s_out, "k", 1)
-    both = k_out[: 8 * SPAN].astype(f32) + s_got[: 8 * SPAN].astype(f32)
-    pair = in_parts(joined(k_out[8 * SPAN :]) + joined(s_got[8 * SPAN :]))
-    sent = jnp.concatenate(
-        [both.astype(b16).reshape(8, SPAN, K), jnp.broadcast_to(pair[None], (8, EXTRA, K))], axis=1
-    )
+    sent = (k_out.astype(f32) + s_got.astype(f32)).astype(b16).reshape(8, SPAN + EXTRA, K)
     got = lax.all_to_all(sent, AXES, 0, 0, axis_index_groups=together("zh", "y"))
-    low = send(x_sum[SPAN:].astype(b16), "zl", 1)
-    got = after(got, low)
+    low = send(x_other.astype(b16), "zl", 1)
+    got = after(got, low, *owns)
     col_sum = jnp.sum(got[:, :SPAN].astype(f32), axis=0)
     totals = jnp.sum(got[:, SPAN:].astype(f32), axis=(0, 1))
-    row_sum = x_sum[:SPAN] + low.astype(f32)
+    row_sum = x_own + low.astype(f32)
     return row_sum, col_sum, totals
 
 
@@ -275,13 +280,12 @@
     for step in range(ITERS):
         gathered, tiles = gather_words(weights, totals, tiles)
         outs = sweep(step == 0, places, live, shares, *gathered, tiles)
-        row_sum, col_sum, totals = scatter_terms(*outs)
+        row_sum, col_sum, totals = scatter_terms(*outs[:-1])
         if step > 0:
-            shares = (K * V / jnp.sum(before)) * (V / before)
+            shares = outs[-1][0]
         expected = weights.astype(jnp.float32) * (shares * row_sum + col_sum)
         if step < ITERS - 1:
             weights = expected.astype(jnp.bfloat16)
-            before = sum_columns(totals, at)
     totals = sum_columns(totals, at)
     return (V * expected / totals).astype(jnp.bfloat16), K * totals / jnp.sum(totals)
 

time: 253 us -> 243 us (0.960)
  Pallas kernels: 16.5 us -> 28.9 us
  starting transfers between devices: 70 us -> 59.4 us
  waiting for transfers between devices: 123 us -> 116 us
  other arithmetic: 27.7 us -> 24.1 us
    ppermute x28 -> x30, starting transfers between devices: 43.4 us -> 30.2 us  [send(): return lax.ppermute(value, AXES, pairs)]
    pallas_call x2, Pallas kernels: 16.5 us -> 28.9 us  [sweep(): pl.pallas_call(partial(tiles_kernel, first), in_specs=[scalars, scalars,...]
    ppermute x28 -> x30, waiting for transfers between devices: 107 us -> 99.9 us  [send(): return lax.ppermute(value, AXES, pairs)]
    concatenate x3 -> x1, other arithmetic: 3.07 us -> 0.02 us  [gather_words(): jnp.concatenate([weights, in_parts(totals)])]
    convert_element_type x2 -> x4, other arithmetic: 4.27 us -> 6.07 us  [the longest x2 5.79 us: scatter_terms(): (k_out.astype(f32) + s_got.astype(f32)).astype(b16)]
  transfers between devices with their start and end apart: 32 -> 34, of which waited for: 22 -> 23; matrix products, arithmetic and copies ran while one was open for 6% -> 5% of each run, Pallas kernels for 0% -> 0%
where the time goes in v3:
time: 243 us; the launch traced here: 239 us
  waiting for transfers between devices  116 us (48%)
  starting transfers between devices  59.4 us (24%)
  Pallas kernels  28.9 us (12%)
  other arithmetic  24.1 us (10%)
  local copies, waits for them, and re-layouts  9.05 us (4%)
    ppermute x30, waiting for transfers between devices, send(): return lax.ppermute(value, AXES, pairs)  99.9 us
    ppermute x30, starting transfers between devices, send(): return lax.ppermute(value, AXES, pairs)  30.2 us
    pallas_call x2, Pallas kernels, sweep(): pl.pallas_call(partial(tiles_kernel, first), in_specs=[scalars, scalars,...  28.9 us
    all_to_all x2, waiting for transfers between devices, gather_words(): lax.all_to_all(copies, AXES, 0, 0, axis_index_groups=together('zh', 'y'))  15.6 us
    all_to_all x2, starting transfers between devices, scatter_terms(): lax.all_to_all(sent, AXES, 0, 0, axis_index_groups=together('zh', 'y'))  15.3 us
    all_to_all x2, starting transfers between devices, gather_words(): lax.all_to_all(copies, AXES, 0, 0, axis_index_groups=together('zh', 'y'))  14 us
    convert_element_type x1, other arithmetic, gather_words(): tiles = after(tiles, row_sent).astype(jnp.bfloat16)  9.35 us
    convert_element_type x2, other arithmetic, scatter_terms(): (k_out.astype(f32) + s_got.astype(f32)).astype(b16)  5.79 us
  transfers between devices with their start and end apart: 34, of which 23 were waited for; matrix products, arithmetic and copies ran while one was open for 5% of the time, Pallas kernels for 0%

profile of v3, /device:TPU:1, one launch (start us, length us, event | category | flops | bytes accessed | tf_op | source)
XLA Modules:
  0.0 239.0 jit_solution(14833837160750240756)
XLA Ops:
  0.6 2.5 %collective-permute-start = (bf16[1024,128]{1,0:T(8,128)(2,1)}, bf16[1024,128]{1,0:T(8,128)(2,1)S(1)}, u32[]{:S(2)}, u32[]{:S(2)}) collective-permute-start(bf16[1024,128]{1,0:T(8,128)(2,1)} %param.5), channel_id=1, source_target_pairs={{0,1},{1,0},{2,3},{3,2},{4,5},{5,4},{6,7},{7,6},{8,9},{9,8},{10,11... | collective-permute-start | bytes 786440 | tf_op jit(solution)/shard_map/ppermute | solution.py:46
  3.2 1.0 constant_dynamic-update-slice_fusion.1
  4.2 5.2 %collective-permute-done = bf16[1024,128]{1,0:T(8,128)(2,1)S(1)} collective-permute-done((bf16[1024,128]{1,0:T(8,128)(2,1)}, bf16[1024,128]{1,0:T(8,128)(2,1)S(1)}, u32[]{:S(2)}, u32[]{:S(2)}) %collective-permute-start) | collective-permute-done | bytes 262176 | tf_op jit(solution)/shard_map/ppermute | solution.py:46
  9.4 2.5 %broadcast_in_dim.9 = bf16[8,1024,128]{2,1,0:T(8,128)(2,1)} broadcast(bf16[1024,128]{1,0:T(8,128)(2,1)} %param.5), dimensions={1,2} | broadcast | bytes 2359296 | tf_op jit(solution)/shard_map/broadcast_in_dim | solution.py:230
  12.0 7.0 %all-to-all-start = ((bf16[8,1024,128]{2,1,0:T(8,128)(2,1)}), bf16[8,1024,128]{2,1,0:T(8,128)(2,1)S(1)}, u32[]{:S(2)}, u32[]{:S(2)}) async-start(bf16[8,1024,128]{2,1,0:T(8,128)(2,1)} %broadcast_in_dim.9), calls=%async_computation | async-start | bytes 4194304 | tf_op jit(solution)/shard_map/all_to_all | solution.py:240
  19.0 2.5 %collective-permute-start.3 = (bf16[2048,128]{1,0:T(8,128)(2,1)S(1)}, bf16[2048,128]{1,0:T(8,128)(2,1)S(1)}, u32[]{:S(2)}, u32[]{:S(2)}) collective-permute-start(bf16[2048,128]{1,0:T(8,128)(2,1)S(1)} %constant_dynamic-update-slice_fusion.row_0), channel_id=1, source_target_pairs={{0,6},{1,7},{2,0},{3,1},{4,2},{5,3},{6,4},{7,5},{8,14},{9,15},{10,... | collective-permute-start | bytes 1572872 | tf_op jit(solution)/shard_map/ppermute | solution.py:46
  21.5 0.5 collective-permute-start.2
  22.0 0.6 collective-permute-start.1
  22.6 9.3 %convert_element_type.114.tiles_in = bf16[64,256,256]{2,1,0:T(8,128)(2,1)} convert(s32[64,256,256]{2,1,0:T(8,128)} %bitcast.66) | non-fusion elementwise | flops 4194304 | bytes 25165824 | tf_op jit(solution)/shard_map/convert_element_type | solution.py:242
  32.0 15.6 %all-to-all-done = bf16[8,1024,128]{2,1,0:T(8,128)(2,1)S(1)} async-done(((bf16[8,1024,128]{2,1,0:T(8,128)(2,1)}), bf16[8,1024,128]{2,1,0:T(8,128)(2,1)S(1)}, u32[]{:S(2)}, u32[]{:S(2)}) %all-to-all-start) | async-done | bytes 2097184 | tf_op jit(solution)/shard_map/all_to_all | solution.py:240
  47.6 0.6 collective-permute-done.1.row_1
  48.2 0.5 collective-permute-start.4
  49.5 3.1 %collective-permute-done.4.other_in = bf16[8192,128]{1,0:T(8,128)(2,1)} collective-permute-done((bf16[8192,128]{1,0:T(8,128)(2,1)S(1)}, bf16[8192,128]{1,0:T(8,128)(2,1)}, u32[]{:S(2)}, u32[]{:S(2)}) %collective-permute-start.4) | collective-permute-done | bytes 2097184 | tf_op jit(solution)/shard_map/ppermute | solution.py:46
  52.6 14.8 %tiles.2 = (bf16[1024,128]{1,0:T(8,128)(2,1)S(1)}, bf16[1024,128]{1,0:T(8,128)(2,1)S(1)}, bf16[1024,128]{1,0:T(8,128)(2,1)S(1)}, bf16[1024,128]{1,0:T(8,128)(2,1...) custom-call(s32[128]{0:T(128)S(1)} %pad_add_fusion.places, ...), custom_call_target="tpu_custom_call" | custom-call | tf_op jit(solution)/shard_map/tiles/pallas_call | solution.py:194
  68.0 4.0 %collective-permute-done.12 = bf16[8320,128]{1,0:T(8,128)(2,1)S(1)} collective-permute-done((bf16[8320,128]{1,0:T(8,128)(2,1)}, bf16[8320,128]{1,0:T(8,128)(2,1)S(1)}, u32[]{:S(2)}, u32[]{:S(2)}) %collective-permute-start.12) | collective-permute-done | bytes 2129952 | tf_op jit(solution)/shard_map/ppermute | solution.py:46
  72.0 2.9 %add_convert_fusion.1 = bf16[8320,128]{1,0:T(8,128)(2,1)} fusion(bf16[8320,128]{1,0:T(8,128)(2,1)S(1)} %collective-permute-done.12, bf16[8320,128]{1,0:T(8,128)(2,1)} %get-tuple-element.55), kind=kLoop, calls=%fused_computation.1 | loop fusion | flops 4259840 | bytes 6389760 | tf_op jit(solution)/shard_map/convert_element_type | solution.py:257
  75.1 7.6 %all-to-all-start.1 = ((bf16[8,1040,128]{2,1,0:T(8,128)(2,1)}), bf16[8,1040,128]{2,1,0:T(8,128)(2,1)}, u32[]{:S(2)}, u32[]{:S(2)}) async-start(bf16[8,1040,128]{2,1,0:T(8,128)(2,1)} %bitcast.68), calls=%async_computation.1 | async-start | bytes 4259840 | tf_op jit(solution)/shard_map/all_to_all | solution.py:258
  82.8 1.5 collective-permute-start.7
  84.3 1.2 collective-permute-start.9
  85.5 11.0 %collective-permute-done.5 = bf16[1024,128]{1,0:T(8,128)(2,1)S(1)} collective-permute-done((bf16[1024,128]{1,0:T(8,128)(2,1)S(1)}, bf16[1024,128]{1,0:T(8,128)(2,1)S(1)}, u32[]{:S(2)}, u32[]{:S(2)}) %collective-permute-start.5) | collective-permute-done | bytes 262176 | tf_op jit(solution)/shard_map/ppermute | solution.py:46
  96.5 1.3 collective-permute-start.8
  97.8 2.6 %collective-permute-start.10 = (bf16[1024,128]{1,0:T(8,128)(2,1)S(1)}, bf16[1024,128]{1,0:T(8,128)(2,1)S(1)}, u32[]{:S(2)}, u32[]{:S(2)}) collective-permute-start(bf16[1024,128]{1,0:T(8,128)(2,1)S(1)} %copy-done.16), channel_id=1, source_target_pairs={{0,6},{1,7},{2,0},{3,1},{4,2},{5,3},{6,4},{7,5},{8,14},{9,15},{10,... | collective-permute-start | bytes 786440 | tf_op jit(solution)/shard_map/ppermute | solution.py:46
  100.9 9.5 %collective-permute-done.6 = bf16[1024,128]{1,0:T(8,128)(2,1)S(1)} collective-permute-done((bf16[1024,128]{1,0:T(8,128)(2,1)S(1)}, bf16[1024,128]{1,0:T(8,128)(2,1)S(1)}, u32[]{:S(2)}, u32[]{:S(2)}) %collective-permute-start.6) | collective-permute-done | bytes 262176 | tf_op jit(solution)/shard_map/ppermute | solution.py:46
  110.4 0.8 collective-permute-done.10
  111.1 2.4 collective-permute-done.11
  113.5 0.8 convert_reduce_fusion.3
  114.3 1.9 convert_reduce_fusion.1
  116.6 0.8 collective-permute-start.13
  117.3 6.8 %collective-permute-done.13 = bf16[1040,128]{1,0:T(8,128)(2,1)S(1)} collective-permute-done((bf16[1040,128]{1,0:T(8,128)(2,1)S(1)}, bf16[1040,128]{1,0:T(8,128)(2,1)S(1)}, u32[]{:S(2)}, u32[]{:S(2)}) %collective-permute-start.13) | collective-permute-done | bytes 266272 | tf_op jit(solution)/shard_map/ppermute | solution.py:46
  124.1 1.6 broadcast_in_dim.10
  125.8 6.9 %all-to-all-start.2 = ((bf16[8,1024,128]{2,1,0:T(8,128)(2,1)}), bf16[8,1024,128]{2,1,0:T(8,128)(2,1)S(1)}, u32[]{:S(2)}, u32[]{:S(2)}) async-start(bf16[8,1024,128]{2,1,0:T(8,128)(2,1)} %broadcast_in_dim.10), calls=%async_computation.2 | async-start | bytes 4194304 | tf_op jit(solution)/shard_map/all_to_all | solution.py:240
  132.8 1.5 collective-permute-start.16
  134.3 0.8 collective-permute-start.15
  135.3 9.4 %collective-permute-done.16.row_3 = bf16[2064,128]{1,0:T(8,128)(2,1)S(1)} collective-permute-done((bf16[2064,128]{1,0:T(8,128)(2,1)S(1)}, bf16[2064,128]{1,0:T(8,128)(2,1)S(1)}, u32[]{:S(2)}, u32[]{:S(2)}) %collective-permute-start.16) | collective-permute-done | bytes 528416 | tf_op jit(solution)/shard_map/ppermute | solution.py:46
  144.8 2.7 %collective-permute-done.15.row_2 = bf16[2064,128]{1,0:T(8,128)(2,1)S(1)} collective-permute-done((bf16[2064,128]{1,0:T(8,128)(2,1)S(1)}, bf16[2064,128]{1,0:T(8,128)(2,1)S(1)}, u32[]{:S(2)}, u32[]{:S(2)}) %collective-permute-start.15) | collective-permute-done | bytes 528416 | tf_op jit(solution)/shard_map/ppermute | solution.py:46
  147.4 0.8 copy-done
  148.2 12.8 %collective-permute-done.14.row_1 = bf16[2064,128]{1,0:T(8,128)(2,1)S(1)} collective-permute-done((bf16[2064,128]{1,0:T(8,128)(2,1)S(1)}, bf16[2064,128]{1,0:T(8,128)(2,1)S(1)}, u32[]{:S(2)}, u32[]{:S(2)}) %collective-permute-start.14) | collective-permute-done | bytes 528416 | tf_op jit(solution)/shard_map/ppermute | solution.py:46
  161.0 0.8 copy-done.2
  161.8 0.5 collective-permute-start.17
  162.3 3.8 %collective-permute-done.17.other_in = bf16[8192,128]{1,0:T(8,128)(2,1)S(1)} collective-permute-done((bf16[8192,128]{1,0:T(8,128)(2,1)S(1)}, bf16[8192,128]{1,0:T(8,128)(2,1)S(1)}, u32[]{:S(2)}, u32[]{:S(2)}) %collective-permute-start.17) | collective-permute-done | bytes 2097184 | tf_op jit(solution)/shard_map/ppermute | solution.py:46
  166.1 1.0 copy-done.1
  167.1 1.0 copy-done.3
  168.2 14.1 %tiles.3 = (bf16[1024,128]{1,0:T(8,128)(2,1)S(1)}, bf16[1024,128]{1,0:T(8,128)(2,1)S(1)}, bf16[1024,128]{1,0:T(8,128)(2,1)S(1)}, bf16[1024,128]{1,0:T(8,128)(2,1...) custom-call(s32[128]{0:T(128)S(1)} %pad_add_fusion.places, ...), custom_call_target="tpu_custom_call" | custom-call | tf_op jit(solution)/shard_map/tiles/pallas_call | solution.py:194
  182.8 4.0 %collective-permute-done.25 = bf16[8320,128]{1,0:T(8,128)(2,1)S(1)} collective-permute-done((bf16[8320,128]{1,0:T(8,128)(2,1)}, bf16[8320,128]{1,0:T(8,128)(2,1)S(1)}, u32[]{:S(2)}, u32[]{:S(2)}) %collective-permute-start.25) | collective-permute-done | bytes 2129952 | tf_op jit(solution)/shard_map/ppermute | solution.py:46
  186.9 2.9 %add_convert_fusion = bf16[8320,128]{1,0:T(8,128)(2,1)} fusion(bf16[8320,128]{1,0:T(8,128)(2,1)S(1)} %collective-permute-done.25, bf16[8320,128]{1,0:T(8,128)(2,1)} %get-tuple-element.73), kind=kLoop, calls=%fused_computation | loop fusion | flops 4259840 | bytes 6389760 | tf_op jit(solution)/shard_map/convert_element_type | solution.py:257
  189.9 7.6 %all-to-all-start.3 = ((bf16[8,1040,128]{2,1,0:T(8,128)(2,1)}), bf16[8,1040,128]{2,1,0:T(8,128)(2,1)}, u32[]{:S(2)}, u32[]{:S(2)}) async-start(bf16[8,1040,128]{2,1,0:T(8,128)(2,1)} %bitcast.67), calls=%async_computation.3 | async-start | bytes 4259840 | tf_op jit(solution)/shard_map/all_to_all | solution.py:258
  197.6 1.7 collective-permute-start.20
  199.3 1.0 collective-permute-start.22
  200.3 6.9 %collective-permute-done.18 = bf16[1024,128]{1,0:T(8,128)(2,1)S(1)} collective-permute-done((bf16[1024,128]{1,0:T(8,128)(2,1)S(1)}, bf16[1024,128]{1,0:T(8,128)(2,1)S(1)}, u32[]{:S(2)}, u32[]{:S(2)}) %collective-permute-start.18) | collective-permute-done | bytes 262176 | tf_op jit(solution)/shard_map/ppermute | solution.py:46
  207.2 3.8 %collective-permute-done.20 = bf16[1024,128]{1,0:T(8,128)(2,1)S(1)} collective-permute-done((bf16[1024,128]{1,0:T(8,128)(2,1)S(1)}, bf16[1024,128]{1,0:T(8,128)(2,1)S(1)}, u32[]{:S(2)}, u32[]{:S(2)}) %collective-permute-start.20) | collective-permute-done | bytes 262176 | tf_op jit(solution)/shard_map/ppermute | solution.py:46
  211.0 1.4 collective-permute-start.21
  212.4 3.4 %collective-permute-start.23 = (bf16[1024,128]{1,0:T(8,128)(2,1)S(1)}, bf16[1024,128]{1,0:T(8,128)(2,1)S(1)}, u32[]{:S(2)}, u32[]{:S(2)}) collective-permute-start(bf16[1024,128]{1,0:T(8,128)(2,1)S(1)} %copy-done.10), channel_id=1, source_target_pairs={{0,6},{1,7},{2,0},{3,1},{4,2},{5,3},{6,4},{7,5},{8,14},{9,15},{10,... | collective-permute-start | bytes 786440 | tf_op jit(solution)/shard_map/ppermute | solution.py:46
  216.5 3.5 %collective-permute-done.21 = bf16[1024,128]{1,0:T(8,128)(2,1)S(1)} collective-permute-done((bf16[1024,128]{1,0:T(8,128)(2,1)S(1)}, bf16[1024,128]{1,0:T(8,128)(2,1)S(1)}, u32[]{:S(2)}, u32[]{:S(2)}) %collective-permute-start.21) | collective-permute-done | bytes 262176 | tf_op jit(solution)/shard_map/ppermute | solution.py:46
  220.0 3.2 %collective-permute-done.23 = bf16[1024,128]{1,0:T(8,128)(2,1)S(1)} collective-permute-done((bf16[1024,128]{1,0:T(8,128)(2,1)S(1)}, bf16[1024,128]{1,0:T(8,128)(2,1)S(1)}, u32[]{:S(2)}, u32[]{:S(2)}) %collective-permute-start.23) | collective-permute-done | bytes 262176 | tf_op jit(solution)/shard_map/ppermute | solution.py:46
  223.1 5.0 %collective-permute-done.24 = bf16[1024,128]{1,0:T(8,128)(2,1)S(1)} collective-permute-done((bf16[1024,128]{1,0:T(8,128)(2,1)S(1)}, bf16[1024,128]{1,0:T(8,128)(2,1)S(1)}, u32[]{:S(2)}, u32[]{:S(2)}) %collective-permute-start.24) | collective-permute-done | bytes 262176 | tf_op jit(solution)/shard_map/ppermute | solution.py:46
  228.1 0.8 convert_reduce_fusion.2
  229.0 1.6 collective-permute-start.27
  230.6 2.0 collective-permute-start.26
  232.6 1.0 collective-permute-done.26
  233.7 0.5 collective-permute-start.29
  234.2 1.9 convert_reduce_fusion
  236.2 0.6 slice_reduce_fusion
  236.8 1.2 multiply_divide_fusion
  238.0 1.0 divide_convert_fusion
  (120 shorter events, 3.2 us)
Async XLA Ops:
  0.6 8.8 %collective-permute-start = (bf16[1024,128]{1,0:T(8,128)(2,1)}, bf16[1024,128]{1,0:T(8,128)(2,1)S(1)}, u32[]{:S(2)}, u32[]{:S(2)}) collective-permute-start(bf16[1024,128]{1,0:T(8,128)(2,1)} %param.5), channel_id=1, source_target_pairs={{0,1},{1,0},{2,3},{3,2},{4,5},{5,4},{6,7},{7,6},{8,9},{9,8},{10,11... | collective-permute-start | bytes 786440 | tf_op jit(solution)/shard_map/ppermute | solution.py:46
  12.0 35.6 %all-to-all-start = ((bf16[8,1024,128]{2,1,0:T(8,128)(2,1)}), bf16[8,1024,128]{2,1,0:T(8,128)(2,1)S(1)}, u32[]{:S(2)}, u32[]{:S(2)}) async-start(bf16[8,1024,128]{2,1,0:T(8,128)(2,1)} %broadcast_in_dim.9), calls=%async_computation | async-start | bytes 4194304 | tf_op jit(solution)/shard_map/all_to_all | solution.py:240
  19.0 28.5 %collective-permute-start.3 = (bf16[2048,128]{1,0:T(8,128)(2,1)S(1)}, bf16[2048,128]{1,0:T(8,128)(2,1)S(1)}, u32[]{:S(2)}, u32[]{:S(2)}) collective-permute-start(bf16[2048,128]{1,0:T(8,128)(2,1)S(1)} %constant_dynamic-update-slice_fusion.row_0), channel_id=1, source_target_pairs={{0,6},{1,7},{2,0},{3,1},{4,2},{5,3},{6,4},{7,5},{8,14},{9,15},{10,... | collective-permute-start | bytes 1572872 | tf_op jit(solution)/shard_map/ppermute | solution.py:46
  21.5 26.1 %collective-permute-start.2 = (bf16[2048,128]{1,0:T(8,128)(2,1)S(1)}, bf16[2048,128]{1,0:T(8,128)(2,1)}, u32[]{:S(2)}, u32[]{:S(2)}) collective-permute-start(bf16[2048,128]{1,0:T(8,128)(2,1)S(1)} %constant_dynamic-update-slice_fusion.row_0), channel_id=1, source_target_pairs={{0,4},{1,5},{2,6},{3,7},{4,0},{5,1},{6,2},{7,3},{8,12},{9,13},{10,... | collective-permute-start | bytes 1572872 | tf_op jit(solution)/shard_map/ppermute | solution.py:46
  22.0 26.2 %collective-permute-start.1 = (bf16[2048,128]{1,0:T(8,128)(2,1)S(1)}, bf16[2048,128]{1,0:T(8,128)(2,1)}, u32[]{:S(2)}, u32[]{:S(2)}) collective-permute-start(bf16[2048,128]{1,0:T(8,128)(2,1)S(1)} %constant_dynamic-update-slice_fusion.row_0), channel_id=1, source_target_pairs={{0,2},{1,3},{2,4},{3,5},{4,6},{5,7},{6,0},{7,1},{8,10},{9,11},{10,... | collective-permute-start | bytes 1572872 | tf_op jit(solution)/shard_map/ppermute | solution.py:46
  22.6 26.7 %copy-start.36 = (s32[1,1,64,2]{2,3,1,0:T(2,128)S(1)}, s32[1,1,64,2]{2,3,1,0:T(2,128)}, u32[]{:S(2)}) copy-start(s32[1,1,64,2]{2,3,1,0:T(2,128)} %param.7) | copy-start | bytes 1540
  22.6 30.0 %copy-start.8 = (f32[128]{0:T(128)S(1)}, f32[128]{0:T(128)}, u32[]{:S(2)}) copy-start(f32[128]{0:T(128)} %param.6) | copy-start | bytes 1540
  48.2 4.4 %collective-permute-start.4 = (bf16[8192,128]{1,0:T(8,128)(2,1)S(1)}, bf16[8192,128]{1,0:T(8,128)(2,1)}, u32[]{:S(2)}, u32[]{:S(2)}) collective-permute-start(bf16[8192,128]{1,0:T(8,128)(2,1)S(1)} %bitcast.60), channel_id=1, source_target_pairs={{0,8},{1,9},{2,10},{3,11},{4,12},{5,13},{6,14},{7,15},{8,0},{9,1},... | collective-permute-start | bytes 6291464 | tf_op jit(solution)/shard_map/ppermute | solution.py:46
  67.4 7.5 %copy-start.6 = (bf16[1024,128]{1,0:T(8,128)(2,1)}, bf16[1024,128]{1,0:T(8,128)(2,1)S(1)}, u32[]{:S(2)}) copy-start(bf16[1024,128]{1,0:T(8,128)(2,1)S(1)} %get-tuple-element.54) | copy-start | bytes 786436
  67.4 7.5 %copy-start.15 = (bf16[1024,128]{1,0:T(8,128)(2,1)}, bf16[1024,128]{1,0:T(8,128)(2,1)S(1)}, u32[]{:S(2)}) copy-start(bf16[1024,128]{1,0:T(8,128)(2,1)S(1)} %get-tuple-element.53) | copy-start | bytes 786436
  67.4 7.5 %copy-start.17 = (bf16[1024,128]{1,0:T(8,128)(2,1)}, bf16[1024,128]{1,0:T(8,128)(2,1)S(1)}, u32[]{:S(2)}) copy-start(bf16[1024,128]{1,0:T(8,128)(2,1)S(1)} %get-tuple-element.50) | copy-start | bytes 786436
  67.5 7.5 %copy-start.19 = (bf16[1024,128]{1,0:T(8,128)(2,1)}, bf16[1024,128]{1,0:T(8,128)(2,1)S(1)}, u32[]{:S(2)}) copy-start(bf16[1024,128]{1,0:T(8,128)(2,1)S(1)} %get-tuple-element.47) | copy-start | bytes 786436
  67.5 7.5 %copy-start.23 = (bf16[1024,128]{1,0:T(8,128)(2,1)}, bf16[1024,128]{1,0:T(8,128)(2,1)S(1)}, u32[]{:S(2)}) copy-start(bf16[1024,128]{1,0:T(8,128)(2,1)S(1)} %get-tuple-element.52) | copy-start | bytes 786436
  67.5 7.5 %copy-start.27 = (bf16[1024,128]{1,0:T(8,128)(2,1)}, bf16[1024,128]{1,0:T(8,128)(2,1)S(1)}, u32[]{:S(2)}) copy-start(bf16[1024,128]{1,0:T(8,128)(2,1)S(1)} %get-tuple-element.49) | copy-start | bytes 786436
  67.5 7.5 %copy-start.31 = (bf16[1024,128]{1,0:T(8,128)(2,1)}, bf16[1024,128]{1,0:T(8,128)(2,1)S(1)}, u32[]{:S(2)}) copy-start(bf16[1024,128]{1,0:T(8,128)(2,1)S(1)} %get-tuple-element.46) | copy-start | bytes 786436
  67.5 4.5 %collective-permute-start.12 = (bf16[8320,128]{1,0:T(8,128)(2,1)}, bf16[8320,128]{1,0:T(8,128)(2,1)S(1)}, u32[]{:S(2)}, u32[]{:S(2)}) collective-permute-start(bf16[8320,128]{1,0:T(8,128)(2,1)} %get-tuple-element.56), channel_id=1, source_target_pairs={{0,8},{1,9},{2,10},{3,11},{4,12},{5,13},{6,14},{7,15},{8,0},{9,1},... | collective-permute-start | bytes 6389768 | tf_op jit(solution)/shard_map/ppermute | solution.py:46
  75.0 7.7 %copy-start.32 = (bf16[1024,128]{1,0:T(8,128)(2,1)S(1)}, bf16[1024,128]{1,0:T(8,128)(2,1)}, u32[]{:S(2)}) copy-start(bf16[1024,128]{1,0:T(8,128)(2,1)} %copy-done.31) | copy-start | bytes 786436
  75.0 7.8 %copy-start.28 = (bf16[1024,128]{1,0:T(8,128)(2,1)S(1)}, bf16[1024,128]{1,0:T(8,128)(2,1)}, u32[]{:S(2)}) copy-start(bf16[1024,128]{1,0:T(8,128)(2,1)} %copy-done.27) | copy-start | bytes 786436
  75.0 9.3 %copy-start.24 = (bf16[1024,128]{1,0:T(8,128)(2,1)S(1)}, bf16[1024,128]{1,0:T(8,128)(2,1)}, u32[]{:S(2)}) copy-start(bf16[1024,128]{1,0:T(8,128)(2,1)} %copy-done.23) | copy-start | bytes 786436
  75.0 21.5 %copy-start.20 = (bf16[1024,128]{1,0:T(8,128)(2,1)S(1)}, bf16[1024,128]{1,0:T(8,128)(2,1)}, u32[]{:S(2)}) copy-start(bf16[1024,128]{1,0:T(8,128)(2,1)} %copy-done.19) | copy-start | bytes 786436
  75.0 21.5 %copy-start.18 = (bf16[1024,128]{1,0:T(8,128)(2,1)S(1)}, bf16[1024,128]{1,0:T(8,128)(2,1)}, u32[]{:S(2)}) copy-start(bf16[1024,128]{1,0:T(8,128)(2,1)} %copy-done.17) | copy-start | bytes 786436
  75.0 22.8 %copy-start.16 = (bf16[1024,128]{1,0:T(8,128)(2,1)S(1)}, bf16[1024,128]{1,0:T(8,128)(2,1)}, u32[]{:S(2)}) copy-start(bf16[1024,128]{1,0:T(8,128)(2,1)} %copy-done.15) | copy-start | bytes 786436
  75.0 25.4 %copy-start.7 = (bf16[1024,128]{1,0:T(8,128)(2,1)S(1)}, bf16[1024,128]{1,0:T(8,128)(2,1)}, u32[]{:S(2)}) copy-start(bf16[1024,128]{1,0:T(8,128)(2,1)} %copy-done.6) | copy-start | bytes 786436
  75.1 38.4 %all-to-all-start.1 = ((bf16[8,1040,128]{2,1,0:T(8,128)(2,1)}), bf16[8,1040,128]{2,1,0:T(8,128)(2,1)}, u32[]{:S(2)}, u32[]{:S(2)}) async-start(bf16[8,1040,128]{2,1,0:T(8,128)(2,1)} %bitcast.68), calls=%async_computation.1 | async-start | bytes 4259840 | tf_op jit(solution)/shard_map/all_to_all | solution.py:258
  82.7 33.6 %copy-start.35 = (bf16[1024,128]{1,0:T(8,128)(2,1)S(1)}, bf16[1024,128]{1,0:T(8,128)(2,1)}, u32[]{:S(2)}) copy-start(bf16[1024,128]{1,0:T(8,128)(2,1)} %param.5) | copy-start | bytes 786436
  82.7 13.8 %collective-permute-start.5 = (bf16[1024,128]{1,0:T(8,128)(2,1)S(1)}, bf16[1024,128]{1,0:T(8,128)(2,1)S(1)}, u32[]{:S(2)}, u32[]{:S(2)}) collective-permute-start(bf16[1024,128]{1,0:T(8,128)(2,1)S(1)} %copy-done.32), channel_id=1, source_target_pairs={{0,2},{1,3},{2,4},{3,5},{4,6},{5,7},{6,0},{7,1},{8,10},{9,11},{10,... | collective-permute-start | bytes 786440 | tf_op jit(solution)/shard_map/ppermute | solution.py:46
  82.8 13.7 %collective-permute-start.7 = (bf16[1024,128]{1,0:T(8,128)(2,1)S(1)}, bf16[1024,128]{1,0:T(8,128)(2,1)S(1)}, u32[]{:S(2)}, u32[]{:S(2)}) collective-permute-start(bf16[1024,128]{1,0:T(8,128)(2,1)S(1)} %copy-done.28), channel_id=1, source_target_pairs={{0,4},{1,5},{2,6},{3,7},{4,0},{5,1},{6,2},{7,3},{8,12},{9,13},{10,... | collective-permute-start | bytes 786440 | tf_op jit(solution)/shard_map/ppermute | solution.py:46
  84.3 13.5 %collective-permute-start.9 = (bf16[1024,128]{1,0:T(8,128)(2,1)S(1)}, bf16[1024,128]{1,0:T(8,128)(2,1)S(1)}, u32[]{:S(2)}, u32[]{:S(2)}) collective-permute-start(bf16[1024,128]{1,0:T(8,128)(2,1)S(1)} %copy-done.24), channel_id=1, source_target_pairs={{0,6},{1,7},{2,0},{3,1},{4,2},{5,3},{6,4},{7,5},{8,14},{9,15},{10,... | collective-permute-start | bytes 786440 | tf_op jit(solution)/shard_map/ppermute | solution.py:46
  96.5 13.9 %collective-permute-start.6 = (bf16[1024,128]{1,0:T(8,128)(2,1)S(1)}, bf16[1024,128]{1,0:T(8,128)(2,1)S(1)}, u32[]{:S(2)}, u32[]{:S(2)}) collective-permute-start(bf16[1024,128]{1,0:T(8,128)(2,1)S(1)} %copy-done.20), channel_id=1, source_target_pairs={{0,2},{1,3},{2,4},{3,5},{4,6},{5,7},{6,0},{7,1},{8,10},{9,11},{10,... | collective-permute-start | bytes 786440 | tf_op jit(solution)/shard_map/ppermute | solution.py:46
  96.5 13.8 %collective-permute-start.8 = (bf16[1024,128]{1,0:T(8,128)(2,1)S(1)}, bf16[1024,128]{1,0:T(8,128)(2,1)S(1)}, u32[]{:S(2)}, u32[]{:S(2)}) collective-permute-start(bf16[1024,128]{1,0:T(8,128)(2,1)S(1)} %copy-done.18), channel_id=1, source_target_pairs={{0,4},{1,5},{2,6},{3,7},{4,0},{5,1},{6,2},{7,3},{8,12},{9,13},{10,... | collective-permute-start | bytes 786440 | tf_op jit(solution)/shard_map/ppermute | solution.py:46
  97.8 13.3 %collective-permute-start.10 = (bf16[1024,128]{1,0:T(8,128)(2,1)S(1)}, bf16[1024,128]{1,0:T(8,128)(2,1)S(1)}, u32[]{:S(2)}, u32[]{:S(2)}) collective-permute-start(bf16[1024,128]{1,0:T(8,128)(2,1)S(1)} %copy-done.16), channel_id=1, source_target_pairs={{0,6},{1,7},{2,0},{3,1},{4,2},{5,3},{6,4},{7,5},{8,14},{9,15},{10,... | collective-permute-start | bytes 786440 | tf_op jit(solution)/shard_map/ppermute | solution.py:46
  100.6 12.9 %collective-permute-start.11 = (bf16[1024,128]{1,0:T(8,128)(2,1)S(1)}, bf16[1024,128]{1,0:T(8,128)(2,1)S(1)}, u32[]{:S(2)}, u32[]{:S(2)}) collective-permute-start(bf16[1024,128]{1,0:T(8,128)(2,1)S(1)} %add_convert_fusion.3), channel_id=1, source_target_pairs={{0,1},{1,0},{2,3},{3,2},{4,5},{5,4},{6,7},{7,6},{8,9},{9,8},{10,11... | collective-permute-start | bytes 786440 | tf_op jit(solution)/shard_map/ppermute | solution.py:46
  116.5 9.3 %copy-start.33 = (bf16[1024,128]{1,0:T(8,128)(2,1)}, bf16[1024,128]{1,0:T(8,128)(2,1)S(1)}, u32[]{:S(2)}) copy-start(bf16[1024,128]{1,0:T(8,128)(2,1)S(1)} %multiply_convert_fusion) | copy-start | bytes 786436
  116.6 7.6 %collective-permute-start.13 = (bf16[1040,128]{1,0:T(8,128)(2,1)S(1)}, bf16[1040,128]{1,0:T(8,128)(2,1)S(1)}, u32[]{:S(2)}, u32[]{:S(2)}) collective-permute-start(bf16[1040,128]{1,0:T(8,128)(2,1)S(1)} %pad_maximum_fusion.1), channel_id=1, source_target_pairs={{0,1},{1,0},{2,3},{3,2},{4,5},{5,4},{6,7},{7,6},{8,9},{9,8},{10,11... | collective-permute-start | bytes 798728 | tf_op jit(solution)/shard_map/ppermute | solution.py:46
  125.8 36.0 %all-to-all-start.2 = ((bf16[8,1024,128]{2,1,0:T(8,128)(2,1)}), bf16[8,1024,128]{2,1,0:T(8,128)(2,1)S(1)}, u32[]{:S(2)}, u32[]{:S(2)}) async-start(bf16[8,1024,128]{2,1,0:T(8,128)(2,1)} %broadcast_in_dim.10), calls=%async_computation.2 | async-start | bytes 4194304 | tf_op jit(solution)/shard_map/all_to_all | solution.py:240
  132.8 12.0 %collective-permute-start.16 = (bf16[2064,128]{1,0:T(8,128)(2,1)S(1)}, bf16[2064,128]{1,0:T(8,128)(2,1)S(1)}, u32[]{:S(2)}, u32[]{:S(2)}) collective-permute-start(bf16[2064,128]{1,0:T(8,128)(2,1)S(1)} %pad_maximum_fusion.row_0), channel_id=1, source_target_pairs={{0,6},{1,7},{2,0},{3,1},{4,2},{5,3},{6,4},{7,5},{8,14},{9,15},{10,... | collective-permute-start | bytes 1585160 | tf_op jit(solution)/shard_map/ppermute | solution.py:46
  134.3 13.2 %collective-permute-start.15 = (bf16[2064,128]{1,0:T(8,128)(2,1)S(1)}, bf16[2064,128]{1,0:T(8,128)(2,1)S(1)}, u32[]{:S(2)}, u32[]{:S(2)}) collective-permute-start(bf16[2064,128]{1,0:T(8,128)(2,1)S(1)} %pad_maximum_fusion.row_0), channel_id=1, source_target_pairs={{0,4},{1,5},{2,6},{3,7},{4,0},{5,1},{6,2},{7,3},{8,12},{9,13},{10,... | collective-permute-start | bytes 1585160 | tf_op jit(solution)/shard_map/ppermute | solution.py:46
  135.1 25.9 %collective-permute-start.14 = (bf16[2064,128]{1,0:T(8,128)(2,1)S(1)}, bf16[2064,128]{1,0:T(8,128)(2,1)S(1)}, u32[]{:S(2)}, u32[]{:S(2)}) collective-permute-start(bf16[2064,128]{1,0:T(8,128)(2,1)S(1)} %pad_maximum_fusion.row_0), channel_id=1, source_target_pairs={{0,2},{1,3},{2,4},{3,5},{4,6},{5,7},{6,0},{7,1},{8,10},{9,11},{10,... | collective-permute-start | bytes 1585160 | tf_op jit(solution)/shard_map/ppermute | solution.py:46
  161.8 4.3 %collective-permute-start.17 = (bf16[8192,128]{1,0:T(8,128)(2,1)S(1)}, bf16[8192,128]{1,0:T(8,128)(2,1)S(1)}, u32[]{:S(2)}, u32[]{:S(2)}) collective-permute-start(bf16[8192,128]{1,0:T(8,128)(2,1)S(1)} %bitcast.62), channel_id=1, source_target_pairs={{0,8},{1,9},{2,10},{3,11},{4,12},{5,13},{6,14},{7,15},{8,0},{9,1},... | collective-permute-start | bytes 6291464 | tf_op jit(solution)/shard_map/ppermute | solution.py:46
  182.3 7.4 %copy-start.4 = (bf16[1024,128]{1,0:T(8,128)(2,1)}, bf16[1024,128]{1,0:T(8,128)(2,1)S(1)}, u32[]{:S(2)}) copy-start(bf16[1024,128]{1,0:T(8,128)(2,1)S(1)} %get-tuple-element.72) | copy-start | bytes 786436
  182.3 7.4 %copy-start.9 = (bf16[1024,128]{1,0:T(8,128)(2,1)}, bf16[1024,128]{1,0:T(8,128)(2,1)S(1)}, u32[]{:S(2)}) copy-start(bf16[1024,128]{1,0:T(8,128)(2,1)S(1)} %get-tuple-element.71) | copy-start | bytes 786436
  182.3 7.4 %copy-start.11 = (bf16[1024,128]{1,0:T(8,128)(2,1)}, bf16[1024,128]{1,0:T(8,128)(2,1)S(1)}, u32[]{:S(2)}) copy-start(bf16[1024,128]{1,0:T(8,128)(2,1)S(1)} %get-tuple-element.68) | copy-start | bytes 786436
  182.3 7.4 %copy-start.13 = (bf16[1024,128]{1,0:T(8,128)(2,1)}, bf16[1024,128]{1,0:T(8,128)(2,1)S(1)}, u32[]{:S(2)}) copy-start(bf16[1024,128]{1,0:T(8,128)(2,1)S(1)} %get-tuple-element.65) | copy-start | bytes 786436
  182.4 4.5 %collective-permute-start.25 = (bf16[8320,128]{1,0:T(8,128)(2,1)}, bf16[8320,128]{1,0:T(8,128)(2,1)S(1)}, u32[]{:S(2)}, u32[]{:S(2)}) collective-permute-start(bf16[8320,128]{1,0:T(8,128)(2,1)} %get-tuple-element.74), channel_id=1, source_target_pairs={{0,8},{1,9},{2,10},{3,11},{4,12},{5,13},{6,14},{7,15},{8,0},{9,1},... | collective-permute-start | bytes 6389768 | tf_op jit(solution)/shard_map/ppermute | solution.py:46
  189.8 7.7 %copy-start.30 = (bf16[1024,128]{1,0:T(8,128)(2,1)S(1)}, bf16[1024,128]{1,0:T(8,128)(2,1)}, u32[]{:S(2)}) copy-start(bf16[1024,128]{1,0:T(8,128)(2,1)} %copy-done.29) | copy-start | bytes 786436
  189.8 7.8 %copy-start.26 = (bf16[1024,128]{1,0:T(8,128)(2,1)S(1)}, bf16[1024,128]{1,0:T(8,128)(2,1)}, u32[]{:S(2)}) copy-start(bf16[1024,128]{1,0:T(8,128)(2,1)} %copy-done.25) | copy-start | bytes 786436
  189.8 9.5 %copy-start.22 = (bf16[1024,128]{1,0:T(8,128)(2,1)S(1)}, bf16[1024,128]{1,0:T(8,128)(2,1)}, u32[]{:S(2)}) copy-start(bf16[1024,128]{1,0:T(8,128)(2,1)} %copy-done.21) | copy-start | bytes 786436
  189.8 17.4 %copy-start.14 = (bf16[1024,128]{1,0:T(8,128)(2,1)S(1)}, bf16[1024,128]{1,0:T(8,128)(2,1)}, u32[]{:S(2)}) copy-start(bf16[1024,128]{1,0:T(8,128)(2,1)} %copy-done.13) | copy-start | bytes 786436
  189.8 21.2 %copy-start.12 = (bf16[1024,128]{1,0:T(8,128)(2,1)S(1)}, bf16[1024,128]{1,0:T(8,128)(2,1)}, u32[]{:S(2)}) copy-start(bf16[1024,128]{1,0:T(8,128)(2,1)} %copy-done.11) | copy-start | bytes 786436
  189.8 22.6 %copy-start.10 = (bf16[1024,128]{1,0:T(8,128)(2,1)S(1)}, bf16[1024,128]{1,0:T(8,128)(2,1)}, u32[]{:S(2)}) copy-start(bf16[1024,128]{1,0:T(8,128)(2,1)} %copy-done.9) | copy-start | bytes 786436
  189.8 26.0 %copy-start.5 = (bf16[1024,128]{1,0:T(8,128)(2,1)S(1)}, bf16[1024,128]{1,0:T(8,128)(2,1)}, u32[]{:S(2)}) copy-start(bf16[1024,128]{1,0:T(8,128)(2,1)} %copy-done.4) | copy-start | bytes 786436
  189.9 38.3 %all-to-all-start.3 = ((bf16[8,1040,128]{2,1,0:T(8,128)(2,1)}), bf16[8,1040,128]{2,1,0:T(8,128)(2,1)}, u32[]{:S(2)}, u32[]{:S(2)}) async-start(bf16[8,1040,128]{2,1,0:T(8,128)(2,1)} %bitcast.67), calls=%async_computation.3 | async-start | bytes 4259840 | tf_op jit(solution)/shard_map/all_to_all | solution.py:258
  197.5 40.5 %copy-start.34 = (bf16[1024,128]{1,0:T(8,128)(2,1)S(1)}, bf16[1024,128]{1,0:T(8,128)(2,1)}, u32[]{:S(2)}) copy-start(bf16[1024,128]{1,0:T(8,128)(2,1)} %copy-done.33) | copy-start | bytes 786436
  197.5 9.7 %collective-permute-start.18 = (bf16[1024,128]{1,0:T(8,128)(2,1)S(1)}, bf16[1024,128]{1,0:T(8,128)(2,1)S(1)}, u32[]{:S(2)}, u32[]{:S(2)}) collective-permute-start(bf16[1024,128]{1,0:T(8,128)(2,1)S(1)} %copy-done.30), channel_id=1, source_target_pairs={{0,2},{1,3},{2,4},{3,5},{4,6},{5,7},{6,0},{7,1},{8,10},{9,11},{10,... | collective-permute-start | bytes 786440 | tf_op jit(solution)/shard_map/ppermute | solution.py:46
  197.6 13.4 %collective-permute-start.20 = (bf16[1024,128]{1,0:T(8,128)(2,1)S(1)}, bf16[1024,128]{1,0:T(8,128)(2,1)S(1)}, u32[]{:S(2)}, u32[]{:S(2)}) collective-permute-start(bf16[1024,128]{1,0:T(8,128)(2,1)S(1)} %copy-done.26), channel_id=1, source_target_pairs={{0,4},{1,5},{2,6},{3,7},{4,0},{5,1},{6,2},{7,3},{8,12},{9,13},{10,... | collective-permute-start | bytes 786440 | tf_op jit(solution)/shard_map/ppermute | solution.py:46
  199.3 13.1 %collective-permute-start.22 = (bf16[1024,128]{1,0:T(8,128)(2,1)S(1)}, bf16[1024,128]{1,0:T(8,128)(2,1)S(1)}, u32[]{:S(2)}, u32[]{:S(2)}) collective-permute-start(bf16[1024,128]{1,0:T(8,128)(2,1)S(1)} %copy-done.22), channel_id=1, source_target_pairs={{0,6},{1,7},{2,0},{3,1},{4,2},{5,3},{6,4},{7,5},{8,14},{9,15},{10,... | collective-permute-start | bytes 786440 | tf_op jit(solution)/shard_map/ppermute | solution.py:46
  207.2 9.3 %collective-permute-start.19 = (bf16[1024,128]{1,0:T(8,128)(2,1)S(1)}, bf16[1024,128]{1,0:T(8,128)(2,1)S(1)}, u32[]{:S(2)}, u32[]{:S(2)}) collective-permute-start(bf16[1024,128]{1,0:T(8,128)(2,1)S(1)} %copy-done.14), channel_id=1, source_target_pairs={{0,2},{1,3},{2,4},{3,5},{4,6},{5,7},{6,0},{7,1},{8,10},{9,11},{10,... | collective-permute-start | bytes 786440 | tf_op jit(solution)/shard_map/ppermute | solution.py:46
  211.0 9.0 %collective-permute-start.21 = (bf16[1024,128]{1,0:T(8,128)(2,1)S(1)}, bf16[1024,128]{1,0:T(8,128)(2,1)S(1)}, u32[]{:S(2)}, u32[]{:S(2)}) collective-permute-start(bf16[1024,128]{1,0:T(8,128)(2,1)S(1)} %copy-done.12), channel_id=1, source_target_pairs={{0,4},{1,5},{2,6},{3,7},{4,0},{5,1},{6,2},{7,3},{8,12},{9,13},{10,... | collective-permute-start | bytes 786440 | tf_op jit(solution)/shard_map/ppermute | solution.py:46
  212.4 10.7 %collective-permute-start.23 = (bf16[1024,128]{1,0:T(8,128)(2,1)S(1)}, bf16[1024,128]{1,0:T(8,128)(2,1)S(1)}, u32[]{:S(2)}, u32[]{:S(2)}) collective-permute-start(bf16[1024,128]{1,0:T(8,128)(2,1)S(1)} %copy-done.10), channel_id=1, source_target_pairs={{0,6},{1,7},{2,0},{3,1},{4,2},{5,3},{6,4},{7,5},{8,14},{9,15},{10,... | collective-permute-start | bytes 786440 | tf_op jit(solution)/shard_map/ppermute | solution.py:46
  216.0 12.1 %collective-permute-start.24 = (bf16[1024,128]{1,0:T(8,128)(2,1)S(1)}, bf16[1024,128]{1,0:T(8,128)(2,1)S(1)}, u32[]{:S(2)}, u32[]{:S(2)}) collective-permute-start(bf16[1024,128]{1,0:T(8,128)(2,1)S(1)} %add_convert_fusion.2), channel_id=1, source_target_pairs={{0,1},{1,0},{2,3},{3,2},{4,5},{5,4},{6,7},{7,6},{8,9},{9,8},{10,11... | collective-permute-start | bytes 786440 | tf_op jit(solution)/shard_map/ppermute | solution.py:46
  228.9 4.7 %collective-permute-start.28 = (f32[8,128]{1,0:T(8,128)S(1)}, f32[8,128]{1,0:T(8,128)S(1)}, u32[]{:S(2)}, u32[]{:S(2)}) collective-permute-start(f32[8,128]{1,0:T(8,128)S(1)} %broadcast_in_dim.11), channel_id=1, source_target_pairs={{0,2},{1,3},{2,4},{3,5},{4,6},{5,7},{6,0},{7,1},{8,10},{9,11},{10,... | collective-permute-start | bytes 12296 | tf_op jit(solution)/shard_map/ppermute | solution.py:46
  229.0 4.6 %collective-permute-start.27 = (f32[8,128]{1,0:T(8,128)S(1)}, f32[8,128]{1,0:T(8,128)S(1)}, u32[]{:S(2)}, u32[]{:S(2)}) collective-permute-start(f32[8,128]{1,0:T(8,128)S(1)} %broadcast_in_dim.11), channel_id=1, source_target_pairs={{0,4},{1,5},{2,6},{3,7},{4,0},{5,1},{6,2},{7,3},{8,12},{9,13},{10,... | collective-permute-start | bytes 12296 | tf_op jit(solution)/shard_map/ppermute | solution.py:46
  230.6 3.0 %collective-permute-start.26 = (f32[8,128]{1,0:T(8,128)S(1)}, f32[8,128]{1,0:T(8,128)S(1)}, u32[]{:S(2)}, u32[]{:S(2)}) collective-permute-start(f32[8,128]{1,0:T(8,128)S(1)} %broadcast_in_dim.11), channel_id=1, source_target_pairs={{0,6},{1,7},{2,0},{3,1},{4,2},{5,3},{6,4},{7,5},{8,14},{9,15},{10,... | collective-permute-start | bytes 12296 | tf_op jit(solution)/shard_map/ppermute | solution.py:46
  233.7 2.5 %collective-permute-start.29 = (f32[8,128]{1,0:T(8,128)S(1)}, f32[8,128]{1,0:T(8,128)S(1)}, u32[]{:S(2)}, u32[]{:S(2)}) collective-permute-start(f32[8,128]{1,0:T(8,128)S(1)} %dynamic-slice_reduce_fusion), channel_id=1, source_target_pairs={{0,1},{1,0},{2,3},{3,2},{4,5},{5,4},{6,7},{7,6},{8,9},{9,8},{10,11... | collective-permute-start | bytes 12296 | tf_op jit(solution)/shard_map/ppermute | solution.py:46
  (7 other events, 25.9 us)
